TPU v7x, 32 devices: a whole 2x2x4 slice. The times are simulated.
32 devices in a mesh: ctx: 4 (over y, core), fsdp: 8 (over z, x).
Axes of the slice: x: 2, y: 2, z: 4, core: 2. Of those that a mesh axis runs over, the one named last changes fastest.
Arguments:
- tokens: bfloat16 [8, 2048, 1024], P('fsdp', 'ctx'), may hold values from -6 to 6
- memory: bfloat16 [8, 2048, 1024], P('fsdp', 'ctx'), may hold values from -6 to 6
- cotangent: bfloat16 [8, 2048, 1024], P('fsdp', 'ctx'), may hold values from -6 to 6
- block_map: int32 [8, 8, 8], P('fsdp'), may hold values from 0 to 1, as said below
- block_order: int32 [8, 4], P('fsdp'), may hold values from 0 to 3, each once within a row
- self_projection: bfloat16 [1024, 3072], P('fsdp'), may hold values from -0.1875 to 0.1875
- self_output: bfloat16 [1024, 1024], P('fsdp'), may hold values from -0.375 to 0.375
- self_query_bias: bfloat16 [1024], P('fsdp'), may hold values from -2.5 to 2.5
- self_value_bias: bfloat16 [1024], P('fsdp'), may hold values from -2.5 to 2.5
- self_output_bias: bfloat16 [1024], P('fsdp'), may hold values from -2.5 to 2.5
- first_gain: bfloat16 [1024], P('fsdp'), may hold values from 0.5 to 1.5
- first_shift: bfloat16 [1024], P('fsdp'), may hold values from -2.5 to 2.5
- cross_query: bfloat16 [1024, 1024], P('fsdp'), may hold values from -0.1875 to 0.1875
- cross_memory: bfloat16 [1024, 2048], P('fsdp'), may hold values from -0.1875 to 0.1875
- cross_output: bfloat16 [1024, 1024], P('fsdp'), may hold values from -0.375 to 0.375
- cross_query_bias: bfloat16 [1024], P('fsdp'), may hold values from -2.5 to 2.5
- cross_value_bias: bfloat16 [1024], P('fsdp'), may hold values from -2.5 to 2.5
- cross_output_bias: bfloat16 [1024], P('fsdp'), may hold values from -2.5 to 2.5
- second_gain: bfloat16 [1024], P('fsdp'), may hold values from 0.5 to 1.5
- second_shift: bfloat16 [1024], P('fsdp'), may hold values from -2.5 to 2.5
- expand_weight: bfloat16 [1024, 4096], P('fsdp'), may hold values from -0.1875 to 0.1875
- reduce_weight: bfloat16 [4096, 1024], P('fsdp'), may hold values from -0.09375 to 0.09375
- expand_bias: bfloat16 [4096], P('fsdp'), may hold values from -2.5 to 2.5
- reduce_bias: bfloat16 [1024], P('fsdp'), may hold values from -2.5 to 2.5
- third_gain: bfloat16 [1024], P('fsdp'), may hold values from 0.5 to 1.5
- third_shift: bfloat16 [1024], P('fsdp'), may hold values from -2.5 to 2.5
Outputs:
- output: bfloat16 [8, 2048, 1024], P('fsdp', 'ctx')
- token_grad: float32 [8, 2048, 1024], P('fsdp', 'ctx')
- memory_grad: float32 [8, 2048, 1024], P('fsdp', 'ctx')
- grad_self_projection: float32 [1024, 3072], P('fsdp')
- grad_self_output: float32 [1024, 1024], P('fsdp')
- grad_self_query_bias: float32 [1024], P('fsdp')
- grad_self_value_bias: float32 [1024], P('fsdp')
- grad_self_output_bias: float32 [1024], P('fsdp')
- grad_first_gain: float32 [1024], P('fsdp')
- grad_first_shift: float32 [1024], P('fsdp')
- grad_cross_query: float32 [1024, 1024], P('fsdp')
- grad_cross_memory: float32 [1024, 2048], P('fsdp')
- grad_cross_output: float32 [1024, 1024], P('fsdp')
- grad_cross_query_bias: float32 [1024], P('fsdp')
- grad_cross_value_bias: float32 [1024], P('fsdp')
- grad_cross_output_bias: float32 [1024], P('fsdp')
- grad_second_gain: float32 [1024], P('fsdp')
- grad_second_shift: float32 [1024], P('fsdp')
- grad_expand_weight: float32 [1024, 4096], P('fsdp')
- grad_reduce_weight: float32 [4096, 1024], P('fsdp')
- grad_expand_bias: float32 [4096], P('fsdp')
- grad_reduce_bias: float32 [1024], P('fsdp')
- grad_third_gain: float32 [1024], P('fsdp')
- grad_third_shift: float32 [1024], P('fsdp')
Inputs may be any that keep to these rules, and one draw needn't show every extreme that they name: block_map[s, i, j] is 1 exactly when j <= i and j is not before the first block of the document holding block i; each sequence holds one or two documents of whole blocks, so every block sees itself. Each row lists every group number once: index c of ctx holds group block_order[s, c] of sequence s, of 512 tokens.
All inputs are finite; a program needn't handle non-finite values.
Results may differ from a plain program's by a relative error of at most 0.022.
Values may be sent and summed in bfloat16 or wider, within the bound.
No kernel may reach another device: no remote copies, remote signals or barrier semaphores. Data moves between devices by JAX's collectives and lax.ppermute only.
A program may use at most 320 MiB of HBM per device.

v0:
```python
import math

import jax
import jax.numpy as jnp
from jax import lax
from jax.sharding import PartitionSpec as P

HEADS = 16
HEAD_DIM = 64
BLK = 256


epsilon = 1e-05
residual_scale = 18.0**0.25
score_scale = 0.125
masked_score = -1e30
gelu_coeff = math.sqrt(2.0 / math.pi)


def gelu_tanh(value):
    return 0.5 * value * (1.0 + jnp.tanh(gelu_coeff * (value + 0.044715 * value * value * value)))


def gelu_slope(value):
    inner = jnp.tanh(gelu_coeff * (value + 0.044715 * value * value * value))
    return 0.5 * (1.0 + inner) + 0.5 * value * (1.0 - inner * inner) * gelu_coeff * (
        1.0 + 3.0 * 0.044715 * value * value
    )


def layer_norm(summed, gain, shift):
    centred = summed - jnp.mean(summed, axis=-1, keepdims=True)
    inverse = lax.rsqrt(jnp.mean(centred * centred, axis=-1, keepdims=True) + epsilon)
    normed = centred * inverse
    return (normed * gain + shift, normed, inverse)


def layer_norm_back(upstream, gain, normed, inverse):
    scaled = upstream * gain
    inner = (
        scaled
        - jnp.mean(scaled, axis=-1, keepdims=True)
        - normed * jnp.mean(scaled * normed, axis=-1, keepdims=True)
    )
    return (inner * inverse, jnp.sum(upstream * normed, axis=0), jnp.sum(upstream, axis=0))


def head_split(matrix):
    return matrix.reshape(matrix.shape[0], HEADS, HEAD_DIM)


def piece_size(length):
    return min(512, length)


def piece_masks(key_blocks, allowed_rows):
    length = key_blocks.shape[0]
    piece = piece_size(length)
    count = length // piece
    if allowed_rows is None:
        return jnp.ones((count, 1, 1), jnp.bool_)
    nblocks = allowed_rows.shape[1]
    onehot = (key_blocks[:, None] == jnp.arange(nblocks, dtype=jnp.int32)[None, :]).astype(
        jnp.float32
    )
    live = jnp.dot(allowed_rows, onehot.T) > 0.5
    return jnp.moveaxis(live.reshape(live.shape[0], count, piece), 1, 0)


def masked_scores(query_heads, key_piece, live):
    scores = (
        jnp.einsum("qhd,khd->hqk", query_heads, key_piece, preferred_element_type=jnp.float32)
        * score_scale
    )
    return jnp.where(live[None], scores, masked_score)


def run_guarded(guarded, live, work, fallback):
    if guarded:
        return lax.cond(jnp.any(live), work, lambda unused: fallback, live)
    return work(live)


def attend_forward(query_heads, key_heads, value_heads, live_pieces, guarded):
    count = live_pieces.shape[0]
    piece = key_heads.shape[0] // count
    key_pieces = key_heads.reshape((count, piece) + key_heads.shape[1:])
    value_pieces = value_heads.reshape((count, piece) + value_heads.shape[1:])
    rows = query_heads.shape[0]

    def first_step(carry, inputs):
        run_max, run_sum = carry
        key_piece, live = inputs

        def work(live_now):
            scores = masked_scores(query_heads, key_piece, live_now)
            new_max = jnp.maximum(run_max, jnp.max(scores, axis=-1))
            shifted = jnp.where(live_now[None], jnp.exp(scores - new_max[:, :, None]), 0.0)
            return (new_max, run_sum * jnp.exp(run_max - new_max) + jnp.sum(shifted, axis=-1))

        return (run_guarded(guarded, live, work, (run_max, run_sum)), None)

    start = (
        jnp.full((HEADS, rows), masked_score, jnp.float32),
        jnp.zeros((HEADS, rows), jnp.float32),
    )
    (final_max, final_sum), unused = lax.scan(first_step, start, (key_pieces, live_pieces))
    log_total = final_max + jnp.log(final_sum)

    def second_step(total, inputs):
        key_piece, value_piece, live = inputs

        def work(live_now):
            scores = masked_scores(query_heads, key_piece, live_now)
            probs = jnp.exp(scores - log_total[:, :, None]).astype(jnp.bfloat16)
            return total + jnp.einsum(
                "hqk,khd->qhd", probs, value_piece, preferred_element_type=jnp.float32
            )

        return (run_guarded(guarded, live, work, total), None)

    empty = jnp.zeros((rows, HEADS, HEAD_DIM), jnp.float32)
    attended, unused = lax.scan(second_step, empty, (key_pieces, value_pieces, live_pieces))
    return (attended, log_total)


def attend_backward(
    query_heads, key_heads, value_heads, log_total, grad_heads, delta, live_pieces, guarded
):
    count = live_pieces.shape[0]
    piece = key_heads.shape[0] // count
    key_pieces = key_heads.reshape((count, piece) + key_heads.shape[1:])
    value_pieces = value_heads.reshape((count, piece) + value_heads.shape[1:])
    rows = query_heads.shape[0]
    blank = jnp.zeros((piece, HEADS, HEAD_DIM), jnp.float32)

    def back_step(grad_query, inputs):
        key_piece, value_piece, live = inputs

        def work(live_now):
            scores = masked_scores(query_heads, key_piece, live_now)
            probs = jnp.exp(scores - log_total[:, :, None])
            grad_probs = jnp.einsum(
                "qhd,khd->hqk", grad_heads, value_piece, preferred_element_type=jnp.float32
            )
            grad_scores = (probs * (grad_probs - delta[:, :, None])).astype(jnp.bfloat16)
            new_query = (
                grad_query
                + jnp.einsum(
                    "hqk,khd->qhd", grad_scores, key_piece, preferred_element_type=jnp.float32
                )
                * score_scale
            )
            grad_key = (
                jnp.einsum(
                    "hqk,qhd->khd", grad_scores, query_heads, preferred_element_type=jnp.float32
                )
                * score_scale
            )
            grad_value = jnp.einsum(
                "hqk,qhd->khd",
                probs.astype(jnp.bfloat16),
                grad_heads,
                preferred_element_type=jnp.float32,
            )
            return (new_query, (grad_key, grad_value))

        return run_guarded(guarded, live, work, (grad_query, (blank, blank)))

    empty = jnp.zeros((rows, HEADS, HEAD_DIM), jnp.float32)
    grad_query, (key_grads, value_grads) = lax.scan(
        back_step, empty, (key_pieces, value_pieces, live_pieces)
    )
    width = HEADS * HEAD_DIM
    return (
        grad_query.reshape(rows, width),
        key_grads.reshape(-1, width),
        value_grads.reshape(-1, width),
    )


def shards(
    tokens,
    memory,
    cotangent,
    block_map,
    block_order,
    self_projection,
    self_output,
    self_query_bias,
    self_value_bias,
    self_output_bias,
    first_gain,
    first_shift,
    cross_query,
    cross_memory,
    cross_output,
    cross_query_bias,
    cross_value_bias,
    cross_output_bias,
    second_gain,
    second_shift,
    expand_weight,
    reduce_weight,
    expand_bias,
    reduce_bias,
    third_gain,
    third_shift,
):
    bf16 = jnp.bfloat16
    f32 = jnp.float32
    rows_in = tokens[0]
    rows = rows_in.shape[0]
    width = rows_in.shape[1]
    ctx_count = lax.axis_size("ctx")
    slot = lax.axis_index("ctx")
    positions = jnp.arange(rows * ctx_count, dtype=jnp.int32)
    group_index = positions // rows
    group_match = group_index[:, None] == jnp.arange(ctx_count, dtype=jnp.int32)[None, :]
    group_place = jnp.sum(jnp.where(group_match, block_order[0][None, :], 0), axis=1)
    key_blocks = (group_place * rows + positions % rows) // BLK
    own_blocks = lax.dynamic_slice_in_dim(key_blocks, slot * rows, rows)
    nblocks = block_map.shape[1]
    own_onehot = (own_blocks[:, None] == jnp.arange(nblocks, dtype=jnp.int32)[None, :]).astype(f32)
    allowed_rows = jnp.dot(own_onehot, block_map[0].astype(f32))
    self_live = piece_masks(key_blocks, allowed_rows)
    (
        projection_full,
        self_out_full,
        query_bias_full,
        value_bias_full,
        out_bias_full,
        gain_one,
        shift_one,
    ) = (
        lax.all_gather(self_projection, "fsdp", axis=0, tiled=True),
        lax.all_gather(self_output, "fsdp", axis=0, tiled=True),
        lax.all_gather(self_query_bias, "fsdp", axis=0, tiled=True),
        lax.all_gather(self_value_bias, "fsdp", axis=0, tiled=True),
        lax.all_gather(self_output_bias, "fsdp", axis=0, tiled=True),
        lax.all_gather(first_gain, "fsdp", axis=0, tiled=True),
        lax.all_gather(first_shift, "fsdp", axis=0, tiled=True),
    )
    projected = jnp.dot(rows_in, projection_full, preferred_element_type=f32)
    queries = (projected[:, :width] + query_bias_full).astype(bf16)
    keys_own = projected[:, width : 2 * width].astype(bf16)
    values_own = (projected[:, 2 * width :] + value_bias_full).astype(bf16)
    keys_all, values_all = (
        lax.all_gather(keys_own, "ctx", axis=0, tiled=True),
        lax.all_gather(values_own, "ctx", axis=0, tiled=True),
    )
    query_heads = head_split(queries)
    key_heads = head_split(keys_all)
    value_heads = head_split(values_all)
    attended, self_total = attend_forward(query_heads, key_heads, value_heads, self_live, True)
    attended_low = attended.reshape(rows, width).astype(bf16)
    branch = jnp.dot(attended_low, self_out_full, preferred_element_type=f32) + out_bias_full
    hidden_one, normed_one, inverse_one = layer_norm(
        residual_scale * rows_in.astype(f32) + branch, gain_one, shift_one
    )
    (
        cross_query_full,
        cross_memory_full,
        cross_out_full,
        cross_qbias_full,
        cross_vbias_full,
        cross_obias_full,
        gain_two,
        shift_two,
    ) = (
        lax.all_gather(cross_query, "fsdp", axis=0, tiled=True),
        lax.all_gather(cross_memory, "fsdp", axis=0, tiled=True),
        lax.all_gather(cross_output, "fsdp", axis=0, tiled=True),
        lax.all_gather(cross_query_bias, "fsdp", axis=0, tiled=True),
        lax.all_gather(cross_value_bias, "fsdp", axis=0, tiled=True),
        lax.all_gather(cross_output_bias, "fsdp", axis=0, tiled=True),
        lax.all_gather(second_gain, "fsdp", axis=0, tiled=True),
        lax.all_gather(second_shift, "fsdp", axis=0, tiled=True),
    )
    hidden_low = hidden_one.astype(bf16)
    cross_queries = (
        jnp.dot(hidden_low, cross_query_full, preferred_element_type=f32) + cross_qbias_full
    ).astype(bf16)
    memory_rows = memory[0]
    memory_proj = jnp.dot(memory_rows, cross_memory_full, preferred_element_type=f32)
    memory_keys = memory_proj[:, :width].astype(bf16)
    memory_values = (memory_proj[:, width:] + cross_vbias_full).astype(bf16)
    memory_keys_all, memory_values_all = (
        lax.all_gather(memory_keys, "ctx", axis=0, tiled=True),
        lax.all_gather(memory_values, "ctx", axis=0, tiled=True),
    )
    cross_heads = head_split(cross_queries)
    memory_key_heads = head_split(memory_keys_all)
    memory_value_heads = head_split(memory_values_all)
    cross_live = piece_masks(jnp.zeros((memory_keys_all.shape[0],), jnp.int32), None)
    cross_attended, cross_total = attend_forward(
        cross_heads, memory_key_heads, memory_value_heads, cross_live, False
    )
    cross_low = cross_attended.reshape(rows, width).astype(bf16)
    cross_branch = jnp.dot(cross_low, cross_out_full, preferred_element_type=f32) + cross_obias_full
    hidden_two, normed_two, inverse_two = layer_norm(
        residual_scale * hidden_one + cross_branch, gain_two, shift_two
    )
    expand_full, reduce_full, expand_bias_full, reduce_bias_full, gain_three, shift_three = (
        lax.all_gather(expand_weight, "fsdp", axis=0, tiled=True),
        lax.all_gather(reduce_weight, "fsdp", axis=0, tiled=True),
        lax.all_gather(expand_bias, "fsdp", axis=0, tiled=True),
        lax.all_gather(reduce_bias, "fsdp", axis=0, tiled=True),
        lax.all_gather(third_gain, "fsdp", axis=0, tiled=True),
        lax.all_gather(third_shift, "fsdp", axis=0, tiled=True),
    )
    hidden_two_low = hidden_two.astype(bf16)
    expanded = jnp.dot(hidden_two_low, expand_full, preferred_element_type=f32) + expand_bias_full
    activated = gelu_tanh(expanded).astype(bf16)
    reduced = jnp.dot(activated, reduce_full, preferred_element_type=f32) + reduce_bias_full
    result, normed_three, inverse_three = layer_norm(
        residual_scale * hidden_two + reduced, gain_three, shift_three
    )
    output = result.astype(bf16)[None]
    upstream = cotangent[0].astype(f32)
    grad_third, grad_third_gain, grad_third_shift = layer_norm_back(
        upstream, gain_three, normed_three, inverse_three
    )
    grad_reduced = grad_third.astype(bf16)
    grad_reduce_bias = jnp.sum(grad_reduced.astype(f32), axis=0)
    grad_reduce_weight = jnp.dot(activated.T, grad_reduced, preferred_element_type=f32)
    grad_activated = jnp.dot(grad_reduced, reduce_full.T, preferred_element_type=f32)
    grad_expanded = (grad_activated * gelu_slope(expanded)).astype(bf16)
    grad_expand_bias = jnp.sum(grad_expanded.astype(f32), axis=0)
    grad_expand_weight = jnp.dot(hidden_two_low.T, grad_expanded, preferred_element_type=f32)
    grad_hidden_two = residual_scale * grad_third + jnp.dot(
        grad_expanded, expand_full.T, preferred_element_type=f32
    )
    grad_second, grad_second_gain, grad_second_shift = layer_norm_back(
        grad_hidden_two, gain_two, normed_two, inverse_two
    )
    grad_cross_branch = grad_second.astype(bf16)
    grad_cross_output_bias = jnp.sum(grad_cross_branch.astype(f32), axis=0)
    grad_cross_output = jnp.dot(cross_low.T, grad_cross_branch, preferred_element_type=f32)
    grad_cross_low = jnp.dot(
        grad_cross_branch, cross_out_full.T, preferred_element_type=f32
    ).astype(bf16)
    grad_cross_heads = head_split(grad_cross_low)
    cross_delta = jnp.sum(grad_cross_heads.astype(f32) * cross_attended, axis=-1).T
    grad_cross_queries, memory_key_terms, memory_value_terms = attend_backward(
        cross_heads,
        memory_key_heads,
        memory_value_heads,
        cross_total,
        grad_cross_heads,
        cross_delta,
        cross_live,
        False,
    )
    grad_memory_keys, grad_memory_values = (
        lax.psum_scatter(
            memory_key_terms.astype(jnp.bfloat16), "ctx", scatter_dimension=0, tiled=True
        ).astype(jnp.float32),
        lax.psum_scatter(
            memory_value_terms.astype(jnp.bfloat16), "ctx", scatter_dimension=0, tiled=True
        ).astype(jnp.float32),
    )
    grad_memory_pair = jnp.concatenate(
        [grad_memory_keys.astype(bf16), grad_memory_values.astype(bf16)], axis=1
    )
    grad_cross_value_bias = jnp.sum(grad_memory_pair[:, width:].astype(f32), axis=0)
    grad_cross_memory = jnp.dot(memory_rows.T, grad_memory_pair, preferred_element_type=f32)
    memory_grad = jnp.dot(grad_memory_pair, cross_memory_full.T, preferred_element_type=f32)[None]
    grad_cross_low_queries = grad_cross_queries.astype(bf16)
    grad_cross_query_bias = jnp.sum(grad_cross_low_queries.astype(f32), axis=0)
    grad_cross_query = jnp.dot(hidden_low.T, grad_cross_low_queries, preferred_element_type=f32)
    grad_hidden_one = residual_scale * grad_second + jnp.dot(
        grad_cross_low_queries, cross_query_full.T, preferred_element_type=f32
    )
    grad_first, grad_first_gain, grad_first_shift = layer_norm_back(
        grad_hidden_one, gain_one, normed_one, inverse_one
    )
    grad_branch = grad_first.astype(bf16)
    grad_self_output_bias = jnp.sum(grad_branch.astype(f32), axis=0)
    grad_self_output = jnp.dot(attended_low.T, grad_branch, preferred_element_type=f32)
    grad_attended = jnp.dot(grad_branch, self_out_full.T, preferred_element_type=f32).astype(bf16)
    grad_attended_heads = head_split(grad_attended)
    self_delta = jnp.sum(grad_attended_heads.astype(f32) * attended, axis=-1).T
    grad_queries, key_terms, value_terms = attend_backward(
        query_heads,
        key_heads,
        value_heads,
        self_total,
        grad_attended_heads,
        self_delta,
        self_live,
        True,
    )
    grad_keys, grad_values = (
        lax.psum_scatter(
            key_terms.astype(jnp.bfloat16), "ctx", scatter_dimension=0, tiled=True
        ).astype(jnp.float32),
        lax.psum_scatter(
            value_terms.astype(jnp.bfloat16), "ctx", scatter_dimension=0, tiled=True
        ).astype(jnp.float32),
    )
    grad_projected = jnp.concatenate(
        [grad_queries.astype(bf16), grad_keys.astype(bf16), grad_values.astype(bf16)], axis=1
    )
    grad_self_query_bias = jnp.sum(grad_projected[:, :width].astype(f32), axis=0)
    grad_self_value_bias = jnp.sum(grad_projected[:, 2 * width :].astype(f32), axis=0)
    grad_self_projection = jnp.dot(rows_in.T, grad_projected, preferred_element_type=f32)
    token_grad = (
        residual_scale * grad_first
        + jnp.dot(grad_projected, projection_full.T, preferred_element_type=f32)
    )[None]
    shares = (
        lax.psum_scatter(
            grad_self_projection.astype(jnp.bfloat16), "fsdp", scatter_dimension=0, tiled=True
        ).astype(jnp.float32),
        lax.psum_scatter(
            grad_self_output.astype(jnp.bfloat16), "fsdp", scatter_dimension=0, tiled=True
        ).astype(jnp.float32),
        lax.psum_scatter(
            grad_self_query_bias.astype(jnp.bfloat16), "fsdp", scatter_dimension=0, tiled=True
        ).astype(jnp.float32),
        lax.psum_scatter(
            grad_self_value_bias.astype(jnp.bfloat16), "fsdp", scatter_dimension=0, tiled=True
        ).astype(jnp.float32),
        lax.psum_scatter(
            grad_self_output_bias.astype(jnp.bfloat16), "fsdp", scatter_dimension=0, tiled=True
        ).astype(jnp.float32),
        lax.psum_scatter(
            grad_first_gain.astype(jnp.bfloat16), "fsdp", scatter_dimension=0, tiled=True
        ).astype(jnp.float32),
        lax.psum_scatter(
            grad_first_shift.astype(jnp.bfloat16), "fsdp", scatter_dimension=0, tiled=True
        ).astype(jnp.float32),
        lax.psum_scatter(
            grad_cross_query.astype(jnp.bfloat16), "fsdp", scatter_dimension=0, tiled=True
        ).astype(jnp.float32),
        lax.psum_scatter(
            grad_cross_memory.astype(jnp.bfloat16), "fsdp", scatter_dimension=0, tiled=True
        ).astype(jnp.float32),
        lax.psum_scatter(
            grad_cross_output.astype(jnp.bfloat16), "fsdp", scatter_dimension=0, tiled=True
        ).astype(jnp.float32),
        lax.psum_scatter(
            grad_cross_query_bias.astype(jnp.bfloat16), "fsdp", scatter_dimension=0, tiled=True
        ).astype(jnp.float32),
        lax.psum_scatter(
            grad_cross_value_bias.astype(jnp.bfloat16), "fsdp", scatter_dimension=0, tiled=True
        ).astype(jnp.float32),
        lax.psum_scatter(
            grad_cross_output_bias.astype(jnp.bfloat16), "fsdp", scatter_dimension=0, tiled=True
        ).astype(jnp.float32),
        lax.psum_scatter(
            grad_second_gain.astype(jnp.bfloat16), "fsdp", scatter_dimension=0, tiled=True
        ).astype(jnp.float32),
        lax.psum_scatter(
            grad_second_shift.astype(jnp.bfloat16), "fsdp", scatter_dimension=0, tiled=True
        ).astype(jnp.float32),
        lax.psum_scatter(
            grad_expand_weight.astype(jnp.bfloat16), "fsdp", scatter_dimension=0, tiled=True
        ).astype(jnp.float32),
        lax.psum_scatter(
            grad_reduce_weight.astype(jnp.bfloat16), "fsdp", scatter_dimension=0, tiled=True
        ).astype(jnp.float32),
        lax.psum_scatter(
            grad_expand_bias.astype(jnp.bfloat16), "fsdp", scatter_dimension=0, tiled=True
        ).astype(jnp.float32),
        lax.psum_scatter(
            grad_reduce_bias.astype(jnp.bfloat16), "fsdp", scatter_dimension=0, tiled=True
        ).astype(jnp.float32),
        lax.psum_scatter(
            grad_third_gain.astype(jnp.bfloat16), "fsdp", scatter_dimension=0, tiled=True
        ).astype(jnp.float32),
        lax.psum_scatter(
            grad_third_shift.astype(jnp.bfloat16), "fsdp", scatter_dimension=0, tiled=True
        ).astype(jnp.float32),
    )
    summed = (
        lax.psum(shares[0].astype(jnp.bfloat16), "ctx").astype(jnp.float32),
        lax.psum(shares[1].astype(jnp.bfloat16), "ctx").astype(jnp.float32),
        lax.psum(shares[2].astype(jnp.bfloat16), "ctx").astype(jnp.float32),
        lax.psum(shares[3].astype(jnp.bfloat16), "ctx").astype(jnp.float32),
        lax.psum(shares[4].astype(jnp.bfloat16), "ctx").astype(jnp.float32),
        lax.psum(shares[5].astype(jnp.bfloat16), "ctx").astype(jnp.float32),
        lax.psum(shares[6].astype(jnp.bfloat16), "ctx").astype(jnp.float32),
        lax.psum(shares[7].astype(jnp.bfloat16), "ctx").astype(jnp.float32),
        lax.psum(shares[8].astype(jnp.bfloat16), "ctx").astype(jnp.float32),
        lax.psum(shares[9].astype(jnp.bfloat16), "ctx").astype(jnp.float32),
        lax.psum(shares[10].astype(jnp.bfloat16), "ctx").astype(jnp.float32),
        lax.psum(shares[11].astype(jnp.bfloat16), "ctx").astype(jnp.float32),
        lax.psum(shares[12].astype(jnp.bfloat16), "ctx").astype(jnp.float32),
        lax.psum(shares[13].astype(jnp.bfloat16), "ctx").astype(jnp.float32),
        lax.psum(shares[14].astype(jnp.bfloat16), "ctx").astype(jnp.float32),
        lax.psum(shares[15].astype(jnp.bfloat16), "ctx").astype(jnp.float32),
        lax.psum(shares[16].astype(jnp.bfloat16), "ctx").astype(jnp.float32),
        lax.psum(shares[17].astype(jnp.bfloat16), "ctx").astype(jnp.float32),
        lax.psum(shares[18].astype(jnp.bfloat16), "ctx").astype(jnp.float32),
        lax.psum(shares[19].astype(jnp.bfloat16), "ctx").astype(jnp.float32),
        lax.psum(shares[20].astype(jnp.bfloat16), "ctx").astype(jnp.float32),
    )
    return (
        output,
        token_grad,
        memory_grad,
        summed[0],
        summed[1],
        summed[2],
        summed[3],
        summed[4],
        summed[5],
        summed[6],
        summed[7],
        summed[8],
        summed[9],
        summed[10],
        summed[11],
        summed[12],
        summed[13],
        summed[14],
        summed[15],
        summed[16],
        summed[17],
        summed[18],
        summed[19],
        summed[20],
    )


def solution(mesh):
    placed = (
        P("fsdp", "ctx", None),
        P("fsdp", "ctx", None),
        P("fsdp", "ctx", None),
        P("fsdp", None, None),
        P("fsdp", None),
        P("fsdp", None),
        P("fsdp", None),
        P("fsdp"),
        P("fsdp"),
        P("fsdp"),
        P("fsdp"),
        P("fsdp"),
        P("fsdp", None),
        P("fsdp", None),
        P("fsdp", None),
        P("fsdp"),
        P("fsdp"),
        P("fsdp"),
        P("fsdp"),
        P("fsdp"),
        P("fsdp", None),
        P("fsdp", None),
        P("fsdp"),
        P("fsdp"),
        P("fsdp"),
        P("fsdp"),
    )
    return jax.shard_map(
        shards,
        mesh=mesh,
        in_specs=placed,
        out_specs=(
            P("fsdp", "ctx", None),
            P("fsdp", "ctx", None),
            P("fsdp", "ctx", None),
            P("fsdp", None),
            P("fsdp", None),
            P("fsdp"),
            P("fsdp"),
            P("fsdp"),
            P("fsdp"),
            P("fsdp"),
            P("fsdp", None),
            P("fsdp", None),
            P("fsdp", None),
            P("fsdp"),
            P("fsdp"),
            P("fsdp"),
            P("fsdp"),
            P("fsdp"),
            P("fsdp", None),
            P("fsdp", None),
            P("fsdp"),
            P("fsdp"),
            P("fsdp"),
            P("fsdp"),
        ),
        check_vma=False,
    )
```

profile of v0, /device:TPU:11, one launch (start us, length us, event | category | flops | bytes accessed | tf_op | source)
XLA Modules:
  0.0 2066.3 jit_solution(10353685843689248089)
XLA Ops:
  19.3 62.8 %all-gather.34.cloned.1.call-done = bf16[1024,2048]{1,0:T(8,128)(2,1)} async-done(((bf16[128,2048]{1,0:T(8,128)(2,1)}), bf16[1024,2048]{1,0:T(8,128)(2,1)}) %all-gather.34.cloned.1.call-update) | async-done | bytes 4194320 | tf_op jit(solution)/shard_map/all_gather | solution.py:272
  92.8 88.5 %all-gather.26.cloned.1.call-done = bf16[1024,3072]{1,0:T(8,128)(2,1)} async-done(((bf16[128,3072]{1,0:T(8,128)(2,1)}), bf16[1024,3072]{1,0:T(8,128)(2,1)}) %all-gather.26.cloned.1.call-update) | async-done | bytes 6291472 | tf_op jit(solution)/shard_map/all_gather | solution.py:236
  368.3 19.7 all-gather.10
  458.1 22.2 %while.81 = (s32[]{:T(128)}, f32[16,512]{1,0:T(8,128)S(1)}, f32[16,512]{1,0:T(8,128)S(1)}, pred[4,512,512]{1,2,0:T(8,128)(4,1)S(1)}, bf16[4,512,16,64]{1,3,2,0:T...) while((s32[]{:T(128)}, f32[16,512]{1,0:T(8,128)S(1)}, f32[16,512]{1,0:T(8,128)S(1)}, ...), condition=%wide.region_7.8_spmd, body=%wide.region_1.7_spmd.sunk | while | flops 570703872 | bytes 37126840 | solution.py:107
  504.1 24.7 %while.82 = (s32[]{:T(128)}, f32[512,16,64]{0,2,1:T(8,128)}, pred[4,512,512]{1,2,0:T(8,128)(4,1)S(1)}, bf16[4,512,16,64]{1,3,2,0:T(8,128)(2,1)}, bf16[512,16,64]...) while((s32[]{:T(128)}, f32[512,16,64]{0,2,1:T(8,128)}, ...), condition=%wide.region_12.13_spmd, body=%wide.region_8.12_spmd.sunk | while | flops 1091305472 | bytes 8160423 | solution.py:123
  542.5 72.4 %while.84 = (s32[]{:T(128)}, f32[16,512]{1,0:T(8,128)S(1)}, f32[16,512]{1,0:T(8,128)S(1)}, bf16[4,512,16,64]{1,3,2,0:T(8,128)(2,1)}, bf16[512,16,64]{0,2,1:T(8,128)(2,1)S(1)}, /*index=5*/s32[]{:T(128)}, s32[]{:T(128)}) while((s32[]{:T(128)}, f32[16,512]{1,0:T(8,128)S(1)}, f32[16,512]{1,0:T(8,128)S(1)}, ...), condition=%wide.region_18.19_spmd.clone, body=%wide.region_15.18_spmd.clone.sunk | while | flops 557883392 | bytes 36077664 | solution.py:107
  614.9 31.2 %while.85 = (s32[]{:T(128)}, f32[512,16,64]{0,2,1:T(8,128)}, bf16[4,512,16,64]{1,3,2,0:T(8,128)(2,1)}, bf16[4,512,16,64]{1,3,2,0:T(8,128)(2,1)}, bf16[512,16,64]...) while((s32[]{:T(128)}, f32[512,16,64]{0,2,1:T(8,128)}, ...), condition=%wide.region_20.21_spmd.clone, body=%wide.region_19.20_spmd.clone.sunk | while | flops 1087373312 | bytes 7374438 | solution.py:123
  665.8 62.2 %all-gather.46.cloned.1.call-done = bf16[4096,1024]{1,0:T(8,128)(2,1)} async-done(((bf16[512,1024]{1,0:T(8,128)(2,1)}), bf16[4096,1024]{1,0:T(8,128)(2,1)}) %all-gather.46.cloned.1.call-update) | async-done | bytes 8388624 | tf_op jit(solution)/shard_map/all_gather | solution.py:306
  743.2 17.3 fusion.144
  781.7 131.4 %while.86 = (s32[]{:T(128)}, f32[512,16,64]{0,2,1:T(8,128)}, bf16[4,512,16,64]{1,3,2,0:T(8,128)(2,1)}, bf16[4,512,16,64]{1,3,2,0:T(8,128)(2,1)}, bf16[4,512,16,6...) while((s32[]{:T(128)}, f32[512,16,64]{0,2,1:T(8,128)}, ...), condition=%wide.region_31.32_spmd.clone, body=%wide.region_30.31_spmd.clone.sunk | while | flops 2720006144 | bytes 108101848 | solution.py:171
  955.1 102.1 %while.83 = (s32[]{:T(128)}, f32[512,16,64]{0,2,1:T(8,128)S(1)}, bf16[4,512,16,64]{1,3,2,0:T(8,128)(2,1)}, bf16[4,512,16,64]{1,3,2,0:T(8,128)(2,1)}, pred[4,512,...) while((s32[]{:T(128)}, f32[512,16,64]{0,2,1:T(8,128)S(1)}, ...), condition=%wide.region_39.40_spmd, body=%wide.region_35.39_spmd.sunk | while | flops 2728656896 | bytes 98666760 | solution.py:171
  958.1 38.2 %conditional.8 = (f32[512,16,64]{0,2,1:T(8,128)S(1)}, bf16[1,512,16,64]{1,3,2,0:T(8,128)(2,1)}, bf16[1,512,16,64]{1,3,2,0:T(8,128)(2,1)}) conditional(s32[]{:T(128)} %convert_element_type.551, f32[512,16,64]{0,2,1:T(8,128)S(1)} %get-tuple-element.1443, (pred[1,512,512]{1,2,0:T(8,128)(4,1)S(1)}, bf16[4,512,16,64]{1,3,2,0:T(8,128)(2,1)}, s32[]{:T(128)}, ...), branch_computations={%region_37.37_spmd, %region_38.38_spmd} | conditional | flops 2728394752 | bytes 93947448 | solution.py:80
  1001.8 36.6 %conditional.8 = (f32[512,16,64]{0,2,1:T(8,128)S(1)}, bf16[1,512,16,64]{1,3,2,0:T(8,128)(2,1)}, bf16[1,512,16,64]{1,3,2,0:T(8,128)(2,1)}) conditional(s32[]{:T(128)} %convert_element_type.551, f32[512,16,64]{0,2,1:T(8,128)S(1)} %get-tuple-element.1443, (pred[1,512,512]{1,2,0:T(8,128)(4,1)S(1)}, bf16[4,512,16,64]{1,3,2,0:T(8,128)(2,1)}, s32[]{:T(128)}, ...), branch_computations={%region_37.37_spmd, %region_38.38_spmd} | conditional | flops 2728394752 | bytes 93947448 | solution.py:80
  1094.1 86.5 %reduce-scatter.18.cloned.1.call-done = bf16[512,1024]{0,1:T(8,128)(2,1)} async-done(((bf16[2048,1024]{0,1:T(8,128)(2,1)}), bf16[512,1024]{0,1:T(8,128)(2,1)}) %reduce-scatter.18.cloned.1.call-update) | async-done | bytes 1048592 | tf_op jit(solution)/shard_map/reduce_scatter | solution.py:398
  1180.6 47.1 %reduce-scatter.16.cloned.1.call-done = bf16[512,1024]{0,1:T(8,128)(2,1)} async-done(((bf16[2048,1024]{0,1:T(8,128)(2,1)}), bf16[512,1024]{0,1:T(8,128)(2,1)}) %reduce-scatter.16.cloned.1.call-update) | async-done | bytes 1048592 | tf_op jit(solution)/shard_map/reduce_scatter | solution.py:395
  1283.1 36.2 %reduce-scatter.36.cloned.1.call-done = bf16[128,2048]{1,0:T(8,128)(2,1)} async-done(((bf16[1024,2048]{1,0:T(8,128)(2,1)}), bf16[128,2048]{1,0:T(8,128)(2,1)}) %reduce-scatter.36.cloned.1.call-update) | async-done | bytes 524304
  1321.4 118.5 %reduce-scatter.34.cloned.1.call-done = bf16[128,3072]{1,0:T(8,128)(2,1)} async-done(((bf16[1024,3072]{1,0:T(8,128)(2,1)}), bf16[128,3072]{1,0:T(8,128)(2,1)}) %reduce-scatter.34.cloned.1.call-update) | async-done | bytes 786448
  1442.2 67.1 %reduce-scatter.28.cloned.1.call-done = bf16[128,1024]{1,0:T(8,128)(2,1)} async-done(((bf16[1024,1024]{1,0:T(8,128)(2,1)}), bf16[128,1024]{1,0:T(8,128)(2,1)}) %reduce-scatter.28.cloned.1.call-update) | async-done | bytes 262160 | tf_op jit(solution)/shard_map/reduce_scatter | solution.py:440
  1509.3 70.6 %reduce-scatter.26.cloned.1.call-done = bf16[128,1024]{1,0:T(8,128)(2,1)} async-done(((bf16[1024,1024]{1,0:T(8,128)(2,1)}), bf16[128,1024]{1,0:T(8,128)(2,1)}) %reduce-scatter.26.cloned.1.call-update) | async-done | bytes 262160 | tf_op jit(solution)/shard_map/reduce_scatter | solution.py:434
  1579.9 71.1 %reduce-scatter.24.cloned.1.call-done = bf16[128,1024]{1,0:T(8,128)(2,1)} async-done(((bf16[1024,1024]{1,0:T(8,128)(2,1)}), bf16[128,1024]{1,0:T(8,128)(2,1)}) %reduce-scatter.24.cloned.1.call-update) | async-done | bytes 262160 | tf_op jit(solution)/shard_map/reduce_scatter | solution.py:416
  1651.0 152.6 %reduce-scatter.32.cloned.1.call-done = bf16[512,1024]{1,0:T(8,128)(2,1)} async-done(((bf16[4096,1024]{1,0:T(8,128)(2,1)}), bf16[512,1024]{1,0:T(8,128)(2,1)}) %reduce-scatter.32.cloned.1.call-update) | async-done | bytes 1048592 | tf_op jit(solution)/shard_map/reduce_scatter | solution.py:461
  1803.7 151.7 %reduce-scatter.30.cloned.1.call-done = bf16[128,4096]{1,0:T(8,128)(2,1)} async-done(((bf16[1024,4096]{1,0:T(8,128)(2,1)}), bf16[128,4096]{1,0:T(8,128)(2,1)}) %reduce-scatter.30.cloned.1.call-update) | async-done | bytes 1048592 | tf_op jit(solution)/shard_map/reduce_scatter | solution.py:458
  1958.0 24.8 %all-reduce.14 = (bf16[1024]{0:T(1024)(128)(2,1)S(1)}, bf16[1024]{0:T(1024)(128)(2,1)S(1)}, bf16[1024]{0:T(1024)(128)(2,1)S(1)}, bf16[1024]{0:T(1024)(128)(2,1)S...) all-reduce(bf16[1024]{0:T(1024)(128)(2,1)S(1)} %reduce_sum.327, ...), channel_id=8, replica_groups=mesh['ctx'=4,'fsdp'=8] {'fsdp'}, use_global_device_ids=true, to_apply=%region_49.50.clone | all-reduce | flops 17408 | bytes 69632
  2018.3 27.9 %all-reduce.19.cloned.1.call-done = (bf16[128,3072]{0,1:T(8,128)(2,1)}, bf16[128,2048]{0,1:T(8,128)(2,1)}, bf16[128,1024]{1,0:T(8,128)(2,1)}, bf16[128,1024]{1,0...) async-done(((bf16[128,3072]{0,1:T(8,128)(2,1)}, bf16[128,2048]{0,1:T(8,128)(2,1)}, bf16[128,1024]{1,0:T(8,128)(2,1)}, ...) | async-done | bytes 4194320 | tf_op jit(solution)/shard_map/psum | solution.py:478
  (504 shorter events, 972.7 us)
Async XLA Ops:
  7.2 74.9 %all-gather.34.cloned.1.call-start = ((), (), s32[]{:S(2)}) async-start(), calls=%async_computation.15 | async-start | bytes 4718592 | tf_op jit(solution)/shard_map/all_gather | solution.py:272
  7.9 173.3 %all-gather.26.cloned.1.call-start = ((), (), s32[]{:S(2)}) async-start(), calls=%async_computation.11 | async-start | bytes 7077888 | tf_op jit(solution)/shard_map/all_gather | solution.py:236
  8.7 385.3 %all-gather.36.cloned.1.call-start = ((), (), s32[]{:S(2)}) async-start(), calls=%async_computation.16 | async-start | bytes 5242880 | tf_op jit(solution)/shard_map/all_gather | solution.py:290
  89.9 325.5 %all-gather.38.cloned.1.call-start = ((), (), s32[]{:S(2)}) async-start(), calls=%async_computation.17 | async-start | bytes 5242880 | tf_op jit(solution)/shard_map/all_gather | solution.py:289
  92.7 344.0 %all-gather.28.cloned.1.call-start = ((), (), s32[]{:S(2)}) async-start(), calls=%async_computation.12 | async-start | bytes 5242880 | tf_op jit(solution)/shard_map/all_gather | solution.py:249
  190.6 289.7 %all-gather.30.cloned.1.call-start = ((), (), s32[]{:S(2)}) async-start(), calls=%async_computation.13 | async-start | bytes 5242880 | tf_op jit(solution)/shard_map/all_gather | solution.py:250
  222.8 309.5 %all-gather.32.cloned.1.call-start = ((), (), s32[]{:S(2)}) async-start(), calls=%async_computation.14 | async-start | bytes 2359296 | tf_op jit(solution)/shard_map/all_gather | solution.py:237
  223.5 314.9 %all-gather.40.cloned.1.call-start = ((), (), s32[]{:S(2)}) async-start(), calls=%async_computation.18 | async-start | bytes 2359296 | tf_op jit(solution)/shard_map/all_gather | solution.py:271
  224.3 423.6 %all-gather.42.cloned.1.call-start = ((), (), s32[]{:S(2)}) async-start(), calls=%async_computation.19 | async-start | bytes 2359296 | tf_op jit(solution)/shard_map/all_gather | solution.py:273
  225.0 428.8 %all-gather.44.cloned.1.call-start = ((), (), s32[]{:S(2)}) async-start(), calls=%async_computation.20 | async-start | bytes 9437184 | tf_op jit(solution)/shard_map/all_gather | solution.py:305
  225.6 502.3 %all-gather.46.cloned.1.call-start = ((), (), s32[]{:S(2)}) async-start(), calls=%async_computation.21 | async-start | bytes 9437184 | tf_op jit(solution)/shard_map/all_gather | solution.py:306
  226.3 849.5 %reduce-scatter.20.cloned.1.call-start = ((), (), s32[]{:S(2)}) async-start(), calls=%async_computation.24 | async-start | bytes 5242880 | tf_op jit(solution)/shard_map/reduce_scatter | solution.py:356
  922.3 155.8 %reduce-scatter.22.cloned.1.call-start = ((), (), s32[]{:S(2)}) async-start(), calls=%async_computation.25 | async-start | bytes 5242880 | tf_op jit(solution)/shard_map/reduce_scatter | solution.py:359
  931.5 249.1 %reduce-scatter.18.cloned.1.call-start = ((), (), s32[]{:S(2)}) async-start(), calls=%async_computation.23 | async-start | bytes 5242880 | tf_op jit(solution)/shard_map/reduce_scatter | solution.py:398
  1066.4 161.2 %reduce-scatter.16.cloned.1.call-start = ((), (), s32[]{:S(2)}) async-start(), calls=%async_computation.22 | async-start | bytes 5242880 | tf_op jit(solution)/shard_map/reduce_scatter | solution.py:395
  1075.5 243.8 %reduce-scatter.36.cloned.1.call-start = ((), (), s32[]{:S(2)}) async-start(), calls=%async_computation.32 | async-start | bytes 4718592
  1092.9 347.0 %reduce-scatter.34.cloned.1.call-start = ((), (), s32[]{:S(2)}) async-start(), calls=%async_computation.31 | async-start | bytes 7077888
  1244.4 264.9 %reduce-scatter.28.cloned.1.call-start = ((), (), s32[]{:S(2)}) async-start(), calls=%async_computation.28 | async-start | bytes 2359296 | tf_op jit(solution)/shard_map/reduce_scatter | solution.py:440
  1249.2 330.7 %reduce-scatter.26.cloned.1.call-start = ((), (), s32[]{:S(2)}) async-start(), calls=%async_computation.27 | async-start | bytes 2359296 | tf_op jit(solution)/shard_map/reduce_scatter | solution.py:434
  1253.4 397.6 %reduce-scatter.24.cloned.1.call-start = ((), (), s32[]{:S(2)}) async-start(), calls=%async_computation.26 | async-start | bytes 2359296 | tf_op jit(solution)/shard_map/reduce_scatter | solution.py:416
  1258.2 545.4 %reduce-scatter.32.cloned.1.call-start = ((), (), s32[]{:S(2)}) async-start(), calls=%async_computation.30 | async-start | bytes 9437184 | tf_op jit(solution)/shard_map/reduce_scatter | solution.py:461
  1272.2 683.2 %reduce-scatter.30.cloned.1.call-start = ((), (), s32[]{:S(2)}) async-start(), calls=%async_computation.29 | async-start | bytes 9437184 | tf_op jit(solution)/shard_map/reduce_scatter | solution.py:458
  1283.0 674.6 %copy-start.27 = (bf16[512,1024]{0,1:T(8,128)(2,1)S(1)}, bf16[512,1024]{0,1:T(8,128)(2,1)}, u32[]{:S(2)}) copy-start(bf16[512,1024]{0,1:T(8,128)(2,1)} %reduce-scatter.18.cloned.1.call-done) | copy-start | bytes 3145732
  1283.1 763.1 %all-reduce.19.cloned.1.call-start = ((), (), s32[]{:S(2)}) async-start(), calls=%async_computation.33 | async-start | bytes 8388608 | tf_op jit(solution)/shard_map/psum | solution.py:478
  (93 other events, 10888.7 us)
Sparse Core Ops, SparseCore 0:
  10.2 71.9 all-gather.33
  84.3 96.9 all-gather.25
  183.4 36.0 all-gather.35
  221.5 34.4 all-gather.37
  258.0 34.4 all-gather.27
  294.5 34.4 all-gather.29
  331.1 47.1 all-gather.31
  380.5 47.8 all-gather.39
  430.5 47.7 all-gather.41
  480.4 122.2 all-gather.43
  604.8 123.1 all-gather.45
  922.4 46.2 reduce-scatter.19
  971.4 44.4 reduce-scatter.21
  1066.5 114.0 reduce-scatter.17
  1183.1 44.4 reduce-scatter.15
  1231.1 88.1 reduce-scatter.35
  1323.1 116.7 reduce-scatter.33
  1443.7 65.5 reduce-scatter.27
  1513.2 66.5 reduce-scatter.25
  1584.2 66.7 reduce-scatter.23
  1655.1 148.5 reduce-scatter.31
  1807.3 148.0 reduce-scatter.29
  1959.0 87.1 all-reduce.18
where the time goes:
time: 2090 us; the launch traced here: 2070 us
  waiting for transfers between devices  1050 us (50%)
  matrix products  447 us (21%)
  blocking collectives  233 us (11%)
  local copies, waits for them, and re-layouts  205 us (10%)
  other arithmetic  104 us (5%)
    unnamed x25, waiting for transfers between devices  160 us
    reduce_scatter x1, waiting for transfers between devices, shards(): lax.psum_scatter(grad_reduce_weight.astype(jnp.bfloat16), 'fsdp', scatter...  153 us
    reduce_scatter x1, waiting for transfers between devices, shards(): lax.psum_scatter(grad_expand_weight.astype(jnp.bfloat16), 'fsdp', scatter...  152 us
    dot_general x12, matrix products, masked_scores(): jnp.einsum('qhd,khd->hqk', query_heads, key_piece, preferred_element_type...  102 us
    all_gather x1, waiting for transfers between devices, shards(): lax.all_gather(self_projection, 'fsdp', axis=0, tiled=True)  88.5 us
    reduce_scatter x1, waiting for transfers between devices, shards(): lax.psum_scatter(value_terms.astype(jnp.bfloat16), 'ctx', scatter_dimensi...  86.5 us
    unnamed x197, local copies, waits for them, and re-layouts  75.5 us
    reduce_scatter x1, waiting for transfers between devices, shards(): lax.psum_scatter(grad_self_output.astype(jnp.bfloat16), 'fsdp', scatter_d...  71.1 us
  transfers between devices with their start and end apart: 23, of which 13 were waited for; matrix products, arithmetic and copies ran while one was open for 26% of the time, Pallas kernels for 0%

commit v1 on v0

--- a/solution.py
+++ b/solution.py
@@ -1,8 +1,11 @@
+import functools
 import math
 
 import jax
 import jax.numpy as jnp
 from jax import lax
+from jax.experimental import pallas as pl
+from jax.experimental.pallas import tpu as pltpu
 from jax.sharding import PartitionSpec as P
 
 HEADS = 16
@@ -43,6 +46,587 @@
         - normed * jnp.mean(scaled * normed, axis=-1, keepdims=True)
     )
     return (inner * inverse, jnp.sum(upstream * normed, axis=0), jnp.sum(upstream, axis=0))
+
+
+score_log2 = 0.125 * math.log2(math.e)
+NT = (((1,), (1,)), ((), ()))
+NN = (((1,), (0,)), ((), ()))
+TN = (((0,), (0,)), ((), ()))
+
+
+def mxu(left, right, dims):
+    return lax.dot_general(left, right, dims, preferred_element_type=jnp.float32)
+
+
+def two_heads(pair):
+    low = lax.broadcasted_iota(jnp.int32, pair.shape, 1) < 64
+    zero = jnp.zeros_like(pair)
+    return jnp.concatenate([jnp.where(low, pair, zero), jnp.where(low, zero, pair)], axis=0)
+
+
+def one_pair(stacked):
+    rows = stacked.shape[0] // 2
+    top = stacked[:rows]
+    low = lax.broadcasted_iota(jnp.int32, top.shape, 1) < 64
+    return jnp.where(low, top, stacked[rows:])
+
+
+def place_of(order_ref, slot_ref, index, per_group):
+    return order_ref[slot_ref[0] ^ (index // per_group)] * per_group + index % per_group
+
+
+def seen(scalars, query_index, key_index, per_group, count):
+    if scalars is None:
+        return None
+    order_ref, map_ref, slot_ref = scalars
+    row = place_of(order_ref, slot_ref, query_index, per_group)
+    column = place_of(order_ref, slot_ref, key_index, per_group)
+    return map_ref[row * count + column] > 0
+
+
+def guarded(flag, work):
+    if flag is None:
+        work()
+    else:
+        pl.when(flag)(work)
+
+
+def pair_lanes(unit):
+    return slice(unit * 128, (unit + 1) * 128)
+
+
+def forward_body(masked, units, chunks, key_rows, pieces, per_group, *refs):
+    scalars = None
+    if masked:
+        scalars, refs = refs[:3], refs[3:]
+    q_ref, refs = refs[0], refs[1:]
+    k_refs, v_refs, refs = refs[:pieces], refs[pieces:2 * pieces], refs[2 * pieces:]
+    o_ref, lse_ref, stacked, scores, top, shift, total, acc = refs
+    rows = stacked.shape[1]
+    query_index = pl.program_id(1)
+
+    def part(ref_list, chunk, unit):
+        if pieces > 1:
+            return ref_list[chunk][:, pair_lanes(unit)]
+        return ref_list[0][chunk * key_rows:(chunk + 1) * key_rows, pair_lanes(unit)]
+
+    for unit in range(units):
+        stacked[unit] = two_heads(q_ref[:, pair_lanes(unit)])
+        top[unit] = jnp.full((rows, 128), -1e30, jnp.float32)
+        total[unit] = jnp.zeros((rows, 128), jnp.float32)
+        acc[unit] = jnp.zeros((rows, 128), jnp.float32)
+    for chunk in range(chunks):
+        flag = seen(scalars, query_index, chunk, per_group, chunks)
+
+        def scan_max(chunk=chunk):
+            for unit in range(units):
+                found = mxu(stacked[unit], part(k_refs, chunk, unit), NT)
+                scores[unit, chunk] = found
+                best = top[unit]
+                for lane in range(0, key_rows, 128):
+                    best = jnp.maximum(best, found[:, lane:lane + 128])
+                top[unit] = best
+
+        guarded(flag, scan_max)
+    for unit in range(units):
+        peak = jnp.max(top[unit], axis=1, keepdims=True) * score_log2
+        shift[unit] = jnp.broadcast_to(peak, (rows, 128))
+    for chunk in range(chunks):
+        flag = seen(scalars, query_index, chunk, per_group, chunks)
+
+        def weigh(chunk=chunk):
+            for unit in range(units):
+                found = scores[unit, chunk]
+                offset = shift[unit]
+                summed = total[unit]
+                parts = []
+                for lane in range(0, key_rows, 128):
+                    weight = jnp.exp2(found[:, lane:lane + 128] * score_log2 - offset)
+                    summed = summed + weight
+                    parts.append(weight.astype(jnp.bfloat16))
+                total[unit] = summed
+                acc[unit] = acc[unit] + mxu(jnp.concatenate(parts, axis=1), part(v_refs, chunk, unit), NN)
+
+        guarded(flag, weigh)
+    for unit in range(units):
+        row_sum = jnp.sum(total[unit], axis=1, keepdims=True)
+        o_ref[:, pair_lanes(unit)] = one_pair(acc[unit] / row_sum).astype(o_ref.dtype)
+        lse = shift[unit] + jnp.log2(row_sum)
+        lse_ref[unit] = lse.T[:8]
+
+
+def backward_body(masked, units, chunks, key_rows, pieces, per_group, *refs):
+    scalars = None
+    if masked:
+        scalars, refs = refs[:3], refs[3:]
+    q_ref, do_ref, o_ref, lse_ref, refs = refs[0], refs[1], refs[2], refs[3], refs[4:]
+    k_refs, v_refs, refs = refs[:pieces], refs[pieces:2 * pieces], refs[2 * pieces:]
+    dq_ref, dk_refs, dv_refs, refs = refs[0], refs[1:1 + pieces], refs[1 + pieces:1 + 2 * pieces], refs[1 + 2 * pieces:]
+    stacked, grads, delta, dq_acc, dk_acc, dv_acc = refs
+    query_index = pl.program_id(1)
+
+    def part(ref_list, chunk, unit):
+        if pieces > 1:
+            return ref_list[chunk][:, pair_lanes(unit)]
+        return ref_list[0][chunk * key_rows:(chunk + 1) * key_rows, pair_lanes(unit)]
+
+    @pl.when(query_index == 0)
+    def clear():
+        dk_acc[...] = jnp.zeros_like(dk_acc)
+        dv_acc[...] = jnp.zeros_like(dv_acc)
+
+    for unit in range(units):
+        lanes = pair_lanes(unit)
+        stacked[unit] = two_heads(q_ref[:, lanes])
+        upstream = do_ref[:, lanes]
+        grads[unit] = two_heads(upstream)
+        product = (upstream.astype(jnp.float32) * o_ref[:, lanes].astype(jnp.float32)).T
+        first = jnp.sum(product[:64], axis=0, keepdims=True)
+        second = jnp.sum(product[64:], axis=0, keepdims=True)
+        delta[unit] = jnp.broadcast_to(jnp.concatenate([first, second], axis=1), delta.shape[1:])
+        dq_acc[unit] = jnp.zeros(dq_acc.shape[1:], jnp.float32)
+    for chunk in range(chunks):
+        flag = seen(scalars, query_index, chunk, per_group, chunks)
+
+        def step(chunk=chunk):
+            for unit in range(units):
+                queries, upstream = stacked[unit], grads[unit]
+                keys, values = part(k_refs, chunk, unit), part(v_refs, chunk, unit)
+                found = mxu(keys, queries, NT)
+                probs = jnp.exp2(found * score_log2 - lse_ref[unit, 0:1])
+                grad_probs = mxu(values, upstream, NT)
+                grad_scores = (probs * (grad_probs - delta[unit, 0:1])).astype(jnp.bfloat16)
+                dv_acc[unit, chunk] += mxu(probs.astype(jnp.bfloat16), upstream, NN)
+                dk_acc[unit, chunk] += mxu(grad_scores, queries, NN)
+                dq_acc[unit] += mxu(grad_scores, keys, TN)
+
+        guarded(flag, step)
+    for unit in range(units):
+        dq_ref[:, pair_lanes(unit)] = (one_pair(dq_acc[unit]) * 0.125).astype(dq_ref.dtype)
+
+    @pl.when(query_index == pl.num_programs(1) - 1)
+    def finish():
+        for unit in range(units):
+            for chunk in range(chunks):
+                if pieces > 1:
+                    rows = slice(None)
+                    dk_ref, dv_ref = dk_refs[chunk], dv_refs[chunk]
+                else:
+                    rows = slice(chunk * key_rows, (chunk + 1) * key_rows)
+                    dk_ref, dv_ref = dk_refs[0], dv_refs[0]
+                dk_ref[rows, pair_lanes(unit)] = (dk_acc[unit, chunk] * 0.125).astype(dk_ref.dtype)
+                dv_ref[rows, pair_lanes(unit)] = dv_acc[unit, chunk].astype(dv_ref.dtype)
+
+
+def attention_forward(q, q_col, k_list, k_col, v_list, v_col, width, scalars, key_rows, units=2, per_group=2):
+    pieces = len(k_list)
+    lanes = units * 128
+    rows = q.shape[0]
+    keys = sum(k.shape[0] for k in k_list)
+    chunks = keys // key_rows
+    groups, blocks = width // lanes, rows // BLK
+    masked = scalars is not None
+    spec_q = pl.BlockSpec((BLK, lanes), lambda h, i, *_: (i, q_col + h))
+    specs_k = [pl.BlockSpec((k.shape[0], lanes), lambda h, i, *_: (0, k_col + h)) for k in k_list]
+    specs_v = [pl.BlockSpec((v.shape[0], lanes), lambda h, i, *_: (0, v_col + h)) for v in v_list]
+    body = functools.partial(forward_body, masked, units, chunks, key_rows, pieces, per_group)
+    pairs = rows * keys * (width // 64)
+    return pl.pallas_call(
+        body,
+        grid_spec=pltpu.PrefetchScalarGridSpec(
+            num_scalar_prefetch=3 if masked else 0,
+            grid=(groups, blocks),
+            in_specs=[spec_q] + specs_k + specs_v,
+            out_specs=[
+                pl.BlockSpec((BLK, lanes), lambda h, i, *_: (i, h)),
+                pl.BlockSpec((units, 8, 2 * BLK), lambda h, i, *_: (h, 0, i)),
+            ],
+            scratch_shapes=[
+                pltpu.VMEM((units, 2 * BLK, 128), jnp.bfloat16),
+                pltpu.VMEM((units, chunks, 2 * BLK, key_rows), jnp.float32),
+                pltpu.VMEM((units, 2 * BLK, 128), jnp.float32),
+                pltpu.VMEM((units, 2 * BLK, 128), jnp.float32),
+                pltpu.VMEM((units, 2 * BLK, 128), jnp.float32),
+                pltpu.VMEM((units, 2 * BLK, 128), jnp.float32),
+            ],
+        ),
+        out_shape=[
+            jax.ShapeDtypeStruct((rows, width), jnp.bfloat16),
+            jax.ShapeDtypeStruct((width // 128, 8, blocks * 2 * BLK), jnp.float32),
+        ],
+        compiler_params=pltpu.CompilerParams(vmem_limit_bytes=48 << 20),
+        cost_estimate=pl.CostEstimate(flops=pairs * 512, transcendentals=pairs, bytes_accessed=4 * (rows + keys) * width),
+    )(*(scalars or ()), q, *k_list, *v_list)
+
+
+def attention_backward(q, q_col, do, o, lse, k_list, k_col, v_list, v_col, width, scalars, key_rows, units=2, per_group=2):
+    pieces = len(k_list)
+    lanes = units * 128
+    rows = q.shape[0]
+    keys = sum(k.shape[0] for k in k_list)
+    chunks = keys // key_rows
+    groups, blocks = width // lanes, rows // BLK
+    masked = scalars is not None
+    spec_q = pl.BlockSpec((BLK, lanes), lambda h, i, *_: (i, q_col + h))
+    spec_o = pl.BlockSpec((BLK, lanes), lambda h, i, *_: (i, h))
+    spec_lse = pl.BlockSpec((units, 8, 2 * BLK), lambda h, i, *_: (h, 0, i))
+    specs_k = [pl.BlockSpec((k.shape[0], lanes), lambda h, i, *_: (0, k_col + h)) for k in k_list]
+    specs_v = [pl.BlockSpec((v.shape[0], lanes), lambda h, i, *_: (0, v_col + h)) for v in v_list]
+    outs_k = [pl.BlockSpec((k.shape[0], lanes), lambda h, i, *_: (0, h)) for k in k_list]
+    body = functools.partial(backward_body, masked, units, chunks, key_rows, pieces, per_group)
+    pairs = rows * keys * (width // 64)
+    shape_k = [jax.ShapeDtypeStruct((k.shape[0], width), jnp.bfloat16) for k in k_list]
+    return pl.pallas_call(
+        body,
+        grid_spec=pltpu.PrefetchScalarGridSpec(
+            num_scalar_prefetch=3 if masked else 0,
+            grid=(groups, blocks),
+            in_specs=[spec_q, spec_o, spec_o, spec_lse] + specs_k + specs_v,
+            out_specs=[spec_o] + outs_k + outs_k,
+            scratch_shapes=[
+                pltpu.VMEM((units, 2 * BLK, 128), jnp.bfloat16),
+                pltpu.VMEM((units, 2 * BLK, 128), jnp.bfloat16),
+                pltpu.VMEM((units, 8, 2 * BLK), jnp.float32),
+                pltpu.VMEM((units, 2 * BLK, 128), jnp.float32),
+                pltpu.VMEM((units, chunks, key_rows, 128), jnp.float32),
+                pltpu.VMEM((units, chunks, key_rows, 128), jnp.float32),
+            ],
+        ),
+        out_shape=[jax.ShapeDtypeStruct((rows, width), jnp.bfloat16)] + shape_k + shape_k,
+        compiler_params=pltpu.CompilerParams(vmem_limit_bytes=48 << 20),
+        cost_estimate=pl.CostEstimate(flops=pairs * 1280, transcendentals=pairs, bytes_accessed=8 * (rows + keys) * width),
+    )(*(scalars or ()), q, do, o, lse, *k_list, *v_list)
+
+
+def core_perm():
+    return [(c, c ^ 1) for c in range(4)]
+
+
+def y_perm():
+    return [(c, c ^ 2) for c in range(4)]
+
+
+def diagonal_perm():
+    return [(c, c ^ 3) for c in range(4)]
+
+
+def x_perm():
+    return [(f, f ^ 1) for f in range(8)]
+
+
+def z_perm(k):
+    return [(f, f ^ (2 * k)) for f in range(8)]
+
+
+def to_core(v):
+    return lax.ppermute(v, "ctx", core_perm())
+
+
+def to_y(v):
+    return lax.ppermute(v, "ctx", y_perm())
+
+
+def to_diagonal(v):
+    return lax.ppermute(v, "ctx", diagonal_perm())
+
+
+def to_x(v):
+    return lax.ppermute(v, "fsdp", x_perm())
+
+
+def to_z(v, k):
+    return lax.ppermute(v, "fsdp", z_perm(k))
+
+
+def fsdp_pieces(own):
+    along = [own] + [to_z(own, k) for k in (1, 2, 3)]
+    return along + [to_x(piece) for piece in along]
+
+
+def fsdp_sources(me):
+    return [me ^ (2 * k + d) for d in (0, 1) for k in range(4)]
+
+
+def place_body(count, stacks, rows, *refs):
+    offsets, refs = refs[0], refs[1:]
+    pieces, outs, sems = refs[:count], refs[count:count + stacks], refs[-1]
+    copies = []
+    for i in range(count):
+        start = pl.multiple_of(offsets[i], rows)
+        for s in range(stacks):
+            source = pieces[i].at[s] if len(pieces[i].shape) == 3 else pieces[i]
+            copy = pltpu.make_async_copy(source, outs[s].at[pl.ds(start, rows)], sems.at[i, s])
+            copy.start()
+            copies.append(copy)
+    for copy in copies:
+        copy.wait()
+
+
+def place(pieces, offsets):
+    shape = pieces[0].shape
+    stacks = shape[0] if len(shape) == 3 else 1
+    rows, columns = shape[-2:]
+    count = len(pieces)
+    out = [jax.ShapeDtypeStruct((count * rows, columns), pieces[0].dtype)] * stacks
+    anywhere = pl.BlockSpec(memory_space=pl.ANY)
+    return pl.pallas_call(
+        functools.partial(place_body, count, stacks, rows),
+        in_specs=[pl.BlockSpec(memory_space=pltpu.SMEM)] + [anywhere] * count,
+        out_specs=[anywhere] * stacks,
+        out_shape=out,
+        scratch_shapes=[pltpu.SemaphoreType.DMA((count, stacks))],
+        cost_estimate=pl.CostEstimate(flops=0, transcendentals=0, bytes_accessed=4 * count * stacks * rows * columns),
+    )(jnp.stack(offsets).astype(jnp.int32), *pieces)
+
+
+def xor_take(stack, me):
+    return jnp.concatenate([lax.dynamic_index_in_dim(stack, n ^ me, 0) for n in range(stack.shape[0])])
+
+
+def sum_over_fsdp(grads, z, x, core):
+    f32, bf16 = jnp.float32, jnp.bfloat16
+    width = grads[0].shape[1]
+    halves = [g.reshape(8, 2, 64, width) for g in grads]
+    send = jnp.stack([lax.dynamic_index_in_dim(h, core ^ 1, 1, keepdims=False) for h in halves])
+    keep = jnp.stack([lax.dynamic_index_in_dim(h, core, 1, keepdims=False) for h in halves])
+    part = (keep.astype(f32) + to_core(send).astype(f32)).astype(bf16)
+    part = part.reshape(len(grads), 4, 2, 64, width)
+    send = lax.dynamic_index_in_dim(part, x ^ 1, 2, keepdims=False)
+    keep = lax.dynamic_index_in_dim(part, x, 2, keepdims=False)
+    part = (keep.astype(f32) + to_x(send).astype(f32)).astype(bf16)
+    got = [to_z(lax.dynamic_index_in_dim(part, z ^ k, 1, keepdims=False), k) for k in (1, 2, 3)]
+    total = lax.dynamic_index_in_dim(part, z, 1, keepdims=False).astype(f32)
+    for piece in got:
+        total = total + piece.astype(f32)
+    low = total.astype(bf16)
+    low = (low.astype(f32) + to_y(low).astype(f32)).astype(bf16)
+    other = to_core(low)
+    first = jnp.where(core == 0, low, other)
+    second = jnp.where(core == 0, other, low)
+    return jnp.concatenate([first, second], axis=1).astype(f32)
+
+
+def sum_everywhere(value):
+    value = value + to_core(value)
+    value = value + to_y(value)
+    value = value + to_x(value)
+    got = [to_z(value, k) for k in (1, 2, 3)]
+    return value + got[0] + got[1] + got[2]
+
+
+def tiled_shards(
+    tokens,
+    memory,
+    cotangent,
+    block_map,
+    block_order,
+    self_projection,
+    self_output,
+    self_query_bias,
+    self_value_bias,
+    self_output_bias,
+    first_gain,
+    first_shift,
+    cross_query,
+    cross_memory,
+    cross_output,
+    cross_query_bias,
+    cross_value_bias,
+    cross_output_bias,
+    second_gain,
+    second_shift,
+    expand_weight,
+    reduce_weight,
+    expand_bias,
+    reduce_bias,
+    third_gain,
+    third_shift,
+):
+    bf16 = jnp.bfloat16
+    f32 = jnp.float32
+    own_rows = tokens[0]
+    rows, width = own_rows.shape
+    me_c, me_f = lax.axis_index("ctx"), lax.axis_index("fsdp")
+    core, z, x = me_c % 2, me_f // 2, me_f % 2
+    share = width // 4
+
+    def dot(left, right):
+        return jnp.dot(left, right, preferred_element_type=f32)
+
+    rows_y = to_y(own_rows)
+    columns = [lax.dynamic_slice(self_projection, (0, part * width + me_c * share), (128, share)) for part in range(3)]
+    projection_pieces = fsdp_pieces(jnp.concatenate(columns, axis=1))
+    rows_core = to_core(own_rows)
+    rows_diagonal = to_core(rows_y)
+    sequence = jnp.concatenate([own_rows, rows_core, rows_y, rows_diagonal])
+    sources = fsdp_sources(me_f)
+    (projection,) = place(projection_pieces, [s * 128 for s in sources])
+
+    vectors = (self_query_bias, self_value_bias, self_output_bias, first_gain, first_shift, cross_query_bias,
+               cross_value_bias, cross_output_bias, second_gain, second_shift, reduce_bias, third_gain, third_shift)
+    packed = jnp.concatenate([jnp.stack(vectors), expand_bias.reshape(4, 128)])
+    gathered = lax.all_gather(packed, "fsdp", axis=0).astype(f32)
+    (query_bias, value_bias, out_bias, gain_one, shift_one, cross_qbias, cross_vbias, cross_obias,
+     gain_two, shift_two, reduce_bias_full, gain_three, shift_three) = [gathered[:, i].reshape(width) for i in range(13)]
+    expand_bias_full = gathered[:, 13:].reshape(4 * width)
+
+    expand_full = lax.all_gather(lax.dynamic_slice_in_dim(expand_weight, me_c * 32, 32), ("fsdp", "ctx"), axis=0, tiled=True)
+    reduce_full = lax.all_gather(lax.dynamic_slice_in_dim(reduce_weight, me_c * 128, 128), ("fsdp", "ctx"), axis=0, tiled=True)
+
+    middle = jnp.stack([cross_memory[:, :width], cross_memory[:, width:], self_output, cross_query, cross_output])
+    half_pieces = fsdp_pieces(lax.dynamic_slice_in_dim(middle, core * 64, 64, axis=1))
+    other_pieces = [to_core(piece) for piece in half_pieces]
+    offsets = [s * 128 + core * 64 for s in sources] + [s * 128 + (core ^ 1) * 64 for s in sources]
+    memory_key_full, memory_value_full, self_out_full, cross_query_full, cross_out_full = place(half_pieces + other_pieces, offsets)
+
+    projected = dot(sequence, projection)
+    bias = jnp.concatenate([
+        lax.dynamic_slice_in_dim(query_bias, me_c * share, share),
+        jnp.zeros((share,), f32),
+        lax.dynamic_slice_in_dim(value_bias, me_c * share, share),
+    ])
+    qkv = (projected + bias).astype(bf16)
+    scalars = (block_order[0], block_map[0].reshape(-1), me_c.reshape(1).astype(jnp.int32))
+    heads_out, self_lse = attention_forward(qkv, 0, [qkv], 1, [qkv], 2, share, scalars, BLK)
+
+    memory_rows = memory[0]
+    memory_keys = dot(memory_rows, memory_key_full).astype(bf16)
+    memory_values = (dot(memory_rows, memory_value_full) + cross_vbias).astype(bf16)
+    keys_y, values_y = to_y(memory_keys), to_y(memory_values)
+    key_list = [memory_keys, to_core(memory_keys), keys_y, to_core(keys_y)]
+    value_list = [memory_values, to_core(memory_values), values_y, to_core(values_y)]
+
+    pieces = [heads_out[i * rows:(i + 1) * rows] for i in range(4)]
+    attended = jnp.concatenate([pieces[0], to_core(pieces[1]), to_y(pieces[2]), to_diagonal(pieces[3])], axis=1)
+    self_out_rel = xor_take(self_out_full.reshape(4, share, width), me_c).reshape(width, width)
+    branch = dot(attended, self_out_rel) + out_bias
+    hidden_one, normed_one, inverse_one = layer_norm(residual_scale * own_rows.astype(f32) + branch, gain_one, shift_one)
+
+    hidden_low = hidden_one.astype(bf16)
+    cross_queries = (dot(hidden_low, cross_query_full) + cross_qbias).astype(bf16)
+    cross_low, cross_lse = attention_forward(cross_queries, 0, key_list, 0, value_list, 0, width, None, rows)
+    cross_branch = dot(cross_low, cross_out_full) + cross_obias
+    hidden_two, normed_two, inverse_two = layer_norm(residual_scale * hidden_one + cross_branch, gain_two, shift_two)
+
+    hidden_two_low = hidden_two.astype(bf16)
+    expanded = dot(hidden_two_low, expand_full) + expand_bias_full
+    activated = gelu_tanh(expanded).astype(bf16)
+    reduced = dot(activated, reduce_full) + reduce_bias_full
+    result, normed_three, inverse_three = layer_norm(residual_scale * hidden_two + reduced, gain_three, shift_three)
+    output = result.astype(bf16)[None]
+
+    upstream = cotangent[0].astype(f32)
+    grad_third, grad_third_gain, grad_third_shift = layer_norm_back(upstream, gain_three, normed_three, inverse_three)
+    grad_reduced = grad_third.astype(bf16)
+    grad_reduce_bias = jnp.sum(grad_reduced.astype(f32), axis=0)
+    grad_reduce_weight = dot(activated.T, grad_reduced).astype(bf16)
+    grad_expanded = (dot(grad_reduced, reduce_full.T) * gelu_slope(expanded)).astype(bf16)
+    grad_expand_bias = jnp.sum(grad_expanded.astype(f32), axis=0)
+    expand_parts = [
+        dot(hidden_two_low.T, grad_expanded[:, i * width:(i + 1) * width]).astype(bf16).reshape(8, 128, width)
+        for i in range(4)
+    ]
+    feed = jnp.concatenate([jnp.stack(expand_parts, axis=1), grad_reduce_weight.reshape(8, 4, 128, width)], axis=2)
+    feed_share = lax.psum_scatter(feed.reshape(32 * 256, width), ("fsdp", "ctx"), scatter_dimension=0, tiled=True)
+    grad_hidden_two = residual_scale * grad_third + dot(grad_expanded, expand_full.T)
+
+    grad_second, grad_second_gain, grad_second_shift = layer_norm_back(grad_hidden_two, gain_two, normed_two, inverse_two)
+    grad_cross_branch = grad_second.astype(bf16)
+    grad_cross_output_bias = jnp.sum(grad_cross_branch.astype(f32), axis=0)
+    grad_cross_output = dot(cross_low.T, grad_cross_branch).astype(bf16)
+    grad_cross_low = dot(grad_cross_branch, cross_out_full.T).astype(bf16)
+    cross_back = attention_backward(
+        cross_queries, 0, grad_cross_low, cross_low, cross_lse, key_list, 0, value_list, 0, width, None, rows
+    )
+    grad_cross_queries = cross_back[0]
+
+    def to_owner(terms):
+        near = terms[0].astype(f32) + to_core(terms[1]).astype(f32)
+        far = (terms[2].astype(f32) + to_core(terms[3]).astype(f32)).astype(bf16)
+        return (near + to_y(far).astype(f32)).astype(bf16)
+
+    grad_memory_keys, grad_memory_values = to_owner(cross_back[1:5]), to_owner(cross_back[5:9])
+
+    grad_cross_query_bias = jnp.sum(grad_cross_queries.astype(f32), axis=0)
+    grad_cross_query = dot(hidden_low.T, grad_cross_queries).astype(bf16)
+    grad_hidden_one = residual_scale * grad_second + dot(grad_cross_queries, cross_query_full.T)
+    grad_first, grad_first_gain, grad_first_shift = layer_norm_back(grad_hidden_one, gain_one, normed_one, inverse_one)
+    grad_branch = grad_first.astype(bf16)
+    grad_self_output_bias = jnp.sum(grad_branch.astype(f32), axis=0)
+    grad_attended = dot(grad_branch, self_out_rel.T).astype(bf16)
+    sends = [grad_attended[:, i * share:(i + 1) * share] for i in range(4)]
+    heads_grad = jnp.concatenate([sends[0], to_core(sends[1]), to_y(sends[2]), to_diagonal(sends[3])])
+    grad_self_output = xor_take(dot(attended.T, grad_branch).astype(bf16).reshape(4, share, width), me_c).reshape(width, width)
+
+    grad_cross_value_bias = jnp.sum(grad_memory_values.astype(f32), axis=0)
+    grad_memory_key_weight = dot(memory_rows.T, grad_memory_keys).astype(bf16)
+    grad_memory_value_weight = dot(memory_rows.T, grad_memory_values).astype(bf16)
+    memory_grad = (dot(grad_memory_keys, memory_key_full.T) + dot(grad_memory_values, memory_value_full.T))[None]
+    middle_sum = sum_over_fsdp(
+        [grad_cross_output, grad_cross_query, grad_memory_key_weight, grad_memory_value_weight, grad_self_output], z, x, core
+    )
+
+    grad_q, grad_k, grad_v = attention_backward(
+        qkv, 0, heads_grad, heads_out, self_lse, [qkv], 1, [qkv], 2, share, scalars, BLK
+    )
+    grad_qkv = jnp.concatenate([grad_q, grad_k, grad_v], axis=1)
+    partial = dot(grad_qkv, projection.T).astype(bf16)
+    near = partial[:rows].astype(f32) + to_core(partial[rows:2 * rows]).astype(f32)
+    far = (partial[2 * rows:3 * rows].astype(f32) + to_core(partial[3 * rows:]).astype(f32)).astype(bf16)
+    token_grad = (residual_scale * grad_first + near + to_y(far).astype(f32))[None]
+
+    own_grad = dot(sequence.T, grad_qkv).astype(bf16).reshape(4, 2, 128, 3 * share)
+    keep = lax.dynamic_index_in_dim(own_grad, x, 1, keepdims=False).astype(f32)
+    part = (keep + to_x(lax.dynamic_index_in_dim(own_grad, x ^ 1, 1, keepdims=False)).astype(f32)).astype(bf16)
+    got = [to_z(lax.dynamic_index_in_dim(part, z ^ k, 0, keepdims=False), k) for k in (1, 2, 3)]
+    total = lax.dynamic_index_in_dim(part, z, 0, keepdims=False).astype(f32)
+    total = (total + got[0].astype(f32) + got[1].astype(f32) + got[2].astype(f32)).astype(bf16)
+    shares = xor_take(jnp.stack([total, to_core(total), to_y(total), to_diagonal(total)]), me_c)
+    grad_self_projection = shares.reshape(4, 128, 3, share).transpose(1, 2, 0, 3).reshape(128, 3 * width).astype(f32)
+
+    value_sums = jnp.stack([jnp.sum(grad_q.astype(f32), axis=0), jnp.sum(grad_v.astype(f32), axis=0)])
+    own_sums = lax.dynamic_update_slice(jnp.zeros((2, width), f32), value_sums, (0, me_c * share))
+    vector_grads = jnp.concatenate([
+        jnp.stack([
+            grad_self_output_bias, grad_first_gain, grad_first_shift, grad_cross_query_bias, grad_cross_value_bias,
+            grad_cross_output_bias, grad_second_gain, grad_second_shift, grad_reduce_bias, grad_third_gain, grad_third_shift,
+        ]),
+        grad_expand_bias.reshape(8, 4, 128).transpose(1, 0, 2).reshape(4, width),
+    ])
+    early = lax.dynamic_slice_in_dim(sum_everywhere(vector_grads), me_f * 128, 128, axis=1)
+    late = lax.dynamic_slice_in_dim(sum_everywhere(own_sums), me_f * 128, 128, axis=1)
+
+    feed_all = xor_take(jnp.stack([feed_share, to_core(feed_share), to_y(feed_share), to_diagonal(feed_share)]), me_c)
+    grad_expand = feed_all[:, :128].transpose(1, 0, 2).reshape(128, 4 * width).astype(f32)
+    grad_reduce = feed_all[:, 128:].reshape(512, width).astype(f32)
+
+    grad_cross_memory = jnp.concatenate([middle_sum[2], middle_sum[3]], axis=1)
+    return (
+        output,
+        token_grad,
+        memory_grad,
+        grad_self_projection,
+        middle_sum[4],
+        late[0],
+        late[1],
+        early[0],
+        early[1],
+        early[2],
+        middle_sum[1],
+        grad_cross_memory,
+        middle_sum[0],
+        early[3],
+        early[4],
+        early[5],
+        early[6],
+        early[7],
+        grad_expand,
+        grad_reduce,
+        early[11:15].reshape(512),
+        early[8],
+        early[9],
+        early[10],
+    )
 
 
 def head_split(matrix):
@@ -179,7 +763,7 @@
     )
 
 
-def shards(
+def plain_shards(
     tokens,
     memory,
     cotangent,
@@ -554,8 +1138,9 @@
         P("fsdp"),
         P("fsdp"),
     )
+    sizes = (mesh.shape["ctx"], mesh.shape["fsdp"])
     return jax.shard_map(
-        shards,
+        tiled_shards if sizes == (4, 8) else plain_shards,
         mesh=mesh,
         in_specs=placed,
         out_specs=(

time: 2090 us -> 1270 us (0.61)
  waiting for transfers between devices: 1050 us -> 406 us
  Pallas kernels: 0 us -> 503 us
  matrix products: 447 us -> 114 us
  blocking collectives: 233 us -> 19.3 us
  local copies, waits for them, and re-layouts: 205 us -> 57.5 us
  starting transfers between devices: 1.55 us -> 98 us
  other arithmetic: 104 us -> 47.8 us
    reduce_scatter x9 -> x1, waiting for transfers between devices: 647 us -> 65.6 us  [tiled_shards(): lax.psum_scatter(feed.reshape(32 * 256, width), ('fsdp', 'ctx'), scatter_...]
    pallas_call x0 -> x6, Pallas kernels: none -> 503 us  [the longest x2 370 us: place(): pl.pallas_call(functools.partial(place_body, count, stacks, rows), in_spe...]
    ppermute x0 -> x75, waiting for transfers between devices: none -> 340 us  [the longest x18 156 us: to_z(): return lax.ppermute(v, 'fsdp', z_perm(k))]
    dot_general x64 -> x27, matrix products: 447 us -> 114 us  [dot(): return jnp.dot(left, right, preferred_element_type=f32)]
    all_gather x11 -> x2, waiting for transfers between devices: 214 us -> 0.01 us  [the longest x1 0.01 us: tiled_shards(): lax.all_gather(lax.dynamic_slice_in_dim(expand_weight, me_c * 32, 32), ('...]
    all_gather x14 -> x1, blocking collectives: 196 us -> 19.3 us  [tiled_shards(): gathered = lax.all_gather(packed, 'fsdp', axis=0).astype(f32)]
    unnamed x25 -> x3, waiting for transfers between devices: 160 us -> 0.05 us
    ppermute x0 -> x75, starting transfers between devices: none -> 97.9 us  [the longest x18 38.8 us: to_z(): return lax.ppermute(v, 'fsdp', z_perm(k))]
  transfers between devices with their start and end apart: 23 -> 78, of which waited for: 13 -> 24; matrix products, arithmetic and copies ran while one was open for 26% -> 11% of each run, Pallas kernels for 0% -> 40%
where the time goes in v1:
time: 1270 us; the launch traced here: 1260 us
  Pallas kernels  503 us (40%)
  waiting for transfers between devices  406 us (32%)
  matrix products  114 us (9%)
  starting transfers between devices  98 us (8%)
  local copies, waits for them, and re-layouts  57.5 us (5%)
  other arithmetic  47.8 us (4%)
  blocking collectives  19.3 us (2%)
  between operations  15.7 us (1%)
    pallas_call x2, Pallas kernels, place(): pl.pallas_call(functools.partial(place_body, count, stacks, rows), in_spe...  370 us
    ppermute x18, waiting for transfers between devices, to_z(): return lax.ppermute(v, 'fsdp', z_perm(k))  156 us
    ppermute x13, waiting for transfers between devices, to_y(): return lax.ppermute(v, 'ctx', y_perm())  123 us
    dot_general x27, matrix products, dot(): return jnp.dot(left, right, preferred_element_type=f32)  114 us
    pallas_call x2, Pallas kernels, attention_backward(): pl.pallas_call(body, grid_spec=pltpu.PrefetchScalarGridSpec(num_scalar_pr...  81 us
    reduce_scatter x1, waiting for transfers between devices, tiled_shards(): lax.psum_scatter(feed.reshape(32 * 256, width), ('fsdp', 'ctx'), scatter_...  65.6 us
    pallas_call x2, Pallas kernels, attention_forward(): pl.pallas_call(body, grid_spec=pltpu.PrefetchScalarGridSpec(num_scalar_pr...  52.5 us
    ppermute x18, starting transfers between devices, to_z(): return lax.ppermute(v, 'fsdp', z_perm(k))  38.8 us
  transfers between devices with their start and end apart: 78, of which 24 were waited for; matrix products, arithmetic and copies ran while one was open for 11% of the time, Pallas kernels for 40%

profile of v1, /device:TPU:11, one launch (start us, length us, event | category | flops | bytes accessed | tf_op | source)
XLA Modules:
  0.0 1260.9 jit_solution(3178146982723137100)
XLA Ops:
  19.1 23.6 %collective-permute-done.4.refs_3_ = bf16[128,768]{1,0:T(8,128)(2,1)S(1)} collective-permute-done((bf16[128,768]{1,0:T(8,128)(2,1)S(1)}, bf16[128,768]{1,0:T(8,128)(2,1)S(1)}, u32[]{:S(2)}, u32[]{:S(2)}) %collective-permute-start.4) | collective-permute-done | bytes 196640 | tf_op jit(solution)/shard_map/ppermute | solution.py:338
  65.9 41.9 %collective-permute-done.14.refs_3_ = bf16[5,64,1024]{2,1,0:T(8,128)(2,1)S(1)} collective-permute-done((bf16[5,64,1024]{2,1,0:T(8,128)(2,1)S(1)}, bf16[5,64,1024]{2,1,0:T(8,128)(2,1)S(1)}, u32[]{:S(2)}, u32[]{:S(2)}) %collective-permute-start.14) | collective-permute-done | bytes 655392 | tf_op jit(solution)/shard_map/ppermute | solution.py:338
  108.3 29.7 %collective-permute-done.15.refs_4_ = bf16[5,64,1024]{2,1,0:T(8,128)(2,1)} collective-permute-done((bf16[5,64,1024]{2,1,0:T(8,128)(2,1)S(1)}, bf16[5,64,1024]{2,1,0:T(8,128)(2,1)}, u32[]{:S(2)}, u32[]{:S(2)}) %collective-permute-start.15) | collective-permute-done | bytes 655392 | tf_op jit(solution)/shard_map/ppermute | solution.py:338
  141.3 14.2 %collective-permute-done.18.refs_7_ = bf16[5,64,1024]{2,1,0:T(8,128)(2,1)} collective-permute-done((bf16[5,64,1024]{2,1,0:T(8,128)(2,1)S(1)}, bf16[5,64,1024]{2,1,0:T(8,128)(2,1)}, u32[]{:S(2)}, u32[]{:S(2)}) %collective-permute-start.18) | collective-permute-done | bytes 655392 | tf_op jit(solution)/shard_map/ppermute | solution.py:334
  158.3 14.0 %collective-permute-done.19.refs_8_ = bf16[5,64,1024]{2,1,0:T(8,128)(2,1)} collective-permute-done((bf16[5,64,1024]{2,1,0:T(8,128)(2,1)}, bf16[5,64,1024]{2,1,0:T(8,128)(2,1)}, u32[]{:S(2)}, u32[]{:S(2)}) %collective-permute-start.19) | collective-permute-done | bytes 655392 | tf_op jit(solution)/shard_map/ppermute | solution.py:334
  178.3 19.3 %all-gather.1 = bf16[8,17,128]{2,1,0:T(8,128)(2,1)S(1)} all-gather(bf16[1,17,128]{2,1,0:T(8,128)(2,1)S(1)} %bitcast.331), channel_id=2, replica_groups=mesh['ctx'=4,'fsdp'=8] {'fsdp'}, dimensions={0}, use_global_device_ids=true | all-gather | bytes 39168 | tf_op jit(solution)/shard_map/all_gather | solution.py:468
  204.1 49.5 %shard_map.433 = bf16[1024,768]{1,0:T(8,128)(2,1)} custom-call(s32[8]{0:T(128)} %stack.254.refs_0_, bf16[128,768]{1,0:T(8,128)(2,1)} %copy-done.45, bf16[128,768]{1,0:T(8,128)(2,1)} %copy-done.59, bf16[128,768]{1,0:T(8,128)(2,1)} %copy-done.60, bf16[128,768]{1,0:T(8,128)(2,1)} %copy-done.61, bf16[128,768]{1,0:T(8,128)(2,1)} %collective-permute-done.6.refs_5_, ...), custom_call_target="tpu_custom_call" | custom-call | bytes 3145728 | tf_op jit(solution)/shard_map/pallas_call | solution.py:372
  253.7 320.1 %shard_map.435 = (bf16[1024,1024]{1,0:T(8,128)(2,1)}, bf16[1024,1024]{1,0:T(8,128)(2,1)}, bf16[1024,1024]{1,0:T(8,128)(2,1)}, bf16[1024,1024]{1,0:T(8,128)(2,1)}, bf16[1024,1024]{1,0:T(8,128)(2,1)}) custom-call(s32[16]{0:T(128)} %stack.284.refs_0_, bf16[5,64,1024]{2,1,0:T(8,128)(2,1)} %copy-done.27, bf16[5,64,1024]{2,1,0:T(8,128)(2,1)} %copy-done.46, ...), custom_call_target="tpu_custom_call" | custom-call | bytes 20971520 | tf_op jit(solution)/shard_map/pallas_call | solution.py:372
  585.2 22.8 %shard_map.434 = (bf16[2048,256]{1,0:T(8,128)(2,1)S(1)}, f32[2,8,4096]{2,1,0:T(8,128)S(1)}) custom-call(s32[4]{0:T(128)S(1)} %bitcast.291, s32[64]{0:T(128)S(1)} %reshape_squeeze.9.refs_1_, s32[1]{0:T(128)} %bitcast.2.refs_2_, bf16[2048,768]{1,0:T(8,128)(2,1)S(1)} %add_convert_fusion.1.refs_3_.refs_4_.refs_5_.refs_7_.refs_8_, ...), custom_call_target="tpu_custom_call" | custom-call | flops 8589934592 | bytes 4194304 | tf_op jit(solution)/shard_map/pallas_call | solution.py:234
  610.9 19.9 %collective-permute-done.12 = bf16[512,256]{1,0:T(8,128)(2,1)S(1)} collective-permute-done((bf16[512,256]{1,0:T(8,128)(2,1)S(1)}, bf16[512,256]{1,0:T(8,128)(2,1)S(1)}, u32[]{:S(2)}, u32[]{:S(2)}) %collective-permute-start.12) | collective-permute-done | bytes 262176 | tf_op jit(solution)/shard_map/ppermute | solution.py:330
  645.8 29.7 %shard_map.436 = (bf16[512,1024]{1,0:T(8,128)(2,1)S(1)}, f32[8,8,1024]{2,1,0:T(8,128)S(1)}) custom-call(bf16[512,1024]{1,0:T(8,128)(2,1)S(1)} %add_convert_fusion.9.refs_0_, bf16[512,1024]{1,0:T(8,128)(2,1)S(1)} %fusion.20.refs_1_.refs_4_, bf16[512,1024]{1,0:T(8,128)(2,1)S(1)} %collective-permute-done.28.refs_2_.refs_5_, ...), custom_call_target="tpu_custom_call" | custom-call | flops 8589934592 | bytes 10485760 | tf_op jit(solution)/shard_map/pallas_call | solution.py:234
  679.9 11.7 fusion.65
  691.6 10.9 fusion.64
  707.6 10.9 convolution_convert_fusion
  718.5 15.7 %convert_reduce_fusion = (f32[4096]{0:T(1024)S(1)}, bf16[512,4096]{1,0:T(8,128)(2,1)}) fusion(f32[512,4096]{1,0:T(8,128)} %fusion.65, f32[4096]{0:T(1024)S(1)} %bitcast.347, bf16[4096,1024]{1,0:T(8,128)(2,1)} %all-gather.7.cloned.1.call-done, f32[512,1024]{1,0:T(8,128)S(1)} %get-tuple-element.126), kind=kOutput, calls=%fused_computation.11 | convolution fusion | flops 4341624832 | bytes 23101440 | tf_op jit(solution)/shard_map/dot_general | solution.py:454
  763.7 52.5 %shard_map.437 = (bf16[512,1024]{1,0:T(8,128)(2,1)S(1)}, bf16[512,1024]{1,0:T(8,128)(2,1)S(1)}, bf16[512,1024]{1,0:T(8,128)(2,1)S(1)}, bf16[512,1024]{1,0:T(8,12...) custom-call(bf16[512,1024]{1,0:T(8,128)(2,1)} %copy-done.12, ...), custom_call_target="tpu_custom_call" | custom-call | flops 21474836480 | bytes 20971520 | tf_op jit(solution)/shard_map/pallas_call | solution.py:279
  838.3 39.4 %collective-permute-done.45 = bf16[512,1024]{1,0:T(8,128)(2,1)S(1)} collective-permute-done((bf16[512,1024]{1,0:T(8,128)(2,1)S(1)}, bf16[512,1024]{1,0:T(8,128)(2,1)S(1)}, u32[]{:S(2)}, u32[]{:S(2)}) %collective-permute-start.45) | collective-permute-done | bytes 1048608 | tf_op jit(solution)/shard_map/ppermute | solution.py:326
  879.3 43.2 %collective-permute-done.42 = bf16[512,1024]{1,0:T(8,128)(2,1)S(1)} collective-permute-done((bf16[512,1024]{1,0:T(8,128)(2,1)S(1)}, bf16[512,1024]{1,0:T(8,128)(2,1)S(1)}, u32[]{:S(2)}, u32[]{:S(2)}) %collective-permute-start.42) | collective-permute-done | bytes 1048608 | tf_op jit(solution)/shard_map/ppermute | solution.py:326
  926.3 65.6 %reduce-scatter.2.cloned.1.call-done = bf16[256,1024]{1,0:T(8,128)(2,1)} async-done(((bf16[8192,1024]{1,0:T(8,128)(2,1)}), bf16[256,1024]{1,0:T(8,128)(2,1)}) %reduce-scatter.2.cloned.1.call-update) | async-done | bytes 524304 | tf_op jit(solution)/shard_map/reduce_scatter | solution.py:530
  1021.8 28.5 %shard_map.438 = (bf16[2048,256]{1,0:T(8,128)(2,1)S(1)}, bf16[2048,256]{1,0:T(8,128)(2,1)S(1)}, bf16[2048,256]{1,0:T(8,128)(2,1)S(1)}) custom-call(s32[4]{0:T(128)S(1)} %bitcast.292, s32[64]{0:T(128)S(1)} %copy-done.4, s32[1]{0:T(128)} %bitcast.2.refs_2_, bf16[2048,768]{1,0:T(8,128)(2,1)} %copy-done.13, bf16[2048,256]{1,0:T(8,128)(2,1)S(1)} %pad_maximum_fusion.7.refs_4_, ...), custom_call_target="tpu_custom_call" | custom-call | flops 21474836480 | bytes 8388608 | tf_op jit(solution)/shard_map/pallas_call | solution.py:279
  1069.0 14.3 %collective-permute-start.65 = (f32[2,1024]{1,0:T(2,128)S(1)}, f32[2,1024]{1,0:T(2,128)S(1)}, u32[]{:S(2)}, u32[]{:S(2)}) collective-permute-start(f32[2,1024]{1,0:T(2,128)S(1)} %add.512), channel_id=1, source_target_pairs={{0,6},{1,7},{2,4},{3,5},{4,2},{5,3},{6,0},{7,1},{8,14},{9,15},{10,... | collective-permute-start | bytes 24584 | tf_op jit(solution)/shard_map/ppermute | solution.py:338
  1139.4 16.7 %collective-permute-done.67 = f32[15,1024]{1,0:T(8,128)S(1)} collective-permute-done((f32[15,1024]{1,0:T(8,128)S(1)}, f32[15,1024]{1,0:T(8,128)S(1)}, u32[]{:S(2)}, u32[]{:S(2)}) %collective-permute-start.67) | collective-permute-done | bytes 61472 | tf_op jit(solution)/shard_map/ppermute | solution.py:326
  1173.8 38.0 %collective-permute-done.57 = bf16[5,64,1024]{2,1,0:T(8,128)(2,1)S(1)} collective-permute-done((bf16[5,64,1024]{2,1,0:T(8,128)(2,1)S(1)}, bf16[5,64,1024]{2,1,0:T(8,128)(2,1)S(1)}, u32[]{:S(2)}, u32[]{:S(2)}) %collective-permute-start.57) | collective-permute-done | bytes 655392 | tf_op jit(solution)/shard_map/ppermute | solution.py:338
  1211.8 11.4 collective-permute-done.56
  (493 shorter events, 301.7 us)
Async XLA Ops:
  7.2 672.6 %all-gather.5.cloned.1.call-start = ((), (), s32[]{:S(2)}) async-start(), calls=%async_computation.1 | async-start | bytes 8650752 | tf_op jit(solution)/shard_map/all_gather | solution.py:473
  9.1 682.4 %all-gather.7.cloned.1.call-start = ((), (), s32[]{:S(2)}) async-start(), calls=%async_computation.2 | async-start | bytes 8650752 | tf_op jit(solution)/shard_map/all_gather | solution.py:474
  10.9 981.0 %reduce-scatter.2.cloned.1.call-start = ((), (), s32[]{:S(2)}) async-start(), calls=%async_computation.3 | async-start | bytes 17301504 | tf_op jit(solution)/shard_map/reduce_scatter | solution.py:530
  43.0 97.8 %collective-permute-start.1 = (bf16[512,1024]{1,0:T(8,128)(2,1)S(1)}, bf16[512,1024]{1,0:T(8,128)(2,1)}, u32[]{:S(2)}, u32[]{:S(2)}) collective-permute-start(bf16[512,1024]{1,0:T(8,128)(2,1)S(1)} %bitcast.384), channel_id=1, source_target_pairs={{0,16},{8,24},{16,0},{24,8},{1,17},{9,25},{17,1},{25,9},{2,18},{10... | collective-permute-start | bytes 3145736 | tf_op jit(solution)/shard_map/ppermute | solution.py:326
  44.4 63.5 %collective-permute-start.14 = (bf16[5,64,1024]{2,1,0:T(8,128)(2,1)S(1)}, bf16[5,64,1024]{2,1,0:T(8,128)(2,1)S(1)}, u32[]{:S(2)}, u32[]{:S(2)}) collective-permute-start(bf16[5,64,1024]{2,1,0:T(8,128)(2,1)S(1)} %constant_dynamic-slice_fusion.29.refs_1_), channel_id=1, source_target_pairs={{0,4},{1,5},{2,6},{3,7},{4,0},{5,1},{6,2},{7,3},{8,12},{9,13},{10,... | collective-permute-start | bytes 1966088 | tf_op jit(solution)/shard_map/ppermute | solution.py:338
  52.3 85.7 %collective-permute-start.15 = (bf16[5,64,1024]{2,1,0:T(8,128)(2,1)S(1)}, bf16[5,64,1024]{2,1,0:T(8,128)(2,1)}, u32[]{:S(2)}, u32[]{:S(2)}) collective-permute-start(bf16[5,64,1024]{2,1,0:T(8,128)(2,1)S(1)} %constant_dynamic-slice_fusion.29.refs_1_), channel_id=1, source_target_pairs={{0,6},{1,7},{2,4},{3,5},{4,2},{5,3},{6,0},{7,1},{8,14},{9,15},{10,... | collective-permute-start | bytes 1966088 | tf_op jit(solution)/shard_map/ppermute | solution.py:338
  57.8 80.5 %collective-permute-start.16 = (bf16[5,64,1024]{2,1,0:T(8,128)(2,1)S(1)}, bf16[5,64,1024]{2,1,0:T(8,128)(2,1)}, u32[]{:S(2)}, u32[]{:S(2)}) collective-permute-start(bf16[5,64,1024]{2,1,0:T(8,128)(2,1)S(1)} %constant_dynamic-slice_fusion.29.refs_1_), channel_id=1, source_target_pairs={{0,1},{1,0},{2,3},{3,2},{4,5},{5,4},{6,7},{7,6},{8,9},{9,8},{10,11... | collective-permute-start | bytes 1966088 | tf_op jit(solution)/shard_map/ppermute | solution.py:334
  58.0 81.4 %collective-permute-start.20 = (bf16[5,64,1024]{2,1,0:T(8,128)(2,1)S(1)}, bf16[5,64,1024]{2,1,0:T(8,128)(2,1)S(1)}, u32[]{:S(2)}, u32[]{:S(2)}) collective-permute-start(bf16[5,64,1024]{2,1,0:T(8,128)(2,1)S(1)} %constant_dynamic-slice_fusion.29.refs_1_), channel_id=1, source_target_pairs={{0,8},{8,0},{16,24},{24,16},{1,9},{9,1},{17,25},{25,17},{2,10},{10... | collective-permute-start | bytes 1966088 | tf_op jit(solution)/shard_map/ppermute | solution.py:322
  140.9 56.7 %collective-permute-start.23 = (bf16[5,64,1024]{2,1,0:T(8,128)(2,1)}, bf16[5,64,1024]{2,1,0:T(8,128)(2,1)}, u32[]{:S(2)}, u32[]{:S(2)}) collective-permute-start(bf16[5,64,1024]{2,1,0:T(8,128)(2,1)} %collective-permute-done.15.refs_4_), channel_id=1, source_target_pairs={{0,8},{8,0},{16,24},{24,16},{1,9},{9,1},{17,25},{25,17},{2,10},{10... | collective-permute-start | bytes 1966088 | tf_op jit(solution)/shard_map/ppermute | solution.py:322
  172.3 81.4 %collective-permute-start.25 = (bf16[5,64,1024]{2,1,0:T(8,128)(2,1)}, bf16[5,64,1024]{2,1,0:T(8,128)(2,1)}, u32[]{:S(2)}, u32[]{:S(2)}) collective-permute-start(bf16[5,64,1024]{2,1,0:T(8,128)(2,1)} %collective-permute-done.17.refs_6_), channel_id=1, source_target_pairs={{0,8},{8,0},{16,24},{24,16},{1,9},{9,1},{17,25},{25,17},{2,10},{10... | collective-permute-start | bytes 1966088 | tf_op jit(solution)/shard_map/ppermute | solution.py:322
  176.2 77.4 %collective-permute-start.26 = (bf16[5,64,1024]{2,1,0:T(8,128)(2,1)}, bf16[5,64,1024]{2,1,0:T(8,128)(2,1)}, u32[]{:S(2)}, u32[]{:S(2)}) collective-permute-start(bf16[5,64,1024]{2,1,0:T(8,128)(2,1)} %collective-permute-done.18.refs_7_), channel_id=1, source_target_pairs={{0,8},{8,0},{16,24},{24,16},{1,9},{9,1},{17,25},{25,17},{2,10},{10... | collective-permute-start | bytes 1966088 | tf_op jit(solution)/shard_map/ppermute | solution.py:322
  177.9 75.8 %collective-permute-start.27 = (bf16[5,64,1024]{2,1,0:T(8,128)(2,1)}, bf16[5,64,1024]{2,1,0:T(8,128)(2,1)}, u32[]{:S(2)}, u32[]{:S(2)}) collective-permute-start(bf16[5,64,1024]{2,1,0:T(8,128)(2,1)} %collective-permute-done.19.refs_8_), channel_id=1, source_target_pairs={{0,8},{8,0},{16,24},{24,16},{1,9},{9,1},{17,25},{25,17},{2,10},{10... | collective-permute-start | bytes 1966088 | tf_op jit(solution)/shard_map/ppermute | solution.py:322
  197.6 382.2 %collective-permute-start = (bf16[512,1024]{1,0:T(8,128)(2,1)}, bf16[512,1024]{1,0:T(8,128)(2,1)}, u32[]{:S(2)}, u32[]{:S(2)}) collective-permute-start(bf16[512,1024]{1,0:T(8,128)(2,1)} %bitcast.383), channel_id=1, source_target_pairs={{0,8},{8,0},{16,24},{24,16},{1,9},{9,1},{17,25},{25,17},{2,10},{10... | collective-permute-start | bytes 3145736 | tf_op jit(solution)/shard_map/ppermute | solution.py:322
  202.5 377.2 %collective-permute-start.2 = (bf16[512,1024]{1,0:T(8,128)(2,1)}, bf16[512,1024]{1,0:T(8,128)(2,1)}, u32[]{:S(2)}, u32[]{:S(2)}) collective-permute-start(bf16[512,1024]{1,0:T(8,128)(2,1)} %collective-permute-done.1), channel_id=1, source_target_pairs={{0,8},{8,0},{16,24},{24,16},{1,9},{9,1},{17,25},{25,17},{2,10},{10... | collective-permute-start | bytes 3145736 | tf_op jit(solution)/shard_map/ppermute | solution.py:322
  576.9 61.5 %collective-permute-start.29 = (bf16[512,1024]{1,0:T(8,128)(2,1)S(1)}, bf16[512,1024]{1,0:T(8,128)(2,1)S(1)}, u32[]{:S(2)}, u32[]{:S(2)}) collective-permute-start(bf16[512,1024]{1,0:T(8,128)(2,1)S(1)} %fusion.20.refs_1_.refs_4_), channel_id=1, source_target_pairs={{0,16},{8,24},{16,0},{24,8},{1,17},{9,25},{17,1},{25,9},{2,18},{10... | collective-permute-start | bytes 3145736 | tf_op jit(solution)/shard_map/ppermute | solution.py:326
  579.2 59.3 %collective-permute-start.32 = (bf16[512,1024]{1,0:T(8,128)(2,1)S(1)}, bf16[512,1024]{1,0:T(8,128)(2,1)S(1)}, u32[]{:S(2)}, u32[]{:S(2)}) collective-permute-start(bf16[512,1024]{1,0:T(8,128)(2,1)S(1)} %fusion.21.refs_5_.refs_8_), channel_id=1, source_target_pairs={{0,16},{8,24},{16,0},{24,8},{1,17},{9,25},{17,1},{25,9},{2,18},{10... | collective-permute-start | bytes 3145736 | tf_op jit(solution)/shard_map/ppermute | solution.py:326
  816.9 62.5 %collective-permute-start.40 = (bf16[512,1024]{1,0:T(8,128)(2,1)S(1)}, bf16[512,1024]{1,0:T(8,128)(2,1)S(1)}, u32[]{:S(2)}, u32[]{:S(2)}) collective-permute-start(bf16[512,1024]{1,0:T(8,128)(2,1)S(1)} %get-tuple-element.59), channel_id=1, source_target_pairs={{0,8},{8,0},{16,24},{24,16},{1,9},{9,1},{17,25},{25,17},{2,10},{10... | collective-permute-start | bytes 3145736 | tf_op jit(solution)/shard_map/ppermute | solution.py:322
  829.0 93.6 %collective-permute-start.42 = (bf16[512,1024]{1,0:T(8,128)(2,1)S(1)}, bf16[512,1024]{1,0:T(8,128)(2,1)S(1)}, u32[]{:S(2)}, u32[]{:S(2)}) collective-permute-start(bf16[512,1024]{1,0:T(8,128)(2,1)S(1)} %add_convert_fusion.5), channel_id=1, source_target_pairs={{0,16},{8,24},{16,0},{24,8},{1,17},{9,25},{17,1},{25,9},{2,18},{10... | collective-permute-start | bytes 3145736 | tf_op jit(solution)/shard_map/ppermute | solution.py:326
  830.6 190.0 %collective-permute-start.36 = (bf16[512,256]{1,0:T(8,128)(2,1)}, bf16[512,256]{1,0:T(8,128)(2,1)}, u32[]{:S(2)}, u32[]{:S(2)}) collective-permute-start(bf16[512,256]{1,0:T(8,128)(2,1)} %get-tuple-element.173), channel_id=1, source_target_pairs={{0,24},{8,16},{16,8},{24,0},{1,25},{9,17},{17,9},{25,1},{2,26},{10... | collective-permute-start | bytes 786440 | tf_op jit(solution)/shard_map/ppermute | solution.py:330
  837.7 182.9 %collective-permute-start.35 = (bf16[512,256]{1,0:T(8,128)(2,1)}, bf16[512,256]{1,0:T(8,128)(2,1)}, u32[]{:S(2)}, u32[]{:S(2)}) collective-permute-start(bf16[512,256]{1,0:T(8,128)(2,1)} %get-tuple-element.174), channel_id=1, source_target_pairs={{0,16},{8,24},{16,0},{24,8},{1,17},{9,25},{17,1},{25,9},{2,18},{10... | collective-permute-start | bytes 786440 | tf_op jit(solution)/shard_map/ppermute | solution.py:326
  1019.4 64.0 %collective-permute-start.53 = (bf16[5,8,64,1024]{3,2,1,0:T(8,128)(2,1)}, bf16[5,8,64,1024]{3,2,1,0:T(8,128)(2,1)}, u32[]{:S(2)}, u32[]{:S(2)}) collective-permute-start(bf16[5,8,64,1024]{3,2,1,0:T(8,128)(2,1)} %get-tuple-element.151), channel_id=1, source_target_pairs={{0,8},{8,0},{16,24},{24,16},{1,9},{9,1},{17,25},{25,17},{2,10},{10... | collective-permute-start | bytes 15728648 | tf_op jit(solution)/shard_map/ppermute | solution.py:322
  1094.2 70.0 %collective-permute-start.54 = (bf16[5,4,64,1024]{3,2,1,0:T(8,128)(2,1)}, bf16[5,4,64,1024]{3,2,1,0:T(8,128)(2,1)}, u32[]{:S(2)}, u32[]{:S(2)}) collective-permute-start(bf16[5,4,64,1024]{3,2,1,0:T(8,128)(2,1)} %dynamic-slice_bitcast_fusion), channel_id=1, source_target_pairs={{0,1},{1,0},{2,3},{3,2},{4,5},{5,4},{6,7},{7,6},{8,9},{9,8},{10,11... | collective-permute-start | bytes 7864328 | tf_op jit(solution)/shard_map/ppermute | solution.py:334
  1116.0 109.6 %collective-permute-start.37 = (bf16[512,1024]{1,0:T(8,128)(2,1)}, bf16[512,1024]{1,0:T(8,128)(2,1)}, u32[]{:S(2)}, u32[]{:S(2)}) collective-permute-start(bf16[512,1024]{1,0:T(8,128)(2,1)} %get-tuple-element.133), channel_id=1, source_target_pairs={{0,8},{8,0},{16,24},{24,16},{1,9},{9,1},{17,25},{25,17},{2,10},{10... | collective-permute-start | bytes 3145736 | tf_op jit(solution)/shard_map/ppermute | solution.py:322
  1127.8 97.9 %collective-permute-start.39 = (bf16[512,1024]{1,0:T(8,128)(2,1)}, bf16[512,1024]{1,0:T(8,128)(2,1)}, u32[]{:S(2)}, u32[]{:S(2)}) collective-permute-start(bf16[512,1024]{1,0:T(8,128)(2,1)} %add_convert_fusion.6), channel_id=1, source_target_pairs={{0,16},{8,24},{16,0},{24,8},{1,17},{9,25},{17,1},{25,9},{2,18},{10... | collective-permute-start | bytes 3145736 | tf_op jit(solution)/shard_map/ppermute | solution.py:326
  (162 other events, 6528.1 us)
Sparse Core Ops, SparseCore 0:
  11.5 118.7 all-gather.4
  133.7 85.8 all-gather.6
  748.1 243.6 reduce-scatter.1

commit v2 on v1

--- a/solution.py
+++ b/solution.py
@@ -5,6 +5,7 @@
 import jax.numpy as jnp
 from jax import lax
 from jax.experimental import pallas as pl
+from jax.experimental.layout import Layout, with_layout_constraint
 from jax.experimental.pallas import tpu as pltpu
 from jax.sharding import PartitionSpec as P
 
@@ -259,7 +260,7 @@
     )(*(scalars or ()), q, *k_list, *v_list)
 
 
-def attention_backward(q, q_col, do, o, lse, k_list, k_col, v_list, v_col, width, scalars, key_rows, units=2, per_group=2):
+def attention_backward(q, q_col, do, o, lse, k_list, k_col, v_list, v_col, width, scalars, key_rows, units=2, per_group=2, o_col=0):
     pieces = len(k_list)
     lanes = units * 128
     rows = q.shape[0]
@@ -268,8 +269,9 @@
     groups, blocks = width // lanes, rows // BLK
     masked = scalars is not None
     spec_q = pl.BlockSpec((BLK, lanes), lambda h, i, *_: (i, q_col + h))
-    spec_o = pl.BlockSpec((BLK, lanes), lambda h, i, *_: (i, h))
-    spec_lse = pl.BlockSpec((units, 8, 2 * BLK), lambda h, i, *_: (h, 0, i))
+    spec_o = pl.BlockSpec((BLK, lanes), lambda h, i, *_: (i, o_col + h))
+    spec_dq = pl.BlockSpec((BLK, lanes), lambda h, i, *_: (i, h))
+    spec_lse = pl.BlockSpec((units, 8, 2 * BLK), lambda h, i, *_: (o_col + h, 0, i))
     specs_k = [pl.BlockSpec((k.shape[0], lanes), lambda h, i, *_: (0, k_col + h)) for k in k_list]
     specs_v = [pl.BlockSpec((v.shape[0], lanes), lambda h, i, *_: (0, v_col + h)) for v in v_list]
     outs_k = [pl.BlockSpec((k.shape[0], lanes), lambda h, i, *_: (0, h)) for k in k_list]
@@ -282,7 +284,7 @@
             num_scalar_prefetch=3 if masked else 0,
             grid=(groups, blocks),
             in_specs=[spec_q, spec_o, spec_o, spec_lse] + specs_k + specs_v,
-            out_specs=[spec_o] + outs_k + outs_k,
+            out_specs=[spec_dq] + outs_k + outs_k,
             scratch_shapes=[
                 pltpu.VMEM((units, 2 * BLK, 128), jnp.bfloat16),
                 pltpu.VMEM((units, 2 * BLK, 128), jnp.bfloat16),
@@ -298,6 +300,131 @@
     )(*(scalars or ()), q, do, o, lse, *k_list, *v_list)
 
 
+def norm_sums(summed):
+    mean = jnp.mean(summed, axis=-1, keepdims=True)
+    centred = summed - mean
+    inverse = lax.rsqrt(jnp.mean(centred * centred, axis=-1, keepdims=True) + epsilon)
+    return centred * inverse, inverse
+
+
+def feed_body(
+    core_ref, hidden_ref, upstream_ref, weights_ref, expand_bias_ref, vectors_ref,
+    out_ref, grad_hidden_ref, send_ref, keep_ref, grad_bias_ref, sums_ref,
+    low, expanded, activated, total, grad_low,
+):
+    step = pl.program_id(0)
+    blocks = pl.num_programs(0) // 2
+    block = step % blocks
+    width = hidden_ref.shape[1]
+    first = weights_ref[:, 0, :128].reshape(width, width)
+    second = weights_ref[:, 0, 128:].reshape(width, width)
+
+    @pl.when(step == 0)
+    def begin():
+        low[...] = hidden_ref[...].astype(jnp.bfloat16)
+        total[...] = residual_scale * hidden_ref[...] + vectors_ref[0:1]
+
+    @pl.when(step < blocks)
+    def forward():
+        wide = mxu(low[...], first, NN) + expand_bias_ref[0]
+        expanded[block] = wide
+        active = gelu_tanh(wide).astype(jnp.bfloat16)
+        activated[block] = active
+        total[...] += mxu(active, second, NN)
+
+    @pl.when(step == blocks)
+    def turn():
+        normed, inverse = norm_sums(total[...])
+        gain = vectors_ref[1:2]
+        out_ref[...] = (normed * gain + vectors_ref[2:3]).astype(out_ref.dtype)
+        upstream = upstream_ref[...].astype(jnp.float32)
+        scaled = upstream * gain
+        grad = inverse * (
+            scaled
+            - jnp.mean(scaled, axis=-1, keepdims=True)
+            - normed * jnp.mean(scaled * normed, axis=-1, keepdims=True)
+        )
+        grad_low[...] = grad.astype(jnp.bfloat16)
+        grad_hidden_ref[...] = residual_scale * grad
+        sums_ref[0:1] = jnp.sum(grad_low[...].astype(jnp.float32), axis=0, keepdims=True)
+        sums_ref[1:2] = jnp.sum(upstream * normed, axis=0, keepdims=True)
+        sums_ref[2:3] = jnp.sum(upstream, axis=0, keepdims=True)
+
+    @pl.when(step >= blocks)
+    def backward():
+        grad_active = mxu(grad_low[...], second, NT)
+        grad_wide = (grad_active * gelu_slope(expanded[block])).astype(jnp.bfloat16)
+        grad_second = mxu(activated[block], grad_low[...], TN).astype(jnp.bfloat16).reshape(-1, 128, width)
+        grad_first = mxu(low[...], grad_wide, TN).astype(jnp.bfloat16).reshape(-1, 128, width)
+
+        @pl.when(block < blocks // 2)
+        def to_send():
+            send_ref[:, 0, 128:] = grad_second
+            send_ref[:, 0, :128] = grad_first
+
+        @pl.when(block >= blocks // 2)
+        def to_keep():
+            keep_ref[:, 0, 128:] = grad_second
+            keep_ref[:, 0, :128] = grad_first
+
+        grad_bias_ref[0] = jnp.sum(grad_wide.astype(jnp.float32), axis=0, keepdims=True)
+        grad_hidden_ref[...] += mxu(grad_wide, first, NT)
+
+
+def feed_forward(core, hidden, upstream, weights, expand_bias, vectors):
+    rows, width = hidden.shape
+    groups, blocks = weights.shape[:2]
+    half = blocks // 2
+
+    def at(i, core_ref):
+        return (i + half * (1 - core_ref[0])) % blocks
+
+    def back(i, core_ref):
+        return (jnp.maximum(i - blocks, 0) + half * (1 - core_ref[0])) % blocks
+
+    whole = pl.BlockSpec((rows, width), lambda i, c: (0, 0))
+    once = pl.BlockSpec((rows, width), lambda i, c: (0, 0), pipeline_mode=pl.Buffered(1))
+    f32, bf16 = jnp.float32, jnp.bfloat16
+    part = (groups, 1, 256, width)
+    return pl.pallas_call(
+        feed_body,
+        grid_spec=pltpu.PrefetchScalarGridSpec(
+            num_scalar_prefetch=1,
+            grid=(2 * blocks,),
+            in_specs=[
+                once, once,
+                pl.BlockSpec(part, lambda i, c: (0, at(i, c), 0, 0)),
+                pl.BlockSpec((1, 1, width), lambda i, c: (at(i, c), 0, 0)),
+                pl.BlockSpec((8, width), lambda i, c: (0, 0)),
+            ],
+            out_specs=[
+                whole, whole,
+                pl.BlockSpec(part, lambda i, c: (0, jnp.clip(i - blocks, 0, half - 1), 0, 0)),
+                pl.BlockSpec(part, lambda i, c: (0, jnp.clip(i - blocks - half, 0, half - 1), 0, 0)),
+                pl.BlockSpec((1, 1, width), lambda i, c: (back(i, c), 0, 0)),
+                pl.BlockSpec((8, width), lambda i, c: (0, 0)),
+            ],
+            scratch_shapes=[
+                pltpu.VMEM((rows, width), bf16),
+                pltpu.VMEM((blocks, rows, width), f32),
+                pltpu.VMEM((blocks, rows, width), bf16),
+                pltpu.VMEM((rows, width), f32),
+                pltpu.VMEM((rows, width), bf16),
+            ],
+        ),
+        out_shape=[
+            jax.ShapeDtypeStruct((rows, width), bf16),
+            jax.ShapeDtypeStruct((rows, width), f32),
+            jax.ShapeDtypeStruct((groups, half, 256, width), bf16),
+            jax.ShapeDtypeStruct((groups, half, 256, width), bf16),
+            jax.ShapeDtypeStruct((blocks, 1, width), f32),
+            jax.ShapeDtypeStruct((8, width), f32),
+        ],
+        compiler_params=pltpu.CompilerParams(vmem_limit_bytes=60 << 20),
+        cost_estimate=pl.CostEstimate(flops=12 * rows * width * width * blocks, transcendentals=2 * rows * width * blocks, bytes_accessed=52 << 20),
+    )(core.reshape(1).astype(jnp.int32), hidden, upstream, weights, expand_bias, vectors)
+
+
 def core_perm():
     return [(c, c ^ 1) for c in range(4)]
 
@@ -347,71 +474,137 @@
     return [me ^ (2 * k + d) for d in (0, 1) for k in range(4)]
 
 
-def place_body(count, stacks, rows, *refs):
+def place_body(plan, *refs):
     offsets, refs = refs[0], refs[1:]
-    pieces, outs, sems = refs[:count], refs[count:count + stacks], refs[-1]
+    outs, sems = refs[-1 - len(plan):-1], refs[-1]
+    pieces = refs[:-1 - len(plan)]
     copies = []
-    for i in range(count):
-        start = pl.multiple_of(offsets[i], rows)
-        for s in range(stacks):
-            source = pieces[i].at[s] if len(pieces[i].shape) == 3 else pieces[i]
-            copy = pltpu.make_async_copy(source, outs[s].at[pl.ds(start, rows)], sems.at[i, s])
+    for i, piece in enumerate(pieces):
+        for s, (lead, first, rows) in enumerate(plan):
+            source = piece if lead is None else piece.at[lead]
+            start = pl.multiple_of(offsets[i] * rows, rows)
+            copy = pltpu.make_async_copy(source.at[pl.ds(first, rows)], outs[s].at[pl.ds(start, rows)], sems.at[i, s])
             copy.start()
             copies.append(copy)
     for copy in copies:
         copy.wait()
 
 
-def place(pieces, offsets):
-    shape = pieces[0].shape
-    stacks = shape[0] if len(shape) == 3 else 1
-    rows, columns = shape[-2:]
+def place(pieces, slots, plan):
+    columns = pieces[0].shape[-1]
     count = len(pieces)
-    out = [jax.ShapeDtypeStruct((count * rows, columns), pieces[0].dtype)] * stacks
+    out = [jax.ShapeDtypeStruct((count * rows, columns), pieces[0].dtype) for _, _, rows in plan]
     anywhere = pl.BlockSpec(memory_space=pl.ANY)
+    moved = 4 * count * columns * sum(rows for _, _, rows in plan)
     return pl.pallas_call(
-        functools.partial(place_body, count, stacks, rows),
+        functools.partial(place_body, plan),
         in_specs=[pl.BlockSpec(memory_space=pltpu.SMEM)] + [anywhere] * count,
-        out_specs=[anywhere] * stacks,
+        out_specs=[pl.BlockSpec(memory_space=pltpu.VMEM)] * len(plan),
         out_shape=out,
-        scratch_shapes=[pltpu.SemaphoreType.DMA((count, stacks))],
-        cost_estimate=pl.CostEstimate(flops=0, transcendentals=0, bytes_accessed=4 * count * stacks * rows * columns),
-    )(jnp.stack(offsets).astype(jnp.int32), *pieces)
+        scratch_shapes=[pltpu.SemaphoreType.DMA((count, len(plan)))],
+        compiler_params=pltpu.CompilerParams(vmem_limit_bytes=(moved // 2) + (4 << 20)),
+        cost_estimate=pl.CostEstimate(flops=0, transcendentals=0, bytes_accessed=moved),
+    )(jnp.stack(slots).astype(jnp.int32), *pieces)
+
+
+def after(value, other):
+    return lax.optimization_barrier((value, other))[0]
 
 
 def xor_take(stack, me):
     return jnp.concatenate([lax.dynamic_index_in_dim(stack, n ^ me, 0) for n in range(stack.shape[0])])
 
 
-def sum_over_fsdp(grads, z, x, core):
-    f32, bf16 = jnp.float32, jnp.bfloat16
-    width = grads[0].shape[1]
-    halves = [g.reshape(8, 2, 64, width) for g in grads]
-    send = jnp.stack([lax.dynamic_index_in_dim(h, core ^ 1, 1, keepdims=False) for h in halves])
-    keep = jnp.stack([lax.dynamic_index_in_dim(h, core, 1, keepdims=False) for h in halves])
-    part = (keep.astype(f32) + to_core(send).astype(f32)).astype(bf16)
-    part = part.reshape(len(grads), 4, 2, 64, width)
-    send = lax.dynamic_index_in_dim(part, x ^ 1, 2, keepdims=False)
-    keep = lax.dynamic_index_in_dim(part, x, 2, keepdims=False)
-    part = (keep.astype(f32) + to_x(send).astype(f32)).astype(bf16)
-    got = [to_z(lax.dynamic_index_in_dim(part, z ^ k, 1, keepdims=False), k) for k in (1, 2, 3)]
-    total = lax.dynamic_index_in_dim(part, z, 1, keepdims=False).astype(f32)
-    for piece in got:
-        total = total + piece.astype(f32)
-    low = total.astype(bf16)
-    low = (low.astype(f32) + to_y(low).astype(f32)).astype(bf16)
-    other = to_core(low)
-    first = jnp.where(core == 0, low, other)
-    second = jnp.where(core == 0, other, low)
-    return jnp.concatenate([first, second], axis=1).astype(f32)
-
-
-def sum_everywhere(value):
-    value = value + to_core(value)
-    value = value + to_y(value)
-    value = value + to_x(value)
-    got = [to_z(value, k) for k in (1, 2, 3)]
-    return value + got[0] + got[1] + got[2]
+def from_fsdp(blocks):
+    got = lax.all_to_all(blocks, "fsdp", 0, 0)
+    return jnp.sum(got.astype(jnp.float32), axis=0)
+
+
+def part_of(parts, index, axis):
+    return lax.dynamic_index_in_dim(parts, index, axis, keepdims=False)
+
+
+def added(keep, got):
+    return (keep.astype(jnp.float32) + got.astype(jnp.float32)).astype(jnp.bfloat16)
+
+
+def halves_dot(pairs, core):
+    def side(index):
+        terms = []
+        for left, right in pairs:
+            half = right.shape[1] // 2
+            chosen = lax.dynamic_slice_in_dim(right, index * half, half, axis=1)
+            terms.append(jnp.dot(left.T, chosen, preferred_element_type=jnp.float32).astype(jnp.bfloat16))
+        return with_layout_constraint(jnp.concatenate(terms, axis=1), Layout(major_to_minor=(0, 1)))
+
+    return side(core), side(core ^ 1)
+
+
+def over_z(parts, z):
+    got = [to_z(part_of(parts, z ^ k, 1), k) for k in (1, 2, 3)]
+    total = part_of(parts, z, 1).astype(jnp.float32)
+    return (total + got[0].astype(jnp.float32) + got[1].astype(jnp.float32) + got[2].astype(jnp.float32)).astype(jnp.bfloat16)
+
+
+def ctx_pieces(own):
+    line = to_y(own)
+    return [own, to_core(own), line, to_core(line)]
+
+
+def spread_feed_body(core_ref, *refs):
+    (own, other), (expand_ref, reduce_ref) = refs[:2], refs[2:]
+    for index, source in ((core_ref[0], own), (1 - core_ref[0], other)):
+        for p in range(2):
+            at = pl.multiple_of(index * 256 + p * 128, 128)
+            reduce_ref[pl.ds(at, 128), :] = source[p, 128:].astype(jnp.float32)
+            for f in range(8):
+                expand_ref[:, pl.ds(at + f * 512, 128)] = source[p, :128, f * 128:(f + 1) * 128].astype(jnp.float32)
+
+
+def spread_projection_body(me_ref, *refs):
+    pieces, (out_ref, vectors_ref) = refs[:4], refs[4:]
+    total = jnp.zeros((8, 384), jnp.float32)
+    for k in range(4):
+        at = pl.multiple_of((me_ref[0] ^ k) * 256, 128)
+        for part in range(3):
+            for pair in range(2):
+                source = pieces[k][:128, pair * 384 + part * 128:pair * 384 + (part + 1) * 128]
+                out_ref[:, pl.ds(at + part * 1024 + pair * 128, 128)] = source.astype(jnp.float32)
+        total = total + pieces[k][128:136, 384:].astype(jnp.float32)
+    for i in range(18):
+        vectors_ref[i:i + 1] = total[i // 3:i // 3 + 1, (i % 3) * 128:(i % 3 + 1) * 128]
+
+
+def spread_middle_body(core_ref, *refs):
+    (early, early_other, late, late_other), (memory_ref, query_ref, cross_ref, self_ref) = refs[:4], refs[4:]
+    for index, first, second in ((core_ref[0], early, late), (1 - core_ref[0], early_other, late_other)):
+        for half, source in ((0, first), (512, second)):
+            at = pl.multiple_of(half + index * 256, 256)
+            memory_ref[:, pl.ds(at, 256)] = source[:, 0:256].astype(jnp.float32)
+            memory_ref[:, pl.ds(at + 1024, 256)] = source[:, 256:512].astype(jnp.float32)
+            query_ref[:, pl.ds(at, 256)] = source[:, 512:768].astype(jnp.float32)
+        at = pl.multiple_of(index * 512, 512)
+        cross_ref[:, pl.ds(at, 512)] = first[:, 768:].astype(jnp.float32)
+        self_ref[:, pl.ds(at, 512)] = second[:, 768:].astype(jnp.float32)
+
+
+def spread(body, index, pieces, shapes):
+    whole = pl.BlockSpec(memory_space=pltpu.VMEM)
+    moved = sum(p.size * 2 for p in pieces) + sum(a * b * 4 for a, b in shapes)
+    return pl.pallas_call(
+        body,
+        in_specs=[pl.BlockSpec(memory_space=pltpu.SMEM)] + [whole] * len(pieces),
+        out_specs=[whole] * len(shapes),
+        out_shape=[jax.ShapeDtypeStruct(shape, jnp.float32) for shape in shapes],
+        compiler_params=pltpu.CompilerParams(vmem_limit_bytes=moved + (4 << 20)),
+        cost_estimate=pl.CostEstimate(flops=0, transcendentals=0, bytes_accessed=moved),
+    )(index.reshape(1).astype(jnp.int32), *pieces)
+
+
+def chip_sums(terms, rows):
+    pairs = terms.reshape(2, 2, rows, terms.shape[1])
+    got = to_core(pairs[:, 1])
+    return pairs[0, 0].astype(jnp.float32) + got[0].astype(jnp.float32), added(pairs[1, 0], got[1])
 
 
 def tiled_shards(
@@ -447,37 +640,43 @@
     own_rows = tokens[0]
     rows, width = own_rows.shape
     me_c, me_f = lax.axis_index("ctx"), lax.axis_index("fsdp")
-    core, z, x = me_c % 2, me_f // 2, me_f % 2
+    core, line, z, x = me_c % 2, me_c // 2, me_f // 2, me_f % 2
     share = width // 4
 
     def dot(left, right):
         return jnp.dot(left, right, preferred_element_type=f32)
 
+    vectors = [self_query_bias, self_value_bias, self_output_bias, first_gain, first_shift, cross_query_bias,
+               cross_value_bias, cross_output_bias, second_gain, second_shift, reduce_bias, third_gain, third_shift]
+    vectors += [expand_bias[i * 128:(i + 1) * 128] for i in range(4)] + [jnp.zeros((128,), bf16)]
+    vector_rows = jnp.stack([jnp.concatenate(vectors[i * 6:i * 6 + 6]) for i in range(3)])
+    columns = [lax.dynamic_slice(self_projection, (0, part * width + me_c * share), (128, share)) for part in range(3)]
+    own_piece = jnp.concatenate([jnp.concatenate(columns, axis=1), vector_rows, jnp.zeros((13, 3 * share), bf16)])
+    projection_pieces = fsdp_pieces(own_piece)
     rows_y = to_y(own_rows)
-    columns = [lax.dynamic_slice(self_projection, (0, part * width + me_c * share), (128, share)) for part in range(3)]
-    projection_pieces = fsdp_pieces(jnp.concatenate(columns, axis=1))
     rows_core = to_core(own_rows)
-    rows_diagonal = to_core(rows_y)
+    rows_diagonal = to_core(after(rows_y, projection_pieces[1:4]))
     sequence = jnp.concatenate([own_rows, rows_core, rows_y, rows_diagonal])
     sources = fsdp_sources(me_f)
-    (projection,) = place(projection_pieces, [s * 128 for s in sources])
-
-    vectors = (self_query_bias, self_value_bias, self_output_bias, first_gain, first_shift, cross_query_bias,
-               cross_value_bias, cross_output_bias, second_gain, second_shift, reduce_bias, third_gain, third_shift)
-    packed = jnp.concatenate([jnp.stack(vectors), expand_bias.reshape(4, 128)])
-    gathered = lax.all_gather(packed, "fsdp", axis=0).astype(f32)
+    projection, vector_blocks = place(projection_pieces, sources, ((None, 0, 128), (None, 128, 16)))
+    vector_blocks = vector_blocks.reshape(8, 16, 3 * share).astype(f32)
+    gathered = [vector_blocks[:, i // 6, (i % 6) * 128:(i % 6 + 1) * 128].reshape(width) for i in range(17)]
     (query_bias, value_bias, out_bias, gain_one, shift_one, cross_qbias, cross_vbias, cross_obias,
-     gain_two, shift_two, reduce_bias_full, gain_three, shift_three) = [gathered[:, i].reshape(width) for i in range(13)]
-    expand_bias_full = gathered[:, 13:].reshape(4 * width)
-
-    expand_full = lax.all_gather(lax.dynamic_slice_in_dim(expand_weight, me_c * 32, 32), ("fsdp", "ctx"), axis=0, tiled=True)
-    reduce_full = lax.all_gather(lax.dynamic_slice_in_dim(reduce_weight, me_c * 128, 128), ("fsdp", "ctx"), axis=0, tiled=True)
-
-    middle = jnp.stack([cross_memory[:, :width], cross_memory[:, width:], self_output, cross_query, cross_output])
-    half_pieces = fsdp_pieces(lax.dynamic_slice_in_dim(middle, core * 64, 64, axis=1))
-    other_pieces = [to_core(piece) for piece in half_pieces]
-    offsets = [s * 128 + core * 64 for s in sources] + [s * 128 + (core ^ 1) * 64 for s in sources]
-    memory_key_full, memory_value_full, self_out_full, cross_query_full, cross_out_full = place(half_pieces + other_pieces, offsets)
+     gain_two, shift_two, reduce_bias_full, gain_three, shift_three) = gathered[:13]
+    expand_bias_blocks = jnp.stack(gathered[13:]).reshape(4, 1, width)
+
+    middle = [cross_memory[:, :width], cross_memory[:, width:], self_output, cross_query, cross_output]
+    middle_own = jnp.stack([lax.dynamic_slice_in_dim(weight, me_c * 32, 32) for weight in middle])
+    middle_all = lax.all_gather(middle_own, ("fsdp", "ctx"), axis=0)
+    memory_key_full, memory_value_full, self_out_full, cross_query_full, cross_out_full = [
+        middle_all[:, i].reshape(width, width) for i in range(5)
+    ]
+    expand_columns = lax.dynamic_index_in_dim(expand_weight.reshape(128, 8, 4, 128), me_c, 2, keepdims=False)
+    feed_own = jnp.concatenate([expand_columns.reshape(128, width), lax.dynamic_slice_in_dim(reduce_weight, me_c * 128, 128)])
+
+    memory_rows = memory[0]
+    memory_y = to_y(after(memory_rows, projection_pieces[4:]))
+    memory_core = to_core(memory_rows)
 
     projected = dot(sequence, projection)
     bias = jnp.concatenate([
@@ -488,144 +687,190 @@
     qkv = (projected + bias).astype(bf16)
     scalars = (block_order[0], block_map[0].reshape(-1), me_c.reshape(1).astype(jnp.int32))
     heads_out, self_lse = attention_forward(qkv, 0, [qkv], 1, [qkv], 2, share, scalars, BLK)
-
-    memory_rows = memory[0]
-    memory_keys = dot(memory_rows, memory_key_full).astype(bf16)
-    memory_values = (dot(memory_rows, memory_value_full) + cross_vbias).astype(bf16)
-    keys_y, values_y = to_y(memory_keys), to_y(memory_values)
-    key_list = [memory_keys, to_core(memory_keys), keys_y, to_core(keys_y)]
-    value_list = [memory_values, to_core(memory_values), values_y, to_core(values_y)]
+    heads_out, memory_y = lax.optimization_barrier((heads_out, memory_y))
+    memory_all = jnp.concatenate([memory_rows, memory_core, memory_y, to_core(memory_y)])
+
+    feed_weights = lax.all_gather(after(feed_own, (middle_all, heads_out)), ("fsdp", "ctx"), axis=0, tiled=True)
+    memory_keys = dot(memory_all, memory_key_full).astype(bf16)
+    memory_values = (dot(memory_all, memory_value_full) + cross_vbias).astype(bf16)
 
     pieces = [heads_out[i * rows:(i + 1) * rows] for i in range(4)]
-    attended = jnp.concatenate([pieces[0], to_core(pieces[1]), to_y(pieces[2]), to_diagonal(pieces[3])], axis=1)
-    self_out_rel = xor_take(self_out_full.reshape(4, share, width), me_c).reshape(width, width)
-    branch = dot(attended, self_out_rel) + out_bias
+    others = after([to_core(pieces[1]), to_y(pieces[2]), to_diagonal(pieces[3])], (memory_keys, memory_values))
+    arrived = jnp.stack([pieces[0]] + others)
+    attended = jnp.concatenate([part_of(arrived, n ^ me_c, 0) for n in range(4)], axis=1)
+    branch = dot(attended, self_out_full) + out_bias
     hidden_one, normed_one, inverse_one = layer_norm(residual_scale * own_rows.astype(f32) + branch, gain_one, shift_one)
 
     hidden_low = hidden_one.astype(bf16)
     cross_queries = (dot(hidden_low, cross_query_full) + cross_qbias).astype(bf16)
-    cross_low, cross_lse = attention_forward(cross_queries, 0, key_list, 0, value_list, 0, width, None, rows)
+    cross_low, cross_lse = attention_forward(cross_queries, 0, [memory_keys], 0, [memory_values], 0, width, None, rows)
     cross_branch = dot(cross_low, cross_out_full) + cross_obias
     hidden_two, normed_two, inverse_two = layer_norm(residual_scale * hidden_one + cross_branch, gain_two, shift_two)
 
-    hidden_two_low = hidden_two.astype(bf16)
-    expanded = dot(hidden_two_low, expand_full) + expand_bias_full
-    activated = gelu_tanh(expanded).astype(bf16)
-    reduced = dot(activated, reduce_full) + reduce_bias_full
-    result, normed_three, inverse_three = layer_norm(residual_scale * hidden_two + reduced, gain_three, shift_three)
-    output = result.astype(bf16)[None]
-
-    upstream = cotangent[0].astype(f32)
-    grad_third, grad_third_gain, grad_third_shift = layer_norm_back(upstream, gain_three, normed_three, inverse_three)
-    grad_reduced = grad_third.astype(bf16)
-    grad_reduce_bias = jnp.sum(grad_reduced.astype(f32), axis=0)
-    grad_reduce_weight = dot(activated.T, grad_reduced).astype(bf16)
-    grad_expanded = (dot(grad_reduced, reduce_full.T) * gelu_slope(expanded)).astype(bf16)
-    grad_expand_bias = jnp.sum(grad_expanded.astype(f32), axis=0)
-    expand_parts = [
-        dot(hidden_two_low.T, grad_expanded[:, i * width:(i + 1) * width]).astype(bf16).reshape(8, 128, width)
-        for i in range(4)
-    ]
-    feed = jnp.concatenate([jnp.stack(expand_parts, axis=1), grad_reduce_weight.reshape(8, 4, 128, width)], axis=2)
-    feed_share = lax.psum_scatter(feed.reshape(32 * 256, width), ("fsdp", "ctx"), scatter_dimension=0, tiled=True)
-    grad_hidden_two = residual_scale * grad_third + dot(grad_expanded, expand_full.T)
+    feed_vectors = jnp.concatenate([jnp.stack([reduce_bias_full, gain_three, shift_three]), jnp.zeros((5, width), f32)])
+    output, grad_hidden_two, feed_send, feed_keep, grad_expand_bias, feed_sums = feed_forward(
+        core, hidden_two, cotangent[0], feed_weights.reshape(8, 4, 256, width), expand_bias_blocks, feed_vectors
+    )
+    feed_got = to_core(feed_send)
 
     grad_second, grad_second_gain, grad_second_shift = layer_norm_back(grad_hidden_two, gain_two, normed_two, inverse_two)
     grad_cross_branch = grad_second.astype(bf16)
     grad_cross_output_bias = jnp.sum(grad_cross_branch.astype(f32), axis=0)
-    grad_cross_output = dot(cross_low.T, grad_cross_branch).astype(bf16)
     grad_cross_low = dot(grad_cross_branch, cross_out_full.T).astype(bf16)
-    cross_back = attention_backward(
-        cross_queries, 0, grad_cross_low, cross_low, cross_lse, key_list, 0, value_list, 0, width, None, rows
-    )
-    grad_cross_queries = cross_back[0]
-
-    def to_owner(terms):
-        near = terms[0].astype(f32) + to_core(terms[1]).astype(f32)
-        far = (terms[2].astype(f32) + to_core(terms[3]).astype(f32)).astype(bf16)
-        return (near + to_y(far).astype(f32)).astype(bf16)
-
-    grad_memory_keys, grad_memory_values = to_owner(cross_back[1:5]), to_owner(cross_back[5:9])
-
+
+    def cross_half(half, queries):
+        return attention_backward(
+            queries, 2 * half, grad_cross_low, cross_low, cross_lse, [memory_keys], 2 * half, [memory_values], 2 * half,
+            width // 2, None, rows, o_col=2 * half
+        )
+
+    def line_split(summed):
+        return summed.reshape(8, 2, 64, summed.shape[1])
+
+    early_q, early_k, early_v = cross_half(0, cross_queries)
+    feed_keep, feed_got = after((feed_keep, feed_got), early_q)
+    feed_half = added(feed_keep, feed_got).reshape(8 * 512, width)
+    feed_share = lax.psum_scatter(feed_half, "fsdp", scatter_dimension=0, tiled=True)
+    first_q, first_k, first_v = after((early_q, early_k, early_v), feed_half)
+    keep, send = halves_dot(
+        [(memory_all, first_k), (memory_all, first_v), (hidden_low, first_q), (cross_low, grad_cross_branch)], core
+    )
+    early_got = to_core(send)
+    late_q, late_k, late_v = cross_half(1, after(cross_queries, (keep, send)))
+    late_q, late_k, late_v, early_got = lax.optimization_barrier((late_q, late_k, late_v, early_got))
+    early = line_split(added(keep, early_got))
+    early_send = part_of(early, line ^ 1, 1)
+    early_got = to_y(early_send)
+    late_q, early_q = after((late_q, early_q), early_send)
+
+    grad_cross_queries = jnp.concatenate([early_q, late_q], axis=1)
     grad_cross_query_bias = jnp.sum(grad_cross_queries.astype(f32), axis=0)
-    grad_cross_query = dot(hidden_low.T, grad_cross_queries).astype(bf16)
     grad_hidden_one = residual_scale * grad_second + dot(grad_cross_queries, cross_query_full.T)
     grad_first, grad_first_gain, grad_first_shift = layer_norm_back(grad_hidden_one, gain_one, normed_one, inverse_one)
     grad_branch = grad_first.astype(bf16)
     grad_self_output_bias = jnp.sum(grad_branch.astype(f32), axis=0)
-    grad_attended = dot(grad_branch, self_out_rel.T).astype(bf16)
-    sends = [grad_attended[:, i * share:(i + 1) * share] for i in range(4)]
-    heads_grad = jnp.concatenate([sends[0], to_core(sends[1]), to_y(sends[2]), to_diagonal(sends[3])])
-    grad_self_output = xor_take(dot(attended.T, grad_branch).astype(bf16).reshape(4, share, width), me_c).reshape(width, width)
-
-    grad_cross_value_bias = jnp.sum(grad_memory_values.astype(f32), axis=0)
-    grad_memory_key_weight = dot(memory_rows.T, grad_memory_keys).astype(bf16)
-    grad_memory_value_weight = dot(memory_rows.T, grad_memory_values).astype(bf16)
-    memory_grad = (dot(grad_memory_keys, memory_key_full.T) + dot(grad_memory_values, memory_value_full.T))[None]
-    middle_sum = sum_over_fsdp(
-        [grad_cross_output, grad_cross_query, grad_memory_key_weight, grad_memory_value_weight, grad_self_output], z, x, core
-    )
-
-    grad_q, grad_k, grad_v = attention_backward(
-        qkv, 0, heads_grad, heads_out, self_lse, [qkv], 1, [qkv], 2, share, scalars, BLK
-    )
-    grad_qkv = jnp.concatenate([grad_q, grad_k, grad_v], axis=1)
-    partial = dot(grad_qkv, projection.T).astype(bf16)
-    near = partial[:rows].astype(f32) + to_core(partial[rows:2 * rows]).astype(f32)
-    far = (partial[2 * rows:3 * rows].astype(f32) + to_core(partial[3 * rows:]).astype(f32)).astype(bf16)
-    token_grad = (residual_scale * grad_first + near + to_y(far).astype(f32))[None]
-
-    own_grad = dot(sequence.T, grad_qkv).astype(bf16).reshape(4, 2, 128, 3 * share)
-    keep = lax.dynamic_index_in_dim(own_grad, x, 1, keepdims=False).astype(f32)
-    part = (keep + to_x(lax.dynamic_index_in_dim(own_grad, x ^ 1, 1, keepdims=False)).astype(f32)).astype(bf16)
-    got = [to_z(lax.dynamic_index_in_dim(part, z ^ k, 0, keepdims=False), k) for k in (1, 2, 3)]
-    total = lax.dynamic_index_in_dim(part, z, 0, keepdims=False).astype(f32)
-    total = (total + got[0].astype(f32) + got[1].astype(f32) + got[2].astype(f32)).astype(bf16)
-    shares = xor_take(jnp.stack([total, to_core(total), to_y(total), to_diagonal(total)]), me_c)
-    grad_self_projection = shares.reshape(4, 128, 3, share).transpose(1, 2, 0, 3).reshape(128, 3 * width).astype(f32)
-
-    value_sums = jnp.stack([jnp.sum(grad_q.astype(f32), axis=0), jnp.sum(grad_v.astype(f32), axis=0)])
-    own_sums = lax.dynamic_update_slice(jnp.zeros((2, width), f32), value_sums, (0, me_c * share))
+    grad_attended = dot(grad_branch, self_out_full.T).astype(bf16)
+    by_heads = jnp.stack([grad_attended[:, i * share:(i + 1) * share] for i in range(4)])
+    sends = [part_of(by_heads, k ^ me_c, 0) for k in range(4)]
+    received = [to_core(sends[1]), to_y(sends[2]), to_diagonal(sends[3])]
+    heads_grad = jnp.concatenate([sends[0]] + received)
+
+    ready_q, ready_k, ready_v, ready_branch = after((late_q, late_k, late_v, grad_branch), received[0])
+    grad_cross_value_bias = jnp.concatenate([jnp.sum(early_v.astype(f32), axis=0), jnp.sum(ready_v.astype(f32), axis=0)])
+    memory_terms = dot(jnp.concatenate([early_k, early_v, ready_k, ready_v], axis=1), jnp.concatenate([
+        memory_key_full[:, :width // 2], memory_value_full[:, :width // 2],
+        memory_key_full[:, width // 2:], memory_value_full[:, width // 2:],
+    ], axis=1).T).astype(bf16)
+    memory_near, memory_far = chip_sums(memory_terms, rows)
+    late_keep, late_send = halves_dot(
+        [(memory_all, ready_k), (memory_all, ready_v), (hidden_low, ready_q), (attended, ready_branch)], core
+    )
+    late_got = to_core(late_send)
+    early = added(part_of(early, line, 1), early_got).reshape(4, 2, 64, 5 * share)
+
+    def heads_back(pair, upstream):
+        return attention_backward(
+            qkv, pair, upstream, heads_out, self_lse, [qkv], 2 + pair, [qkv], 4 + pair, share // 2, scalars, BLK,
+            units=1, o_col=pair,
+        )
+
+    def own_blocks(grads):
+        return dot(sequence.T, grads).astype(bf16).reshape(8, 128, grads.shape[1])
+
+    heads_grad = after(heads_grad, (early, late_keep, late_send, memory_far))
+    memory_got = to_y(memory_far)
+    early_got = to_x(part_of(early, x ^ 1, 1))
+    first_heads = jnp.concatenate(heads_back(0, heads_grad), axis=1)
+    first_heads, early_got, late_got = lax.optimization_barrier((first_heads, early_got, late_got))
+    first_blocks = own_blocks(first_heads)
+    late = added(late_keep, late_got).reshape(4, 2, 128, 5 * share)
+    late_got = to_x(part_of(late, x ^ 1, 1))
+    early = added(part_of(early, x, 1), early_got)
+    early_sends = [part_of(early, z ^ k, 0) for k in (1, 2, 3)]
+    first_total = from_fsdp(first_blocks)
+    second_heads = jnp.concatenate(heads_back(1, after(heads_grad, (first_blocks, late, early_sends))), axis=1)
+    early_pieces = [to_z(piece, k) for piece, k in zip(early_sends, (1, 2, 3))]
+    second_heads, early_pieces, late_got, memory_got, feed_share = lax.optimization_barrier(
+        (second_heads, early_pieces, late_got, memory_got, feed_share)
+    )
+    second_blocks = own_blocks(second_heads)
+    ready_first, ready_second = after((first_heads, second_heads), second_blocks)
+    token_terms = (
+        dot(ready_first, jnp.concatenate([projection[:, i * share:i * share + 128] for i in range(3)], axis=1).T)
+        + dot(ready_second, jnp.concatenate([projection[:, i * share + 128:(i + 1) * share] for i in range(3)], axis=1).T)
+    ).astype(bf16)
+    token_near, token_far = chip_sums(token_terms, rows)
+    token_got = to_y(token_far)
+    token_grad = (residual_scale * grad_first + token_near + token_got.astype(f32))[None]
+    memory_grad = (memory_near + memory_got.astype(f32))[None]
+
+    both_heads = [first_heads.astype(f32), second_heads.astype(f32)]
+    head_sums = jnp.stack([
+        jnp.concatenate([jnp.sum(half[:, at:at + 128], axis=0) for half in both_heads]) for at in (0, 256)
+    ])
+    head_sums = lax.dynamic_update_slice(jnp.zeros((2, width), f32), head_sums, (0, me_c * share))
     vector_grads = jnp.concatenate([
         jnp.stack([
             grad_self_output_bias, grad_first_gain, grad_first_shift, grad_cross_query_bias, grad_cross_value_bias,
-            grad_cross_output_bias, grad_second_gain, grad_second_shift, grad_reduce_bias, grad_third_gain, grad_third_shift,
+            grad_cross_output_bias, grad_second_gain, grad_second_shift,
         ]),
-        grad_expand_bias.reshape(8, 4, 128).transpose(1, 0, 2).reshape(4, width),
+        feed_sums[:3],
+        grad_expand_bias.reshape(4, width),
+        head_sums,
+        jnp.zeros((1, width), f32),
     ])
-    early = lax.dynamic_slice_in_dim(sum_everywhere(vector_grads), me_f * 128, 128, axis=1)
-    late = lax.dynamic_slice_in_dim(sum_everywhere(own_sums), me_f * 128, 128, axis=1)
-
-    feed_all = xor_take(jnp.stack([feed_share, to_core(feed_share), to_y(feed_share), to_diagonal(feed_share)]), me_c)
-    grad_expand = feed_all[:, :128].transpose(1, 0, 2).reshape(128, 4 * width).astype(f32)
-    grad_reduce = feed_all[:, 128:].reshape(512, width).astype(f32)
-
-    grad_cross_memory = jnp.concatenate([middle_sum[2], middle_sum[3]], axis=1)
+    vector_rows = vector_grads.reshape(6, 3, 8, 128).transpose(2, 0, 1, 3).reshape(8, 6, 384).astype(bf16)
+    blocks = jnp.concatenate([second_blocks, vector_rows, jnp.zeros((8, 10, 384), bf16)], axis=1)
+    second_total = from_fsdp(blocks)
+    padded = jnp.concatenate([first_total, jnp.zeros((16, 384), f32)])
+    total = after(jnp.concatenate([padded, second_total], axis=1).astype(bf16), token_got)
+
+    early = part_of(early, z, 0).astype(f32)
+    for piece in early_pieces:
+        early = early + piece.astype(f32)
+    early = early.astype(bf16)
+    late = over_z(added(after(part_of(late, x, 1), (blocks, token_far)), late_got)[None], z)[0]
+    early_got = to_y(early)
+    early = jnp.concatenate([jnp.where(line == 0, early, early_got), jnp.where(line == 0, early_got, early)])
+    late = added(late, to_y(late))
+    grad_cross_memory, grad_cross_query, grad_cross_output, grad_self_output = spread(
+        spread_middle_body, core, [early, to_core(early), late, to_core(late)],
+        [(128, 2 * width), (128, width), (128, width), (128, width)],
+    )
+
+    grad_self_projection, sums = spread(
+        spread_projection_body, me_c, ctx_pieces(total), [(128, 3 * width), (18, 128)]
+    )
+
+    feed_share = after(feed_share, (blocks, token_far))
+    feed_own = added(feed_share, to_y(feed_share)).reshape(2, 256, width)
+    grad_expand, grad_reduce = spread(spread_feed_body, core, [feed_own, to_core(feed_own)], [(128, 4 * width), (512, width)])
+
     return (
-        output,
+        output[None],
         token_grad,
         memory_grad,
         grad_self_projection,
-        middle_sum[4],
-        late[0],
-        late[1],
-        early[0],
-        early[1],
-        early[2],
-        middle_sum[1],
+        grad_self_output,
+        sums[15],
+        sums[16],
+        sums[0],
+        sums[1],
+        sums[2],
+        grad_cross_query,
         grad_cross_memory,
-        middle_sum[0],
-        early[3],
-        early[4],
-        early[5],
-        early[6],
-        early[7],
+        grad_cross_output,
+        sums[3],
+        sums[4],
+        sums[5],
+        sums[6],
+        sums[7],
         grad_expand,
         grad_reduce,
-        early[11:15].reshape(512),
-        early[8],
-        early[9],
-        early[10],
+        sums[11:15].reshape(512),
+        sums[8],
+        sums[9],
+        sums[10],
     )
 
 

time: 1270 us -> 672 us (0.53)
  Pallas kernels: 503 us -> 194 us
  waiting for transfers between devices: 406 us -> 185 us
  starting transfers between devices: 98 us -> 65.7 us
  matrix products: 114 us -> 82.1 us
  blocking collectives: 19.3 us -> 0 us
  other arithmetic: 47.8 us -> 66 us
    pallas_call x2 -> x5, Pallas kernels: 370 us -> 54.6 us  [the longest x1 46.2 us: feed_forward(): pl.pallas_call(feed_body, grid_spec=pltpu.PrefetchScalarGridSpec(num_scal...]
    ppermute x13 -> x11, waiting for transfers between devices: 123 us -> 27.4 us  [to_y(): return lax.ppermute(v, 'ctx', y_perm())]
    ppermute x18 -> x9, waiting for transfers between devices: 156 us -> 62.8 us  [to_z(): return lax.ppermute(v, 'fsdp', z_perm(k))]
    all_gather x2, waiting for transfers between devices: 0.01 us -> 66.2 us  [the longest x1 56 us: tiled_shards(): lax.all_gather(after(feed_own, (middle_all, heads_out)), ('fsdp', 'ctx'),...]
    reduce_scatter x1, waiting for transfers between devices: 65.6 us -> 0.02 us  [tiled_shards(): lax.psum_scatter(feed_half, 'fsdp', scatter_dimension=0, tiled=True)]
    dot_general x27 -> x14, matrix products: 114 us -> 58 us  [dot(): return jnp.dot(left, right, preferred_element_type=f32)]
    dot_general x0 -> x16, matrix products: none -> 24.1 us  [side(): jnp.dot(left.T, chosen, preferred_element_type=jnp.float32)]
    ppermute x28 -> x16, starting transfers between devices: 36.2 us -> 13.4 us  [to_core(): return lax.ppermute(v, 'ctx', core_perm())]
  transfers between devices with their start and end apart: 78 -> 49, of which waited for: 24 -> 17; matrix products, arithmetic and copies ran while one was open for 11% -> 24% of each run, Pallas kernels for 40% -> 22%
where the time goes in v2:
time: 672 us; the launch traced here: 662 us
  Pallas kernels  194 us (29%)
  waiting for transfers between devices  185 us (28%)
  matrix products  82.1 us (12%)
  other arithmetic  66 us (10%)
  starting transfers between devices  65.7 us (10%)
  local copies, waits for them, and re-layouts  52.3 us (8%)
  between operations  15.7 us (2%)
    pallas_call x4, Pallas kernels, attention_backward(): pl.pallas_call(body, grid_spec=pltpu.PrefetchScalarGridSpec(num_scalar_pr...  89 us
    ppermute x9, waiting for transfers between devices, to_z(): return lax.ppermute(v, 'fsdp', z_perm(k))  62.8 us
    dot_general x14, matrix products, dot(): return jnp.dot(left, right, preferred_element_type=f32)  58 us
    all_gather x1, waiting for transfers between devices, tiled_shards(): lax.all_gather(after(feed_own, (middle_all, heads_out)), ('fsdp', 'ctx'),...  56 us
    pallas_call x2, Pallas kernels, attention_forward(): pl.pallas_call(body, grid_spec=pltpu.PrefetchScalarGridSpec(num_scalar_pr...  50.7 us
    pallas_call x1, Pallas kernels, feed_forward(): pl.pallas_call(feed_body, grid_spec=pltpu.PrefetchScalarGridSpec(num_scal...  46.2 us
    convert_element_type x10, other arithmetic, added(): (keep.astype(jnp.float32) + got.astype(jnp.float32)).astype(jnp.bfloat16)  27.8 us
    ppermute x11, waiting for transfers between devices, to_y(): return lax.ppermute(v, 'ctx', y_perm())  27.4 us
  transfers between devices with their start and end apart: 49, of which 17 were waited for; matrix products, arithmetic and copies ran while one was open for 24% of the time, Pallas kernels for 22%

profile of v2, /device:TPU:11, one launch (start us, length us, event | category | flops | bytes accessed | tf_op | source)
XLA Modules:
  0.0 661.6 jit_solution(13870233175761913304)
XLA Ops:
  27.9 9.7 %collective-permute-done.3.refs_3_ = bf16[144,768]{1,0:T(8,128)(2,1)S(1)} collective-permute-done((bf16[144,768]{1,0:T(8,128)(2,1)S(1)}, bf16[144,768]{1,0:T(8,128)(2,1)S(1)}, u32[]{:S(2)}, u32[]{:S(2)}) %collective-permute-start.3) | collective-permute-done | bytes 221216 | tf_op jit(solution)/shard_map/ppermute | solution.py:465
  37.6 10.3 %collective-permute-done.4.refs_4_ = bf16[144,768]{1,0:T(8,128)(2,1)S(1)} collective-permute-done((bf16[144,768]{1,0:T(8,128)(2,1)S(1)}, bf16[144,768]{1,0:T(8,128)(2,1)S(1)}, u32[]{:S(2)}, u32[]{:S(2)}) %collective-permute-start.4) | collective-permute-done | bytes 221216 | tf_op jit(solution)/shard_map/ppermute | solution.py:465
  62.7 8.1 %collective-permute-done.7.refs_6_ = bf16[144,768]{1,0:T(8,128)(2,1)S(1)} collective-permute-done((bf16[144,768]{1,0:T(8,128)(2,1)S(1)}, bf16[144,768]{1,0:T(8,128)(2,1)S(1)}, u32[]{:S(2)}, u32[]{:S(2)}) %collective-permute-start.7) | collective-permute-done | bytes 221216 | tf_op jit(solution)/shard_map/ppermute | solution.py:461
  91.2 21.2 %shard_map.434 = (bf16[2048,256]{1,0:T(8,128)(2,1)S(1)}, f32[2,8,4096]{2,1,0:T(8,128)S(1)}) custom-call(s32[4]{0:T(128)S(1)} %bitcast.275, s32[64]{0:T(128)S(1)} %reshape_squeeze.24.refs_1_, s32[1]{0:T(128)} %bitcast.3.refs_2_.me_ref, bf16[2048,768]{1,0:T(8,128)(2,1)S(1)} %add_convert_fusion.3.refs_3_.refs_4_.refs_5_.refs_7_.refs_8_, ...), custom_call_target="tpu_custom_call" | custom-call | flops 8589934592 | bytes 4194304 | tf_op jit(solution)/shard_map/pallas_call | solution.py:235
  112.4 14.7 %collective-permute-done.10 = bf16[512,1024]{1,0:T(8,128)(2,1)S(1)} collective-permute-done((bf16[512,1024]{1,0:T(8,128)(2,1)}, bf16[512,1024]{1,0:T(8,128)(2,1)S(1)}, u32[]{:S(2)}, u32[]{:S(2)}) %collective-permute-start.10) | collective-permute-done | bytes 1048608 | tf_op jit(solution)/shard_map/ppermute | solution.py:453
  128.1 10.2 %all-gather.6.cloned.1.call-done = bf16[160,32,1024]{2,1,0:T(8,128)(2,1)} async-done(((bf16[5,32,1024]{2,1,0:T(8,128)(2,1)}), bf16[160,32,1024]{2,1,0:T(8,128)(2,1)}) %all-gather.6.cloned.1.call-update) | async-done | bytes 10485776 | tf_op jit(solution)/shard_map/all_gather | solution.py:670
  153.8 6.1 convolution_convert_fusion.refs_1_.refs_4_
  165.2 29.5 %shard_map.435 = (bf16[512,1024]{1,0:T(8,128)(2,1)S(1)}, f32[8,8,1024]{2,1,0:T(8,128)S(1)}) custom-call(bf16[512,1024]{1,0:T(8,128)(2,1)S(1)} %add_convert_fusion.8.refs_0_, bf16[2048,1024]{1,0:T(8,128)(2,1)} %convolution_convert_fusion.refs_1_.refs_4_, bf16[2048,1024]{1,0:T(8,128)(2,1)} %add_convert_fusion.2.refs_2_.refs_5_), custom_call_target="tpu_custom_call" | custom-call | flops 8589934592 | bytes 10485760 | tf_op jit(solution)/shard_map/pallas_call | solution.py:235
  199.4 56.0 %all-gather.4.cloned.1.call-done = bf16[8192,1024]{1,0:T(8,128)(2,1)} async-done(((bf16[256,1024]{1,0:T(8,128)(2,1)}), bf16[8192,1024]{1,0:T(8,128)(2,1)}) %all-gather.4.cloned.1.call-update) | async-done | bytes 16777232 | tf_op jit(solution)/shard_map/all_gather | solution.py:693
  255.4 46.2 %shard_map.436 = (bf16[512,1024]{1,0:T(8,128)(2,1)}, f32[512,1024]{1,0:T(8,128)}, bf16[8,2,256,1024]{3,2,1,0:T(8,128)(2,1)}, bf16[8,2,256,1024]{3,2,1,0:T(8,128)...) custom-call(s32[1]{0:T(128)} %bitcast.core_ref, f32[512,1024]{1,0:T(8,128)} %multiply_add_fusion.1.hidden_ref, ...), custom_call_target="tpu_custom_call" | custom-call | flops 25769803776 | bytes 54525952 | tf_op jit(solution)/shard_map/pallas_call | solution.py:389
  312.1 27.4 %shard_map.437 = (bf16[512,512]{1,0:T(8,128)(2,1)S(1)}, bf16[2048,512]{1,0:T(8,128)(2,1)S(1)}, bf16[2048,512]{1,0:T(8,128)(2,1)}) custom-call(bf16[512,1024]{1,0:T(8,128)(2,1)S(1)} %copy-done.14, bf16[512,1024]{1,0:T(8,128)(2,1)S(1)} %convolution_convert_fusion.2.refs_1_, bf16[512,1024]{1,0:T(8,128)(2,1)S(1)} %copy-done.7, f32[8,8,1024]{2,1,0:T(8,128)S(1)} %copy-done.20, ...), custom_call_target="tpu_custom_call" | custom-call | flops 10737418240 | bytes 10485760 | tf_op jit(solution)/shard_map/pallas_call | solution.py:281
  339.5 11.9 %add_convert_fusion = bf16[8,2,256,1024]{3,2,1,0:T(8,128)(2,1)} fusion(bf16[8,2,256,1024]{3,2,1,0:T(8,128)(2,1)} %collective-permute-done.16, bf16[8,2,256,1024]{3,2,1,0:T(8,128)(2,1)} %get-tuple-element.117), kind=kLoop, calls=%fused_computation | loop fusion | flops 16777216 | bytes 25165824 | tf_op jit(solution)/shard_map/convert_element_type | solution.py:528
  370.5 27.3 %shard_map.438 = (bf16[512,512]{1,0:T(8,128)(2,1)S(1)}, bf16[2048,512]{1,0:T(8,128)(2,1)S(1)}, bf16[2048,512]{1,0:T(8,128)(2,1)}) custom-call(bf16[512,1024]{1,0:T(8,128)(2,1)S(1)} %copy-done.15, bf16[512,1024]{1,0:T(8,128)(2,1)S(1)} %copy-done.17, bf16[512,1024]{1,0:T(8,128)(2,1)S(1)} %copy-done.9, f32[8,8,1024]{2,1,0:T(8,128)S(1)} %copy-done.21, ...), custom_call_target="tpu_custom_call" | custom-call | flops 10737418240 | bytes 10485760 | tf_op jit(solution)/shard_map/pallas_call | solution.py:281
  417.9 13.9 %fusion.15 = bf16[2048,1024]{1,0:T(8,128)(2,1)} fusion(bf16[1024,512]{1,0:T(8,128)(2,1)} %get-tuple-element.271, bf16[1024,512]{1,0:T(8,128)(2,1)} %get-tuple-element.196, bf16[1024,512]{1,0:T(8,128)(2,1)} %get-tuple-element.272, bf16[1024,512]{1,0:T(8,128)(2,1)S(1)} %get-tuple-element.195, bf16[2048,512]{1,0:T(8,128)(2,1)} %get-tuple-element.133, ...), kind=kOutput, calls=%fused_computation.23 | convolution fusion | flops 8642363392 | bytes 16777216 | tf_op jit(solution)/shard_map/dot_general | solution.py:647
  450.7 6.3 collective-permute-done.20
  466.0 17.3 %shard_map.439 = (bf16[2048,128]{1,0:T(8,128)(2,1)S(1)}, bf16[2048,128]{1,0:T(8,128)(2,1)S(1)}, bf16[2048,128]{1,0:T(8,128)(2,1)S(1)}) custom-call(s32[4]{0:T(128)S(1)} %bitcast.276, s32[64]{0:T(128)S(1)} %reshape_squeeze.24.refs_1_, s32[1]{0:T(128)} %bitcast.3.refs_2_.me_ref, bf16[2048,768]{1,0:T(8,128)(2,1)} %copy-done.18, ...), custom_call_target="tpu_custom_call" | custom-call | flops 10737418240 | bytes 4194304 | tf_op jit(solution)/shard_map/pallas_call | solution.py:281
  491.3 8.8 %collective-permute-start.26 = (bf16[64,1280]{1,0:T(8,128)(2,1)}, bf16[64,1280]{1,0:T(8,128)(2,1)}, u32[]{:S(2)}, u32[]{:S(2)}) collective-permute-start(bf16[64,1280]{1,0:T(8,128)(2,1)} %get-tuple-element.228), channel_id=1, source_target_pairs={{0,4},{1,5},{2,6},{3,7},{4,0},{5,1},{6,2},{7,3},{8,12},{9,13},{10,... | collective-permute-start | bytes 491528 | tf_op jit(solution)/shard_map/ppermute | solution.py:465
  505.6 6.5 all-to-all-start
  512.1 17.0 %shard_map.440 = (bf16[2048,128]{1,0:T(8,128)(2,1)S(1)}, bf16[2048,128]{1,0:T(8,128)(2,1)S(1)}, bf16[2048,128]{1,0:T(8,128)(2,1)S(1)}) custom-call(s32[4]{0:T(128)S(1)} %bitcast.277, s32[64]{0:T(128)S(1)} %reshape_squeeze.24.refs_1_, s32[1]{0:T(128)} %bitcast.3.refs_2_.me_ref, bf16[2048,768]{1,0:T(8,128)(2,1)} %copy-done.18, ...), custom_call_target="tpu_custom_call" | custom-call | flops 10737418240 | bytes 4194304 | tf_op jit(solution)/shard_map/pallas_call | solution.py:281
  556.7 14.6 %all-to-all-start.1 = ((bf16[8,144,384]{2,1,0:T(8,128)(2,1)}), bf16[8,144,384]{2,1,0:T(8,128)(2,1)S(1)}, u32[]{:S(2)}, u32[]{:S(2)}) async-start(bf16[8,144,384]{2,1,0:T(8,128)(2,1)} %maximum_maximum_fusion), calls=%async_computation.2 | async-start | bytes 1769472 | tf_op jit(solution)/shard_map/all_to_all | solution.py:519
  581.2 12.2 %collective-permute-done.37 = bf16[1,128,1280]{2,1,0:T(8,128)(2,1)S(1)} collective-permute-done((bf16[1,128,1280]{2,1,0:T(8,128)(2,1)S(1)}, bf16[1,128,1280]{2,1,0:T(8,128)(2,1)S(1)}, u32[]{:S(2)}, u32[]{:S(2)}) %collective-permute-start.37) | collective-permute-done | bytes 327712 | tf_op jit(solution)/shard_map/ppermute | solution.py:465
  593.4 18.7 %collective-permute-done.38 = bf16[1,128,1280]{2,1,0:T(8,128)(2,1)S(1)} collective-permute-done((bf16[1,128,1280]{2,1,0:T(8,128)(2,1)S(1)}, bf16[1,128,1280]{2,1,0:T(8,128)(2,1)S(1)}, u32[]{:S(2)}, u32[]{:S(2)}) %collective-permute-start.38) | collective-permute-done | bytes 327712 | tf_op jit(solution)/shard_map/ppermute | solution.py:465
  612.1 8.1 %collective-permute-done.39 = bf16[1,128,1280]{2,1,0:T(8,128)(2,1)S(1)} collective-permute-done((bf16[1,128,1280]{2,1,0:T(8,128)(2,1)S(1)}, bf16[1,128,1280]{2,1,0:T(8,128)(2,1)S(1)}, u32[]{:S(2)}, u32[]{:S(2)}) %collective-permute-start.39) | collective-permute-done | bytes 327712 | tf_op jit(solution)/shard_map/ppermute | solution.py:465
  623.4 9.1 %collective-permute-done.40 = bf16[128,1280]{1,0:T(8,128)(2,1)} collective-permute-done((bf16[128,1280]{1,0:T(8,128)(2,1)S(1)}, bf16[128,1280]{1,0:T(8,128)(2,1)}, u32[]{:S(2)}, u32[]{:S(2)}) %collective-permute-start.40) | collective-permute-done | bytes 327712 | tf_op jit(solution)/shard_map/ppermute | solution.py:453
  (464 shorter events, 234.8 us)
Async XLA Ops:
  7.3 131.0 %all-gather.6.cloned.1.call-start = ((), (), s32[]{:S(2)}) async-start(), calls=%async_computation.5 | async-start | bytes 10813440 | tf_op jit(solution)/shard_map/all_gather | solution.py:670
  11.9 243.6 %all-gather.4.cloned.1.call-start = ((), (), s32[]{:S(2)}) async-start(), calls=%async_computation.3 | async-start | bytes 17301504 | tf_op jit(solution)/shard_map/all_gather | solution.py:693
  11.9 36.0 %collective-permute-start.1 = (bf16[512,1024]{1,0:T(8,128)(2,1)}, bf16[512,1024]{1,0:T(8,128)(2,1)}, u32[]{:S(2)}, u32[]{:S(2)}) collective-permute-start(bf16[512,1024]{1,0:T(8,128)(2,1)} %bitcast.1), channel_id=1, source_target_pairs={{0,16},{8,24},{16,0},{24,8},{1,17},{9,25},{17,1},{25,9},{2,18},{10... | collective-permute-start | bytes 3145736 | tf_op jit(solution)/shard_map/ppermute | solution.py:453
  22.2 63.3 %collective-permute-start = (bf16[512,1024]{1,0:T(8,128)(2,1)}, bf16[512,1024]{1,0:T(8,128)(2,1)}, u32[]{:S(2)}, u32[]{:S(2)}) collective-permute-start(bf16[512,1024]{1,0:T(8,128)(2,1)} %bitcast.1), channel_id=1, source_target_pairs={{0,8},{8,0},{16,24},{24,16},{1,9},{9,1},{17,25},{25,17},{2,10},{10... | collective-permute-start | bytes 3145736 | tf_op jit(solution)/shard_map/ppermute | solution.py:449
  47.9 37.6 %collective-permute-start.5 = (bf16[512,1024]{1,0:T(8,128)(2,1)}, bf16[512,1024]{1,0:T(8,128)(2,1)}, u32[]{:S(2)}, u32[]{:S(2)}) collective-permute-start(bf16[512,1024]{1,0:T(8,128)(2,1)} %collective-permute-done.1), channel_id=1, source_target_pairs={{0,8},{8,0},{16,24},{24,16},{1,9},{9,1},{17,25},{25,17},{2,10},{10... | collective-permute-start | bytes 3145736 | tf_op jit(solution)/shard_map/ppermute | solution.py:449
  85.2 41.9 %collective-permute-start.10 = (bf16[512,1024]{1,0:T(8,128)(2,1)}, bf16[512,1024]{1,0:T(8,128)(2,1)S(1)}, u32[]{:S(2)}, u32[]{:S(2)}) collective-permute-start(bf16[512,1024]{1,0:T(8,128)(2,1)} %bitcast.303), channel_id=1, source_target_pairs={{0,16},{8,24},{16,0},{24,8},{1,17},{9,25},{17,1},{25,9},{2,18},{10... | collective-permute-start | bytes 3145736 | tf_op jit(solution)/shard_map/ppermute | solution.py:453
  138.4 391.1 %reduce-scatter.2.cloned.1.call-start = ((), (), s32[]{:S(2)}) async-start(), calls=%async_computation.4 | async-start | bytes 9437184 | tf_op jit(solution)/shard_map/reduce_scatter | solution.py:733
  301.7 37.8 %collective-permute-start.16 = (bf16[8,2,256,1024]{3,2,1,0:T(8,128)(2,1)}, bf16[8,2,256,1024]{3,2,1,0:T(8,128)(2,1)}, u32[]{:S(2)}, u32[]{:S(2)}) collective-permute-start(bf16[8,2,256,1024]{3,2,1,0:T(8,128)(2,1)} %get-tuple-element.116), channel_id=1, source_target_pairs={{0,8},{8,0},{16,24},{24,16},{1,9},{9,1},{17,25},{25,17},{2,10},{10... | collective-permute-start | bytes 25165832 | tf_op jit(solution)/shard_map/ppermute | solution.py:449
  359.9 37.9 %collective-permute-start.17 = (bf16[1024,1280]{1,0:T(8,128)(2,1)}, bf16[1024,1280]{1,0:T(8,128)(2,1)}, u32[]{:S(2)}, u32[]{:S(2)}) collective-permute-start(bf16[1024,1280]{1,0:T(8,128)(2,1)} %pad_maximum_fusion.3), channel_id=1, source_target_pairs={{0,8},{8,0},{16,24},{24,16},{1,9},{9,1},{17,25},{25,17},{2,10},{10... | collective-permute-start | bytes 7864328 | tf_op jit(solution)/shard_map/ppermute | solution.py:449
  414.6 43.5 %collective-permute-start.21 = (bf16[8,64,1280]{2,1,0:T(8,128)(2,1)}, bf16[8,64,1280]{2,1,0:T(8,128)(2,1)}, u32[]{:S(2)}, u32[]{:S(2)}) collective-permute-start(bf16[8,64,1280]{2,1,0:T(8,128)(2,1)} %dynamic-slice_bitcast_fusion.2), channel_id=1, source_target_pairs={{0,16},{8,24},{16,0},{24,8},{1,17},{9,25},{17,1},{25,9},{2,18},{10... | collective-permute-start | bytes 3932168 | tf_op jit(solution)/shard_map/ppermute | solution.py:453
  415.0 35.6 %collective-permute-start.19 = (bf16[512,256]{1,0:T(8,128)(2,1)}, bf16[512,256]{1,0:T(8,128)(2,1)}, u32[]{:S(2)}, u32[]{:S(2)}) collective-permute-start(bf16[512,256]{1,0:T(8,128)(2,1)} %get-tuple-element.210), channel_id=1, source_target_pairs={{0,16},{8,24},{16,0},{24,8},{1,17},{9,25},{17,1},{25,9},{2,18},{10... | collective-permute-start | bytes 786440 | tf_op jit(solution)/shard_map/ppermute | solution.py:453
  416.0 40.9 %collective-permute-start.20 = (bf16[512,256]{1,0:T(8,128)(2,1)}, bf16[512,256]{1,0:T(8,128)(2,1)}, u32[]{:S(2)}, u32[]{:S(2)}) collective-permute-start(bf16[512,256]{1,0:T(8,128)(2,1)} %get-tuple-element.209), channel_id=1, source_target_pairs={{0,24},{8,16},{16,8},{24,0},{1,25},{9,17},{17,9},{25,1},{2,26},{10... | collective-permute-start | bytes 786440 | tf_op jit(solution)/shard_map/ppermute | solution.py:457
  440.3 43.2 %collective-permute-start.24 = (bf16[1024,1280]{1,0:T(8,128)(2,1)S(1)}, bf16[1024,1280]{1,0:T(8,128)(2,1)S(1)}, u32[]{:S(2)}, u32[]{:S(2)}) collective-permute-start(bf16[1024,1280]{1,0:T(8,128)(2,1)S(1)} %pad_maximum_fusion.5), channel_id=1, source_target_pairs={{0,8},{8,0},{16,24},{24,16},{1,9},{9,1},{17,25},{25,17},{2,10},{10... | collective-permute-start | bytes 7864328 | tf_op jit(solution)/shard_map/ppermute | solution.py:449
  464.8 64.7 %collective-permute-start.29 = (bf16[512,1024]{1,0:T(8,128)(2,1)}, bf16[512,1024]{1,0:T(8,128)(2,1)}, u32[]{:S(2)}, u32[]{:S(2)}) collective-permute-start(bf16[512,1024]{1,0:T(8,128)(2,1)} %fusion.27), channel_id=1, source_target_pairs={{0,16},{8,24},{16,0},{24,8},{1,17},{9,25},{17,1},{25,9},{2,18},{10... | collective-permute-start | bytes 3145736 | tf_op jit(solution)/shard_map/ppermute | solution.py:453
  487.5 41.9 %collective-permute-start.28 = (bf16[4,128,1280]{2,1,0:T(8,128)(2,1)}, bf16[4,128,1280]{2,1,0:T(8,128)(2,1)}, u32[]{:S(2)}, u32[]{:S(2)}) collective-permute-start(bf16[4,128,1280]{2,1,0:T(8,128)(2,1)} %get-tuple-element.194), channel_id=1, source_target_pairs={{0,1},{1,0},{2,3},{3,2},{4,5},{5,4},{6,7},{7,6},{8,9},{9,8},{10,11... | collective-permute-start | bytes 3932168 | tf_op jit(solution)/shard_map/ppermute | solution.py:461
  488.6 40.8 %collective-permute-start.25 = (bf16[64,1280]{1,0:T(8,128)(2,1)}, bf16[64,1280]{1,0:T(8,128)(2,1)}, u32[]{:S(2)}, u32[]{:S(2)}) collective-permute-start(bf16[64,1280]{1,0:T(8,128)(2,1)} %get-tuple-element.229), channel_id=1, source_target_pairs={{0,2},{1,3},{2,0},{3,1},{4,6},{5,7},{6,4},{7,5},{8,10},{9,11},{10,... | collective-permute-start | bytes 491528 | tf_op jit(solution)/shard_map/ppermute | solution.py:465
  491.3 38.1 %collective-permute-start.26 = (bf16[64,1280]{1,0:T(8,128)(2,1)}, bf16[64,1280]{1,0:T(8,128)(2,1)}, u32[]{:S(2)}, u32[]{:S(2)}) collective-permute-start(bf16[64,1280]{1,0:T(8,128)(2,1)} %get-tuple-element.228), channel_id=1, source_target_pairs={{0,4},{1,5},{2,6},{3,7},{4,0},{5,1},{6,2},{7,3},{8,12},{9,13},{10,... | collective-permute-start | bytes 491528 | tf_op jit(solution)/shard_map/ppermute | solution.py:465
  500.1 29.3 %collective-permute-start.27 = (bf16[64,1280]{1,0:T(8,128)(2,1)}, bf16[64,1280]{1,0:T(8,128)(2,1)}, u32[]{:S(2)}, u32[]{:S(2)}) collective-permute-start(bf16[64,1280]{1,0:T(8,128)(2,1)} %get-tuple-element.227), channel_id=1, source_target_pairs={{0,6},{1,7},{2,4},{3,5},{4,2},{5,3},{6,0},{7,1},{8,14},{9,15},{10,... | collective-permute-start | bytes 491528 | tf_op jit(solution)/shard_map/ppermute | solution.py:465
  505.6 46.3 %all-to-all-start = ((bf16[8,128,384]{2,1,0:T(8,128)(2,1)}), bf16[8,128,384]{2,1,0:T(8,128)(2,1)}, u32[]{:S(2)}, u32[]{:S(2)}) async-start(bf16[8,128,384]{2,1,0:T(8,128)(2,1)} %bitcast.307), calls=%async_computation.1 | async-start | bytes 1572864 | tf_op jit(solution)/shard_map/all_to_all | solution.py:519
  556.7 66.5 %all-to-all-start.1 = ((bf16[8,144,384]{2,1,0:T(8,128)(2,1)}), bf16[8,144,384]{2,1,0:T(8,128)(2,1)S(1)}, u32[]{:S(2)}, u32[]{:S(2)}) async-start(bf16[8,144,384]{2,1,0:T(8,128)(2,1)} %maximum_maximum_fusion), calls=%async_computation.2 | async-start | bytes 1769472 | tf_op jit(solution)/shard_map/all_to_all | solution.py:519
  576.4 35.7 %collective-permute-start.38 = (bf16[1,128,1280]{2,1,0:T(8,128)(2,1)S(1)}, bf16[1,128,1280]{2,1,0:T(8,128)(2,1)S(1)}, u32[]{:S(2)}, u32[]{:S(2)}) collective-permute-start(bf16[1,128,1280]{2,1,0:T(8,128)(2,1)S(1)} %get-tuple-element.207), channel_id=1, source_target_pairs={{0,4},{1,5},{2,6},{3,7},{4,0},{5,1},{6,2},{7,3},{8,12},{9,13},{10,... | collective-permute-start | bytes 983048 | tf_op jit(solution)/shard_map/ppermute | solution.py:465
  578.4 41.7 %collective-permute-start.39 = (bf16[1,128,1280]{2,1,0:T(8,128)(2,1)S(1)}, bf16[1,128,1280]{2,1,0:T(8,128)(2,1)S(1)}, u32[]{:S(2)}, u32[]{:S(2)}) collective-permute-start(bf16[1,128,1280]{2,1,0:T(8,128)(2,1)S(1)} %get-tuple-element.206), channel_id=1, source_target_pairs={{0,6},{1,7},{2,4},{3,5},{4,2},{5,3},{6,0},{7,1},{8,14},{9,15},{10,... | collective-permute-start | bytes 983048 | tf_op jit(solution)/shard_map/ppermute | solution.py:465
  579.7 58.3 %collective-permute-start.31 = (bf16[512,1024]{1,0:T(8,128)(2,1)}, bf16[512,1024]{1,0:T(8,128)(2,1)}, u32[]{:S(2)}, u32[]{:S(2)}) collective-permute-start(bf16[512,1024]{1,0:T(8,128)(2,1)} %fusion.23), channel_id=1, source_target_pairs={{0,16},{8,24},{16,0},{24,8},{1,17},{9,25},{17,1},{25,9},{2,18},{10... | collective-permute-start | bytes 3145736 | tf_op jit(solution)/shard_map/ppermute | solution.py:453
  580.9 55.3 %collective-permute-start.42 = (bf16[512,1024]{1,0:T(8,128)(2,1)S(1)}, bf16[512,1024]{1,0:T(8,128)(2,1)}, u32[]{:S(2)}, u32[]{:S(2)}) collective-permute-start(bf16[512,1024]{1,0:T(8,128)(2,1)S(1)} %copy-done.60), channel_id=1, source_target_pairs={{0,16},{8,24},{16,0},{24,8},{1,17},{9,25},{17,1},{25,9},{2,18},{10... | collective-permute-start | bytes 3145736 | tf_op jit(solution)/shard_map/ppermute | solution.py:453
  (129 other events, 1125.9 us)
Sparse Core Ops, SparseCore 0:
  12.0 126.3 all-gather.5
  141.8 113.5 all-gather.3
  362.9 158.8 reduce-scatter.1

commit v3 on v2

--- a/solution.py
+++ b/solution.py
@@ -777,7 +777,16 @@
     def own_blocks(grads):
         return dot(sequence.T, grads).astype(bf16).reshape(8, 128, grads.shape[1])
 
-    heads_grad = after(heads_grad, (early, late_keep, late_send, memory_far))
+    vector_grads = jnp.concatenate([
+        jnp.stack([
+            grad_self_output_bias, grad_first_gain, grad_first_shift, grad_cross_query_bias, grad_cross_value_bias,
+            grad_cross_output_bias, grad_second_gain, grad_second_shift,
+        ]),
+        feed_sums[:3],
+        grad_expand_bias.reshape(4, width),
+    ])
+    vector_rows = vector_grads.reshape(5, 3, 8, 128).transpose(2, 0, 1, 3).reshape(8, 5, 384).astype(bf16)
+    heads_grad = after(heads_grad, (early, late_keep, late_send, memory_far, vector_rows))
     memory_got = to_y(memory_far)
     early_got = to_x(part_of(early, x ^ 1, 1))
     first_heads = jnp.concatenate(heads_back(0, heads_grad), axis=1)
@@ -800,7 +809,9 @@
         + dot(ready_second, jnp.concatenate([projection[:, i * share + 128:(i + 1) * share] for i in range(3)], axis=1).T)
     ).astype(bf16)
     token_near, token_far = chip_sums(token_terms, rows)
-    token_got = to_y(token_far)
+    feed_near = feed_share
+    feed_far = to_y(feed_share)
+    token_got = to_y(after(token_far, feed_far))
     token_grad = (residual_scale * grad_first + token_near + token_got.astype(f32))[None]
     memory_grad = (memory_near + memory_got.astype(f32))[None]
 
@@ -809,18 +820,9 @@
         jnp.concatenate([jnp.sum(half[:, at:at + 128], axis=0) for half in both_heads]) for at in (0, 256)
     ])
     head_sums = lax.dynamic_update_slice(jnp.zeros((2, width), f32), head_sums, (0, me_c * share))
-    vector_grads = jnp.concatenate([
-        jnp.stack([
-            grad_self_output_bias, grad_first_gain, grad_first_shift, grad_cross_query_bias, grad_cross_value_bias,
-            grad_cross_output_bias, grad_second_gain, grad_second_shift,
-        ]),
-        feed_sums[:3],
-        grad_expand_bias.reshape(4, width),
-        head_sums,
-        jnp.zeros((1, width), f32),
-    ])
-    vector_rows = vector_grads.reshape(6, 3, 8, 128).transpose(2, 0, 1, 3).reshape(8, 6, 384).astype(bf16)
-    blocks = jnp.concatenate([second_blocks, vector_rows, jnp.zeros((8, 10, 384), bf16)], axis=1)
+    head_rows = jnp.concatenate([head_sums, jnp.zeros((1, width), f32)])
+    head_rows = head_rows.reshape(3, 8, 128).transpose(1, 0, 2).reshape(8, 1, 384).astype(bf16)
+    blocks = jnp.concatenate([second_blocks, vector_rows, head_rows, jnp.zeros((8, 10, 384), bf16)], axis=1)
     second_total = from_fsdp(blocks)
     padded = jnp.concatenate([first_total, jnp.zeros((16, 384), f32)])
     total = after(jnp.concatenate([padded, second_total], axis=1).astype(bf16), token_got)
@@ -842,8 +844,7 @@
         spread_projection_body, me_c, ctx_pieces(total), [(128, 3 * width), (18, 128)]
     )
 
-    feed_share = after(feed_share, (blocks, token_far))
-    feed_own = added(feed_share, to_y(feed_share)).reshape(2, 256, width)
+    feed_own = added(feed_near, feed_far).reshape(2, 256, width)
     grad_expand, grad_reduce = spread(spread_feed_body, core, [feed_own, to_core(feed_own)], [(128, 4 * width), (512, width)])
 
     return (

time: 672 us -> 656 us (0.976)
  waiting for transfers between devices: 185 us -> 174 us
  Pallas kernels: 194 us -> 201 us
    all_gather x1, waiting for transfers between devices: 56 us -> 47.5 us  [tiled_shards(): lax.all_gather(after(feed_own, (middle_all, heads_out)), ('fsdp', 'ctx'),...]
    pallas_call x2, Pallas kernels: 50.7 us -> 58.4 us  [attention_forward(): pl.pallas_call(body, grid_spec=pltpu.PrefetchScalarGridSpec(num_scalar_pr...]
    unnamed x227 -> x219, local copies, waits for them, and re-layouts: 25.9 us -> 23.6 us
  transfers between devices with their start and end apart: 49 -> 49, of which waited for: 17 -> 19; matrix products, arithmetic and copies ran while one was open for 24% -> 24% of each run, Pallas kernels for 22% -> 24%
where the time goes in v3:
time: 656 us; the launch traced here: 651 us
  Pallas kernels  201 us (31%)
  waiting for transfers between devices  174 us (27%)
  matrix products  83.3 us (13%)
  other arithmetic  64.8 us (10%)
  starting transfers between devices  62.3 us (9%)
  local copies, waits for them, and re-layouts  50.1 us (8%)
  between operations  15.7 us (2%)
    pallas_call x4, Pallas kernels, attention_backward(): pl.pallas_call(body, grid_spec=pltpu.PrefetchScalarGridSpec(num_scalar_pr...  87.6 us
    ppermute x9, waiting for transfers between devices, to_z(): return lax.ppermute(v, 'fsdp', z_perm(k))  60 us
    pallas_call x2, Pallas kernels, attention_forward(): pl.pallas_call(body, grid_spec=pltpu.PrefetchScalarGridSpec(num_scalar_pr...  58.4 us
    dot_general x14, matrix products, dot(): return jnp.dot(left, right, preferred_element_type=f32)  58.2 us
    all_gather x1, waiting for transfers between devices, tiled_shards(): lax.all_gather(after(feed_own, (middle_all, heads_out)), ('fsdp', 'ctx'),...  47.5 us
    pallas_call x1, Pallas kernels, feed_forward(): pl.pallas_call(feed_body, grid_spec=pltpu.PrefetchScalarGridSpec(num_scal...  46.2 us
    convert_element_type x10, other arithmetic, added(): (keep.astype(jnp.float32) + got.astype(jnp.float32)).astype(jnp.bfloat16)  28.2 us
    dot_general x16, matrix products, side(): jnp.dot(left.T, chosen, preferred_element_type=jnp.float32)  25.2 us
  transfers between devices with their start and end apart: 49, of which 19 were waited for; matrix products, arithmetic and copies ran while one was open for 24% of the time, Pallas kernels for 24%

profile of v3, /device:TPU:11, one launch (start us, length us, event | category | flops | bytes accessed | tf_op | source)
XLA Modules:
  0.0 650.6 jit_solution(1973004205105352164)
XLA Ops:
  27.9 9.7 %collective-permute-done.3.refs_3_ = bf16[144,768]{1,0:T(8,128)(2,1)S(1)} collective-permute-done((bf16[144,768]{1,0:T(8,128)(2,1)S(1)}, bf16[144,768]{1,0:T(8,128)(2,1)S(1)}, u32[]{:S(2)}, u32[]{:S(2)}) %collective-permute-start.3) | collective-permute-done | bytes 221216 | tf_op jit(solution)/shard_map/ppermute | solution.py:465
  37.6 10.3 %collective-permute-done.4.refs_4_ = bf16[144,768]{1,0:T(8,128)(2,1)S(1)} collective-permute-done((bf16[144,768]{1,0:T(8,128)(2,1)S(1)}, bf16[144,768]{1,0:T(8,128)(2,1)S(1)}, u32[]{:S(2)}, u32[]{:S(2)}) %collective-permute-start.4) | collective-permute-done | bytes 221216 | tf_op jit(solution)/shard_map/ppermute | solution.py:465
  62.7 8.1 %collective-permute-done.7.refs_6_ = bf16[144,768]{1,0:T(8,128)(2,1)S(1)} collective-permute-done((bf16[144,768]{1,0:T(8,128)(2,1)S(1)}, bf16[144,768]{1,0:T(8,128)(2,1)S(1)}, u32[]{:S(2)}, u32[]{:S(2)}) %collective-permute-start.7) | collective-permute-done | bytes 221216 | tf_op jit(solution)/shard_map/ppermute | solution.py:461
  91.2 20.4 %shard_map.434 = (bf16[2048,256]{1,0:T(8,128)(2,1)S(1)}, f32[2,8,4096]{2,1,0:T(8,128)S(1)}) custom-call(s32[4]{0:T(128)S(1)} %bitcast.285, s32[64]{0:T(128)S(1)} %reshape_squeeze.24.refs_1_, s32[1]{0:T(128)} %bitcast.3.refs_2_.me_ref, bf16[2048,768]{1,0:T(8,128)(2,1)S(1)} %add_convert_fusion.3.refs_3_.refs_4_.refs_5_.refs_7_.refs_8_, ...), custom_call_target="tpu_custom_call" | custom-call | flops 8589934592 | bytes 4194304 | tf_op jit(solution)/shard_map/pallas_call | solution.py:235
  111.6 15.5 %collective-permute-done.10 = bf16[512,1024]{1,0:T(8,128)(2,1)S(1)} collective-permute-done((bf16[512,1024]{1,0:T(8,128)(2,1)}, bf16[512,1024]{1,0:T(8,128)(2,1)S(1)}, u32[]{:S(2)}, u32[]{:S(2)}) %collective-permute-start.10) | collective-permute-done | bytes 1048608 | tf_op jit(solution)/shard_map/ppermute | solution.py:453
  128.1 10.2 %all-gather.6.cloned.1.call-done = bf16[160,32,1024]{2,1,0:T(8,128)(2,1)} async-done(((bf16[5,32,1024]{2,1,0:T(8,128)(2,1)}), bf16[160,32,1024]{2,1,0:T(8,128)(2,1)}) %all-gather.6.cloned.1.call-update) | async-done | bytes 10485776 | tf_op jit(solution)/shard_map/all_gather | solution.py:670
  147.7 6.1 add_convert_fusion.2.refs_2_.refs_5_
  153.8 6.1 convolution_convert_fusion.refs_1_.refs_4_
  165.3 38.0 %shard_map.435 = (bf16[512,1024]{1,0:T(8,128)(2,1)S(1)}, f32[8,8,1024]{2,1,0:T(8,128)S(1)}) custom-call(bf16[512,1024]{1,0:T(8,128)(2,1)S(1)} %add_convert_fusion.8.refs_0_, bf16[2048,1024]{1,0:T(8,128)(2,1)} %convolution_convert_fusion.refs_1_.refs_4_, bf16[2048,1024]{1,0:T(8,128)(2,1)} %add_convert_fusion.2.refs_2_.refs_5_), custom_call_target="tpu_custom_call" | custom-call | flops 8589934592 | bytes 10485760 | tf_op jit(solution)/shard_map/pallas_call | solution.py:235
  207.9 47.5 %all-gather.4.cloned.1.call-done = bf16[8192,1024]{1,0:T(8,128)(2,1)} async-done(((bf16[256,1024]{1,0:T(8,128)(2,1)}), bf16[8192,1024]{1,0:T(8,128)(2,1)}) %all-gather.4.cloned.1.call-update) | async-done | bytes 16777232 | tf_op jit(solution)/shard_map/all_gather | solution.py:693
  255.4 46.2 %shard_map.436 = (bf16[512,1024]{1,0:T(8,128)(2,1)}, f32[512,1024]{1,0:T(8,128)}, bf16[8,2,256,1024]{3,2,1,0:T(8,128)(2,1)}, bf16[8,2,256,1024]{3,2,1,0:T(8,128)...) custom-call(s32[1]{0:T(128)} %bitcast.core_ref, f32[512,1024]{1,0:T(8,128)} %multiply_add_fusion.1.hidden_ref, ...), custom_call_target="tpu_custom_call" | custom-call | flops 25769803776 | bytes 54525952 | tf_op jit(solution)/shard_map/pallas_call | solution.py:389
  311.2 27.4 %shard_map.437 = (bf16[512,512]{1,0:T(8,128)(2,1)S(1)}, bf16[2048,512]{1,0:T(8,128)(2,1)S(1)}, bf16[2048,512]{1,0:T(8,128)(2,1)}) custom-call(bf16[512,1024]{1,0:T(8,128)(2,1)S(1)} %copy-done.15, bf16[512,1024]{1,0:T(8,128)(2,1)S(1)} %convolution_convert_fusion.2.refs_1_, bf16[512,1024]{1,0:T(8,128)(2,1)S(1)} %copy-done.7, f32[8,8,1024]{2,1,0:T(8,128)S(1)} %copy-done.21, ...), custom_call_target="tpu_custom_call" | custom-call | flops 10737418240 | bytes 10485760 | tf_op jit(solution)/shard_map/pallas_call | solution.py:281
  338.5 11.9 %add_convert_fusion = bf16[8,2,256,1024]{3,2,1,0:T(8,128)(2,1)} fusion(bf16[8,2,256,1024]{3,2,1,0:T(8,128)(2,1)} %collective-permute-done.16, bf16[8,2,256,1024]{3,2,1,0:T(8,128)(2,1)} %get-tuple-element.117), kind=kLoop, calls=%fused_computation | loop fusion | flops 16777216 | bytes 25165824 | tf_op jit(solution)/shard_map/convert_element_type | solution.py:528
  370.5 27.3 %shard_map.438 = (bf16[512,512]{1,0:T(8,128)(2,1)S(1)}, bf16[2048,512]{1,0:T(8,128)(2,1)S(1)}, bf16[2048,512]{1,0:T(8,128)(2,1)}) custom-call(bf16[512,1024]{1,0:T(8,128)(2,1)S(1)} %copy-done.16, bf16[512,1024]{1,0:T(8,128)(2,1)S(1)} %copy-done.18, bf16[512,1024]{1,0:T(8,128)(2,1)S(1)} %copy-done.9, f32[8,8,1024]{2,1,0:T(8,128)S(1)} %copy-done.22, ...), custom_call_target="tpu_custom_call" | custom-call | flops 10737418240 | bytes 10485760 | tf_op jit(solution)/shard_map/pallas_call | solution.py:281
  422.8 14.1 %fusion.15 = bf16[2048,1024]{1,0:T(8,128)(2,1)} fusion(bf16[1024,512]{1,0:T(8,128)(2,1)} %get-tuple-element.271, bf16[1024,512]{1,0:T(8,128)(2,1)} %get-tuple-element.196, bf16[1024,512]{1,0:T(8,128)(2,1)} %get-tuple-element.272, bf16[1024,512]{1,0:T(8,128)(2,1)S(1)} %copy-done.70, bf16[2048,512]{1,0:T(8,128)(2,1)} %get-tuple-element.133, ...), kind=kOutput, calls=%fused_computation.23 | convolution fusion | flops 8642363392 | bytes 16777216 | tf_op jit(solution)/shard_map/dot_general | solution.py:647
  454.4 6.0 collective-permute-done.20
  469.2 16.5 %shard_map.439 = (bf16[2048,128]{1,0:T(8,128)(2,1)S(1)}, bf16[2048,128]{1,0:T(8,128)(2,1)S(1)}, bf16[2048,128]{1,0:T(8,128)(2,1)S(1)}) custom-call(s32[4]{0:T(128)S(1)} %bitcast.286, s32[64]{0:T(128)S(1)} %reshape_squeeze.24.refs_1_, s32[1]{0:T(128)} %bitcast.3.refs_2_.me_ref, bf16[2048,768]{1,0:T(8,128)(2,1)} %copy-done.19, ...), custom_call_target="tpu_custom_call" | custom-call | flops 10737418240 | bytes 4194304 | tf_op jit(solution)/shard_map/pallas_call | solution.py:281
  493.4 9.4 %collective-permute-start.26 = (bf16[64,1280]{1,0:T(8,128)(2,1)}, bf16[64,1280]{1,0:T(8,128)(2,1)}, u32[]{:S(2)}, u32[]{:S(2)}) collective-permute-start(bf16[64,1280]{1,0:T(8,128)(2,1)} %get-tuple-element.228), channel_id=1, source_target_pairs={{0,4},{1,5},{2,6},{3,7},{4,0},{5,1},{6,2},{7,3},{8,12},{9,13},{10,... | collective-permute-start | bytes 491528 | tf_op jit(solution)/shard_map/ppermute | solution.py:465
  508.3 6.5 %all-to-all-start = ((bf16[8,128,384]{2,1,0:T(8,128)(2,1)}), bf16[8,128,384]{2,1,0:T(8,128)(2,1)}, u32[]{:S(2)}, u32[]{:S(2)}) async-start(bf16[8,128,384]{2,1,0:T(8,128)(2,1)} %bitcast.317), calls=%async_computation.1 | async-start | bytes 1572864 | tf_op jit(solution)/shard_map/all_to_all | solution.py:519
  514.9 16.5 %shard_map.440 = (bf16[2048,128]{1,0:T(8,128)(2,1)S(1)}, bf16[2048,128]{1,0:T(8,128)(2,1)S(1)}, bf16[2048,128]{1,0:T(8,128)(2,1)S(1)}) custom-call(s32[4]{0:T(128)S(1)} %bitcast.287, s32[64]{0:T(128)S(1)} %reshape_squeeze.24.refs_1_, s32[1]{0:T(128)} %bitcast.3.refs_2_.me_ref, bf16[2048,768]{1,0:T(8,128)(2,1)} %copy-done.19, ...), custom_call_target="tpu_custom_call" | custom-call | flops 10737418240 | bytes 4194304 | tf_op jit(solution)/shard_map/pallas_call | solution.py:281
  554.1 14.4 %all-to-all-start.1 = ((bf16[8,144,384]{2,1,0:T(8,128)(2,1)}), bf16[8,144,384]{2,1,0:T(8,128)(2,1)}, u32[]{:S(2)}, u32[]{:S(2)}) async-start(bf16[8,144,384]{2,1,0:T(8,128)(2,1)} %maximum_maximum_fusion), calls=%async_computation.2 | async-start | bytes 1769472 | tf_op jit(solution)/shard_map/all_to_all | solution.py:519
  581.1 9.2 %collective-permute-done.38 = bf16[1,128,1280]{2,1,0:T(8,128)(2,1)S(1)} collective-permute-done((bf16[1,128,1280]{2,1,0:T(8,128)(2,1)S(1)}, bf16[1,128,1280]{2,1,0:T(8,128)(2,1)S(1)}, u32[]{:S(2)}, u32[]{:S(2)}) %collective-permute-start.38) | collective-permute-done | bytes 327712 | tf_op jit(solution)/shard_map/ppermute | solution.py:465
  590.2 18.9 %collective-permute-done.39 = bf16[1,128,1280]{2,1,0:T(8,128)(2,1)S(1)} collective-permute-done((bf16[1,128,1280]{2,1,0:T(8,128)(2,1)S(1)}, bf16[1,128,1280]{2,1,0:T(8,128)(2,1)S(1)}, u32[]{:S(2)}, u32[]{:S(2)}) %collective-permute-start.39) | collective-permute-done | bytes 327712 | tf_op jit(solution)/shard_map/ppermute | solution.py:465
  609.1 8.0 %collective-permute-done.40 = bf16[1,128,1280]{2,1,0:T(8,128)(2,1)S(1)} collective-permute-done((bf16[1,128,1280]{2,1,0:T(8,128)(2,1)S(1)}, bf16[1,128,1280]{2,1,0:T(8,128)(2,1)S(1)}, u32[]{:S(2)}, u32[]{:S(2)}) %collective-permute-start.40) | collective-permute-done | bytes 327712 | tf_op jit(solution)/shard_map/ppermute | solution.py:465
  (456 shorter events, 230.8 us)
Async XLA Ops:
  7.3 131.0 %all-gather.6.cloned.1.call-start = ((), (), s32[]{:S(2)}) async-start(), calls=%async_computation.5 | async-start | bytes 10813440 | tf_op jit(solution)/shard_map/all_gather | solution.py:670
  11.8 243.6 %all-gather.4.cloned.1.call-start = ((), (), s32[]{:S(2)}) async-start(), calls=%async_computation.3 | async-start | bytes 17301504 | tf_op jit(solution)/shard_map/all_gather | solution.py:693
  11.9 36.0 %collective-permute-start.1 = (bf16[512,1024]{1,0:T(8,128)(2,1)}, bf16[512,1024]{1,0:T(8,128)(2,1)}, u32[]{:S(2)}, u32[]{:S(2)}) collective-permute-start(bf16[512,1024]{1,0:T(8,128)(2,1)} %bitcast.1), channel_id=1, source_target_pairs={{0,16},{8,24},{16,0},{24,8},{1,17},{9,25},{17,1},{25,9},{2,18},{10... | collective-permute-start | bytes 3145736 | tf_op jit(solution)/shard_map/ppermute | solution.py:453
  22.2 63.3 %collective-permute-start = (bf16[512,1024]{1,0:T(8,128)(2,1)}, bf16[512,1024]{1,0:T(8,128)(2,1)}, u32[]{:S(2)}, u32[]{:S(2)}) collective-permute-start(bf16[512,1024]{1,0:T(8,128)(2,1)} %bitcast.1), channel_id=1, source_target_pairs={{0,8},{8,0},{16,24},{24,16},{1,9},{9,1},{17,25},{25,17},{2,10},{10... | collective-permute-start | bytes 3145736 | tf_op jit(solution)/shard_map/ppermute | solution.py:449
  47.9 37.6 %collective-permute-start.5 = (bf16[512,1024]{1,0:T(8,128)(2,1)}, bf16[512,1024]{1,0:T(8,128)(2,1)}, u32[]{:S(2)}, u32[]{:S(2)}) collective-permute-start(bf16[512,1024]{1,0:T(8,128)(2,1)} %collective-permute-done.1), channel_id=1, source_target_pairs={{0,8},{8,0},{16,24},{24,16},{1,9},{9,1},{17,25},{25,17},{2,10},{10... | collective-permute-start | bytes 3145736 | tf_op jit(solution)/shard_map/ppermute | solution.py:449
  85.2 41.9 %collective-permute-start.10 = (bf16[512,1024]{1,0:T(8,128)(2,1)}, bf16[512,1024]{1,0:T(8,128)(2,1)S(1)}, u32[]{:S(2)}, u32[]{:S(2)}) collective-permute-start(bf16[512,1024]{1,0:T(8,128)(2,1)} %bitcast.313), channel_id=1, source_target_pairs={{0,16},{8,24},{16,0},{24,8},{1,17},{9,25},{17,1},{25,9},{2,18},{10... | collective-permute-start | bytes 3145736 | tf_op jit(solution)/shard_map/ppermute | solution.py:453
  138.4 393.3 %reduce-scatter.2.cloned.1.call-start = ((), (), s32[]{:S(2)}) async-start(), calls=%async_computation.4 | async-start | bytes 9437184 | tf_op jit(solution)/shard_map/reduce_scatter | solution.py:733
  301.7 36.9 %collective-permute-start.16 = (bf16[8,2,256,1024]{3,2,1,0:T(8,128)(2,1)}, bf16[8,2,256,1024]{3,2,1,0:T(8,128)(2,1)}, u32[]{:S(2)}, u32[]{:S(2)}) collective-permute-start(bf16[8,2,256,1024]{3,2,1,0:T(8,128)(2,1)} %get-tuple-element.116), channel_id=1, source_target_pairs={{0,8},{8,0},{16,24},{24,16},{1,9},{9,1},{17,25},{25,17},{2,10},{10... | collective-permute-start | bytes 25165832 | tf_op jit(solution)/shard_map/ppermute | solution.py:449
  359.0 38.8 %collective-permute-start.17 = (bf16[1024,1280]{1,0:T(8,128)(2,1)}, bf16[1024,1280]{1,0:T(8,128)(2,1)}, u32[]{:S(2)}, u32[]{:S(2)}) collective-permute-start(bf16[1024,1280]{1,0:T(8,128)(2,1)} %pad_maximum_fusion.3), channel_id=1, source_target_pairs={{0,8},{8,0},{16,24},{24,16},{1,9},{9,1},{17,25},{25,17},{2,10},{10... | collective-permute-start | bytes 7864328 | tf_op jit(solution)/shard_map/ppermute | solution.py:449
  418.3 43.3 %collective-permute-start.21 = (bf16[8,64,1280]{2,1,0:T(8,128)(2,1)}, bf16[8,64,1280]{2,1,0:T(8,128)(2,1)}, u32[]{:S(2)}, u32[]{:S(2)}) collective-permute-start(bf16[8,64,1280]{2,1,0:T(8,128)(2,1)} %dynamic-slice_bitcast_fusion.2), channel_id=1, source_target_pairs={{0,16},{8,24},{16,0},{24,8},{1,17},{9,25},{17,1},{25,9},{2,18},{10... | collective-permute-start | bytes 3932168 | tf_op jit(solution)/shard_map/ppermute | solution.py:453
  418.4 36.0 %collective-permute-start.19 = (bf16[512,256]{1,0:T(8,128)(2,1)}, bf16[512,256]{1,0:T(8,128)(2,1)}, u32[]{:S(2)}, u32[]{:S(2)}) collective-permute-start(bf16[512,256]{1,0:T(8,128)(2,1)} %get-tuple-element.210), channel_id=1, source_target_pairs={{0,16},{8,24},{16,0},{24,8},{1,17},{9,25},{17,1},{25,9},{2,18},{10... | collective-permute-start | bytes 786440 | tf_op jit(solution)/shard_map/ppermute | solution.py:453
  419.9 40.5 %collective-permute-start.20 = (bf16[512,256]{1,0:T(8,128)(2,1)}, bf16[512,256]{1,0:T(8,128)(2,1)}, u32[]{:S(2)}, u32[]{:S(2)}) collective-permute-start(bf16[512,256]{1,0:T(8,128)(2,1)} %get-tuple-element.209), channel_id=1, source_target_pairs={{0,24},{8,16},{16,8},{24,0},{1,25},{9,17},{17,9},{25,1},{2,26},{10... | collective-permute-start | bytes 786440 | tf_op jit(solution)/shard_map/ppermute | solution.py:457
  445.3 42.9 %collective-permute-start.24 = (bf16[1024,1280]{1,0:T(8,128)(2,1)S(1)}, bf16[1024,1280]{1,0:T(8,128)(2,1)S(1)}, u32[]{:S(2)}, u32[]{:S(2)}) collective-permute-start(bf16[1024,1280]{1,0:T(8,128)(2,1)S(1)} %pad_maximum_fusion.5), channel_id=1, source_target_pairs={{0,8},{8,0},{16,24},{24,16},{1,9},{9,1},{17,25},{25,17},{2,10},{10... | collective-permute-start | bytes 7864328 | tf_op jit(solution)/shard_map/ppermute | solution.py:449
  468.0 63.6 %collective-permute-start.29 = (bf16[512,1024]{1,0:T(8,128)(2,1)}, bf16[512,1024]{1,0:T(8,128)(2,1)}, u32[]{:S(2)}, u32[]{:S(2)}) collective-permute-start(bf16[512,1024]{1,0:T(8,128)(2,1)} %fusion.27), channel_id=1, source_target_pairs={{0,16},{8,24},{16,0},{24,8},{1,17},{9,25},{17,1},{25,9},{2,18},{10... | collective-permute-start | bytes 3145736 | tf_op jit(solution)/shard_map/ppermute | solution.py:453
  490.7 41.0 %collective-permute-start.28 = (bf16[4,128,1280]{2,1,0:T(8,128)(2,1)}, bf16[4,128,1280]{2,1,0:T(8,128)(2,1)}, u32[]{:S(2)}, u32[]{:S(2)}) collective-permute-start(bf16[4,128,1280]{2,1,0:T(8,128)(2,1)} %get-tuple-element.194), channel_id=1, source_target_pairs={{0,1},{1,0},{2,3},{3,2},{4,5},{5,4},{6,7},{7,6},{8,9},{9,8},{10,11... | collective-permute-start | bytes 3932168 | tf_op jit(solution)/shard_map/ppermute | solution.py:461
  491.8 39.8 %collective-permute-start.25 = (bf16[64,1280]{1,0:T(8,128)(2,1)}, bf16[64,1280]{1,0:T(8,128)(2,1)}, u32[]{:S(2)}, u32[]{:S(2)}) collective-permute-start(bf16[64,1280]{1,0:T(8,128)(2,1)} %get-tuple-element.229), channel_id=1, source_target_pairs={{0,2},{1,3},{2,0},{3,1},{4,6},{5,7},{6,4},{7,5},{8,10},{9,11},{10,... | collective-permute-start | bytes 491528 | tf_op jit(solution)/shard_map/ppermute | solution.py:465
  493.4 38.2 %collective-permute-start.26 = (bf16[64,1280]{1,0:T(8,128)(2,1)}, bf16[64,1280]{1,0:T(8,128)(2,1)}, u32[]{:S(2)}, u32[]{:S(2)}) collective-permute-start(bf16[64,1280]{1,0:T(8,128)(2,1)} %get-tuple-element.228), channel_id=1, source_target_pairs={{0,4},{1,5},{2,6},{3,7},{4,0},{5,1},{6,2},{7,3},{8,12},{9,13},{10,... | collective-permute-start | bytes 491528 | tf_op jit(solution)/shard_map/ppermute | solution.py:465
  502.9 28.7 %collective-permute-start.27 = (bf16[64,1280]{1,0:T(8,128)(2,1)}, bf16[64,1280]{1,0:T(8,128)(2,1)}, u32[]{:S(2)}, u32[]{:S(2)}) collective-permute-start(bf16[64,1280]{1,0:T(8,128)(2,1)} %get-tuple-element.227), channel_id=1, source_target_pairs={{0,6},{1,7},{2,4},{3,5},{4,2},{5,3},{6,0},{7,1},{8,14},{9,15},{10,... | collective-permute-start | bytes 491528 | tf_op jit(solution)/shard_map/ppermute | solution.py:465
  508.3 39.8 %all-to-all-start = ((bf16[8,128,384]{2,1,0:T(8,128)(2,1)}), bf16[8,128,384]{2,1,0:T(8,128)(2,1)}, u32[]{:S(2)}, u32[]{:S(2)}) async-start(bf16[8,128,384]{2,1,0:T(8,128)(2,1)} %bitcast.317), calls=%async_computation.1 | async-start | bytes 1572864 | tf_op jit(solution)/shard_map/all_to_all | solution.py:519
  554.1 65.3 %all-to-all-start.1 = ((bf16[8,144,384]{2,1,0:T(8,128)(2,1)}), bf16[8,144,384]{2,1,0:T(8,128)(2,1)}, u32[]{:S(2)}, u32[]{:S(2)}) async-start(bf16[8,144,384]{2,1,0:T(8,128)(2,1)} %maximum_maximum_fusion), calls=%async_computation.2 | async-start | bytes 1769472 | tf_op jit(solution)/shard_map/all_to_all | solution.py:519
  573.5 35.6 %collective-permute-start.39 = (bf16[1,128,1280]{2,1,0:T(8,128)(2,1)S(1)}, bf16[1,128,1280]{2,1,0:T(8,128)(2,1)S(1)}, u32[]{:S(2)}, u32[]{:S(2)}) collective-permute-start(bf16[1,128,1280]{2,1,0:T(8,128)(2,1)S(1)} %get-tuple-element.207), channel_id=1, source_target_pairs={{0,4},{1,5},{2,6},{3,7},{4,0},{5,1},{6,2},{7,3},{8,12},{9,13},{10,... | collective-permute-start | bytes 983048 | tf_op jit(solution)/shard_map/ppermute | solution.py:465
  575.6 41.6 %collective-permute-start.40 = (bf16[1,128,1280]{2,1,0:T(8,128)(2,1)S(1)}, bf16[1,128,1280]{2,1,0:T(8,128)(2,1)S(1)}, u32[]{:S(2)}, u32[]{:S(2)}) collective-permute-start(bf16[1,128,1280]{2,1,0:T(8,128)(2,1)S(1)} %get-tuple-element.206), channel_id=1, source_target_pairs={{0,6},{1,7},{2,4},{3,5},{4,2},{5,3},{6,0},{7,1},{8,14},{9,15},{10,... | collective-permute-start | bytes 983048 | tf_op jit(solution)/shard_map/ppermute | solution.py:465
  580.0 52.7 %collective-permute-start.43 = (bf16[2,256,1024]{2,1,0:T(8,128)(2,1)S(1)}, bf16[2,256,1024]{2,1,0:T(8,128)(2,1)S(1)}, u32[]{:S(2)}, u32[]{:S(2)}) collective-permute-start(bf16[2,256,1024]{2,1,0:T(8,128)(2,1)S(1)} %bitcast.281), channel_id=1, source_target_pairs={{0,8},{8,0},{16,24},{24,16},{1,9},{9,1},{17,25},{25,17},{2,10},{10... | collective-permute-start | bytes 3145736 | tf_op jit(solution)/shard_map/ppermute | solution.py:449
  580.8 48.0 %collective-permute-start.32 = (bf16[512,1024]{1,0:T(8,128)(2,1)}, bf16[512,1024]{1,0:T(8,128)(2,1)}, u32[]{:S(2)}, u32[]{:S(2)}) collective-permute-start(bf16[512,1024]{1,0:T(8,128)(2,1)} %fusion.23), channel_id=1, source_target_pairs={{0,16},{8,24},{16,0},{24,8},{1,17},{9,25},{17,1},{25,9},{2,18},{10... | collective-permute-start | bytes 3145736 | tf_op jit(solution)/shard_map/ppermute | solution.py:453
  (124 other events, 1113.5 us)
Sparse Core Ops, SparseCore 0:
  12.0 126.3 all-gather.5
  141.8 113.6 all-gather.3
  362.0 158.8 reduce-scatter.1

commit v4 on v3

--- a/solution.py
+++ b/solution.py
@@ -166,11 +166,6 @@
     stacked, grads, delta, dq_acc, dk_acc, dv_acc = refs
     query_index = pl.program_id(1)
 
-    def part(ref_list, chunk, unit):
-        if pieces > 1:
-            return ref_list[chunk][:, pair_lanes(unit)]
-        return ref_list[0][chunk * key_rows:(chunk + 1) * key_rows, pair_lanes(unit)]
-
     @pl.when(query_index == 0)
     def clear():
         dk_acc[...] = jnp.zeros_like(dk_acc)
@@ -186,37 +181,37 @@
         second = jnp.sum(product[64:], axis=0, keepdims=True)
         delta[unit] = jnp.broadcast_to(jnp.concatenate([first, second], axis=1), delta.shape[1:])
         dq_acc[unit] = jnp.zeros(dq_acc.shape[1:], jnp.float32)
-    for chunk in range(chunks):
-        flag = seen(scalars, query_index, chunk, per_group, chunks)
-
-        def step(chunk=chunk):
-            for unit in range(units):
-                queries, upstream = stacked[unit], grads[unit]
-                keys, values = part(k_refs, chunk, unit), part(v_refs, chunk, unit)
-                found = mxu(keys, queries, NT)
-                probs = jnp.exp2(found * score_log2 - lse_ref[unit, 0:1])
-                grad_probs = mxu(values, upstream, NT)
-                grad_scores = (probs * (grad_probs - delta[unit, 0:1])).astype(jnp.bfloat16)
-                dv_acc[unit, chunk] += mxu(probs.astype(jnp.bfloat16), upstream, NN)
-                dk_acc[unit, chunk] += mxu(grad_scores, queries, NN)
-                dq_acc[unit] += mxu(grad_scores, keys, TN)
-
-        guarded(flag, step)
+    def step(first, count):
+        rows = slice(first * key_rows, (first + count) * key_rows)
+        for unit in range(units):
+            queries, upstream = stacked[unit], grads[unit]
+            keys, values = k_refs[0][rows, pair_lanes(unit)], v_refs[0][rows, pair_lanes(unit)]
+            found = mxu(keys, queries, NT)
+            probs = jnp.exp2(found * score_log2 - lse_ref[unit, 0:1])
+            grad_probs = mxu(values, upstream, NT)
+            grad_scores = (probs * (grad_probs - delta[unit, 0:1])).astype(jnp.bfloat16)
+            dv_acc[unit, rows] += mxu(probs.astype(jnp.bfloat16), upstream, NN)
+            dk_acc[unit, rows] += mxu(grad_scores, queries, NN)
+            dq_acc[unit] += mxu(grad_scores, keys, TN)
+
+    if masked:
+        for chunk in range(0, chunks, 2):
+            first = seen(scalars, query_index, chunk, per_group, chunks)
+            second = seen(scalars, query_index, chunk + 1, per_group, chunks)
+            pl.when(first & second)(functools.partial(step, chunk, 2))
+            pl.when(first & jnp.logical_not(second))(functools.partial(step, chunk, 1))
+            pl.when(second & jnp.logical_not(first))(functools.partial(step, chunk + 1, 1))
+    else:
+        for chunk in range(chunks):
+            step(chunk, 1)
     for unit in range(units):
         dq_ref[:, pair_lanes(unit)] = (one_pair(dq_acc[unit]) * 0.125).astype(dq_ref.dtype)
 
     @pl.when(query_index == pl.num_programs(1) - 1)
     def finish():
         for unit in range(units):
-            for chunk in range(chunks):
-                if pieces > 1:
-                    rows = slice(None)
-                    dk_ref, dv_ref = dk_refs[chunk], dv_refs[chunk]
-                else:
-                    rows = slice(chunk * key_rows, (chunk + 1) * key_rows)
-                    dk_ref, dv_ref = dk_refs[0], dv_refs[0]
-                dk_ref[rows, pair_lanes(unit)] = (dk_acc[unit, chunk] * 0.125).astype(dk_ref.dtype)
-                dv_ref[rows, pair_lanes(unit)] = dv_acc[unit, chunk].astype(dv_ref.dtype)
+            dk_refs[0][:, pair_lanes(unit)] = (dk_acc[unit] * 0.125).astype(jnp.bfloat16)
+            dv_refs[0][:, pair_lanes(unit)] = dv_acc[unit].astype(jnp.bfloat16)
 
 
 def attention_forward(q, q_col, k_list, k_col, v_list, v_col, width, scalars, key_rows, units=2, per_group=2):
@@ -290,8 +285,8 @@
                 pltpu.VMEM((units, 2 * BLK, 128), jnp.bfloat16),
                 pltpu.VMEM((units, 8, 2 * BLK), jnp.float32),
                 pltpu.VMEM((units, 2 * BLK, 128), jnp.float32),
-                pltpu.VMEM((units, chunks, key_rows, 128), jnp.float32),
-                pltpu.VMEM((units, chunks, key_rows, 128), jnp.float32),
+                pltpu.VMEM((units, keys, 128), jnp.float32),
+                pltpu.VMEM((units, keys, 128), jnp.float32),
             ],
         ),
         out_shape=[jax.ShapeDtypeStruct((rows, width), jnp.bfloat16)] + shape_k + shape_k,

time: 656 us -> 648 us (0.988)
  starting transfers between devices: 62.3 us -> 52.4 us
  Pallas kernels: 201 us -> 193 us
  waiting for transfers between devices: 174 us -> 181 us
    all_gather x1, waiting for transfers between devices: 47.5 us -> 56 us  [tiled_shards(): lax.all_gather(after(feed_own, (middle_all, heads_out)), ('fsdp', 'ctx'),...]
  transfers between devices with their start and end apart: 49 -> 49, of which waited for: 19 -> 20; matrix products, arithmetic and copies ran while one was open for 24% -> 24% of each run, Pallas kernels for 24% -> 23%
where the time goes in v4:
time: 648 us; the launch traced here: 641 us
  Pallas kernels  193 us (30%)
  waiting for transfers between devices  181 us (28%)
  matrix products  83.1 us (13%)
  other arithmetic  64.8 us (10%)
  starting transfers between devices  52.4 us (8%)
  local copies, waits for them, and re-layouts  50 us (8%)
  between operations  15.7 us (2%)
    pallas_call x4, Pallas kernels, attention_backward(): pl.pallas_call(body, grid_spec=pltpu.PrefetchScalarGridSpec(num_scalar_pr...  86 us
    dot_general x14, matrix products, dot(): return jnp.dot(left, right, preferred_element_type=f32)  58 us
    ppermute x9, waiting for transfers between devices, to_z(): return lax.ppermute(v, 'fsdp', z_perm(k))  56.5 us
    all_gather x1, waiting for transfers between devices, tiled_shards(): lax.all_gather(after(feed_own, (middle_all, heads_out)), ('fsdp', 'ctx'),...  56 us
    pallas_call x2, Pallas kernels, attention_forward(): pl.pallas_call(body, grid_spec=pltpu.PrefetchScalarGridSpec(num_scalar_pr...  52.5 us
    pallas_call x1, Pallas kernels, feed_forward(): pl.pallas_call(feed_body, grid_spec=pltpu.PrefetchScalarGridSpec(num_scal...  46.2 us
    convert_element_type x10, other arithmetic, added(): (keep.astype(jnp.float32) + got.astype(jnp.float32)).astype(jnp.bfloat16)  28.2 us
    ppermute x11, waiting for transfers between devices, to_y(): return lax.ppermute(v, 'ctx', y_perm())  27.1 us
  transfers between devices with their start and end apart: 49, of which 20 were waited for; matrix products, arithmetic and copies ran while one was open for 24% of the time, Pallas kernels for 23%

profile of v4, /device:TPU:11, one launch (start us, length us, event | category | flops | bytes accessed | tf_op | source)
XLA Modules:
  0.0 640.8 jit_solution(4392946503073674924)
XLA Ops:
  27.9 9.7 %collective-permute-done.3.refs_3_ = bf16[144,768]{1,0:T(8,128)(2,1)S(1)} collective-permute-done((bf16[144,768]{1,0:T(8,128)(2,1)S(1)}, bf16[144,768]{1,0:T(8,128)(2,1)S(1)}, u32[]{:S(2)}, u32[]{:S(2)}) %collective-permute-start.3) | collective-permute-done | bytes 221216 | tf_op jit(solution)/shard_map/ppermute | solution.py:460
  37.6 10.3 %collective-permute-done.4.refs_4_ = bf16[144,768]{1,0:T(8,128)(2,1)S(1)} collective-permute-done((bf16[144,768]{1,0:T(8,128)(2,1)S(1)}, bf16[144,768]{1,0:T(8,128)(2,1)S(1)}, u32[]{:S(2)}, u32[]{:S(2)}) %collective-permute-start.4) | collective-permute-done | bytes 221216 | tf_op jit(solution)/shard_map/ppermute | solution.py:460
  62.7 8.1 %collective-permute-done.7.refs_6_ = bf16[144,768]{1,0:T(8,128)(2,1)S(1)} collective-permute-done((bf16[144,768]{1,0:T(8,128)(2,1)S(1)}, bf16[144,768]{1,0:T(8,128)(2,1)S(1)}, u32[]{:S(2)}, u32[]{:S(2)}) %collective-permute-start.7) | collective-permute-done | bytes 221216 | tf_op jit(solution)/shard_map/ppermute | solution.py:456
  85.6 5.6 add_convert_fusion.3.refs_3_.refs_4_.refs_5_.refs_7_.refs_8_
  91.2 23.0 %shard_map.434 = (bf16[2048,256]{1,0:T(8,128)(2,1)S(1)}, f32[2,8,4096]{2,1,0:T(8,128)S(1)}) custom-call(s32[4]{0:T(128)S(1)} %bitcast.285, s32[64]{0:T(128)S(1)} %reshape_squeeze.24.refs_1_, s32[1]{0:T(128)} %bitcast.3.refs_2_.me_ref, bf16[2048,768]{1,0:T(8,128)(2,1)S(1)} %add_convert_fusion.3.refs_3_.refs_4_.refs_5_.refs_7_.refs_8_, ...), custom_call_target="tpu_custom_call" | custom-call | flops 8589934592 | bytes 4194304 | tf_op jit(solution)/shard_map/pallas_call | solution.py:230
  114.2 12.9 %collective-permute-done.10 = bf16[512,1024]{1,0:T(8,128)(2,1)S(1)} collective-permute-done((bf16[512,1024]{1,0:T(8,128)(2,1)}, bf16[512,1024]{1,0:T(8,128)(2,1)S(1)}, u32[]{:S(2)}, u32[]{:S(2)}) %collective-permute-start.10) | collective-permute-done | bytes 1048608 | tf_op jit(solution)/shard_map/ppermute | solution.py:448
  128.1 10.2 %all-gather.6.cloned.1.call-done = bf16[160,32,1024]{2,1,0:T(8,128)(2,1)} async-done(((bf16[5,32,1024]{2,1,0:T(8,128)(2,1)}), bf16[160,32,1024]{2,1,0:T(8,128)(2,1)}) %all-gather.6.cloned.1.call-update) | async-done | bytes 10485776 | tf_op jit(solution)/shard_map/all_gather | solution.py:665
  147.7 6.1 add_convert_fusion.2.refs_2_.refs_5_
  153.8 6.1 convolution_convert_fusion.refs_1_.refs_4_
  165.3 29.5 %shard_map.435 = (bf16[512,1024]{1,0:T(8,128)(2,1)S(1)}, f32[8,8,1024]{2,1,0:T(8,128)S(1)}) custom-call(bf16[512,1024]{1,0:T(8,128)(2,1)S(1)} %add_convert_fusion.8.refs_0_, bf16[2048,1024]{1,0:T(8,128)(2,1)} %convolution_convert_fusion.refs_1_.refs_4_, bf16[2048,1024]{1,0:T(8,128)(2,1)} %add_convert_fusion.2.refs_2_.refs_5_), custom_call_target="tpu_custom_call" | custom-call | flops 8589934592 | bytes 10485760 | tf_op jit(solution)/shard_map/pallas_call | solution.py:230
  199.4 56.0 %all-gather.4.cloned.1.call-done = bf16[8192,1024]{1,0:T(8,128)(2,1)} async-done(((bf16[256,1024]{1,0:T(8,128)(2,1)}), bf16[8192,1024]{1,0:T(8,128)(2,1)}) %all-gather.4.cloned.1.call-update) | async-done | bytes 16777232 | tf_op jit(solution)/shard_map/all_gather | solution.py:688
  255.4 46.2 %shard_map.436 = (bf16[512,1024]{1,0:T(8,128)(2,1)}, f32[512,1024]{1,0:T(8,128)}, bf16[8,2,256,1024]{3,2,1,0:T(8,128)(2,1)}, bf16[8,2,256,1024]{3,2,1,0:T(8,128)...) custom-call(s32[1]{0:T(128)} %bitcast.core_ref, f32[512,1024]{1,0:T(8,128)} %multiply_add_fusion.1.hidden_ref, ...), custom_call_target="tpu_custom_call" | custom-call | flops 25769803776 | bytes 54525952 | tf_op jit(solution)/shard_map/pallas_call | solution.py:384
  311.1 27.4 %shard_map.437 = (bf16[512,512]{1,0:T(8,128)(2,1)S(1)}, bf16[2048,512]{1,0:T(8,128)(2,1)S(1)}, bf16[2048,512]{1,0:T(8,128)(2,1)}) custom-call(bf16[512,1024]{1,0:T(8,128)(2,1)S(1)} %copy-done.15, bf16[512,1024]{1,0:T(8,128)(2,1)S(1)} %convolution_convert_fusion.2.refs_1_, bf16[512,1024]{1,0:T(8,128)(2,1)S(1)} %copy-done.7, f32[8,8,1024]{2,1,0:T(8,128)S(1)} %copy-done.21, ...), custom_call_target="tpu_custom_call" | custom-call | flops 10737418240 | bytes 10485760 | tf_op jit(solution)/shard_map/pallas_call | solution.py:276
  338.5 11.9 %add_convert_fusion = bf16[8,2,256,1024]{3,2,1,0:T(8,128)(2,1)} fusion(bf16[8,2,256,1024]{3,2,1,0:T(8,128)(2,1)} %collective-permute-done.16, bf16[8,2,256,1024]{3,2,1,0:T(8,128)(2,1)} %get-tuple-element.117), kind=kLoop, calls=%fused_computation | loop fusion | flops 16777216 | bytes 25165824 | tf_op jit(solution)/shard_map/convert_element_type | solution.py:523
  370.5 27.3 %shard_map.438 = (bf16[512,512]{1,0:T(8,128)(2,1)S(1)}, bf16[2048,512]{1,0:T(8,128)(2,1)S(1)}, bf16[2048,512]{1,0:T(8,128)(2,1)}) custom-call(bf16[512,1024]{1,0:T(8,128)(2,1)S(1)} %copy-done.16, bf16[512,1024]{1,0:T(8,128)(2,1)S(1)} %copy-done.18, bf16[512,1024]{1,0:T(8,128)(2,1)S(1)} %copy-done.9, f32[8,8,1024]{2,1,0:T(8,128)S(1)} %copy-done.22, ...), custom_call_target="tpu_custom_call" | custom-call | flops 10737418240 | bytes 10485760 | tf_op jit(solution)/shard_map/pallas_call | solution.py:276
  422.8 13.9 %fusion.15 = bf16[2048,1024]{1,0:T(8,128)(2,1)} fusion(bf16[1024,512]{1,0:T(8,128)(2,1)} %get-tuple-element.271, bf16[1024,512]{1,0:T(8,128)(2,1)} %get-tuple-element.196, bf16[1024,512]{1,0:T(8,128)(2,1)} %get-tuple-element.272, bf16[1024,512]{1,0:T(8,128)(2,1)S(1)} %copy-done.70, bf16[2048,512]{1,0:T(8,128)(2,1)} %get-tuple-element.133, ...), kind=kOutput, calls=%fused_computation.23 | convolution fusion | flops 8642363392 | bytes 16777216 | tf_op jit(solution)/shard_map/dot_general | solution.py:642
  454.4 6.0 collective-permute-done.20
  469.2 15.8 %shard_map.439 = (bf16[2048,128]{1,0:T(8,128)(2,1)S(1)}, bf16[2048,128]{1,0:T(8,128)(2,1)S(1)}, bf16[2048,128]{1,0:T(8,128)(2,1)S(1)}) custom-call(s32[4]{0:T(128)S(1)} %bitcast.286, s32[64]{0:T(128)S(1)} %reshape_squeeze.24.refs_1_, s32[1]{0:T(128)} %bitcast.3.refs_2_.me_ref, bf16[2048,768]{1,0:T(8,128)(2,1)} %copy-done.19, ...), custom_call_target="tpu_custom_call" | custom-call | flops 10737418240 | bytes 4194304 | tf_op jit(solution)/shard_map/pallas_call | solution.py:276
  502.9 6.8 %all-to-all-start = ((bf16[8,128,384]{2,1,0:T(8,128)(2,1)}), bf16[8,128,384]{2,1,0:T(8,128)(2,1)}, u32[]{:S(2)}, u32[]{:S(2)}) async-start(bf16[8,128,384]{2,1,0:T(8,128)(2,1)} %bitcast.317), calls=%async_computation.1 | async-start | bytes 1572864 | tf_op jit(solution)/shard_map/all_to_all | solution.py:514
  509.7 15.6 %shard_map.440 = (bf16[2048,128]{1,0:T(8,128)(2,1)S(1)}, bf16[2048,128]{1,0:T(8,128)(2,1)S(1)}, bf16[2048,128]{1,0:T(8,128)(2,1)S(1)}) custom-call(s32[4]{0:T(128)S(1)} %bitcast.287, s32[64]{0:T(128)S(1)} %reshape_squeeze.24.refs_1_, s32[1]{0:T(128)} %bitcast.3.refs_2_.me_ref, bf16[2048,768]{1,0:T(8,128)(2,1)} %copy-done.19, ...), custom_call_target="tpu_custom_call" | custom-call | flops 10737418240 | bytes 4194304 | tf_op jit(solution)/shard_map/pallas_call | solution.py:276
  549.0 9.2 %all-to-all-start.1 = ((bf16[8,144,384]{2,1,0:T(8,128)(2,1)}), bf16[8,144,384]{2,1,0:T(8,128)(2,1)}, u32[]{:S(2)}, u32[]{:S(2)}) async-start(bf16[8,144,384]{2,1,0:T(8,128)(2,1)} %maximum_maximum_fusion), calls=%async_computation.2 | async-start | bytes 1769472 | tf_op jit(solution)/shard_map/all_to_all | solution.py:514
  565.6 7.6 %collective-permute-done.36 = bf16[64,1280]{1,0:T(8,128)(2,1)S(1)} collective-permute-done((bf16[64,1280]{1,0:T(8,128)(2,1)S(1)}, bf16[64,1280]{1,0:T(8,128)(2,1)S(1)}, u32[]{:S(2)}, u32[]{:S(2)}) %collective-permute-start.36) | collective-permute-done | bytes 163872 | tf_op jit(solution)/shard_map/ppermute | solution.py:448
  580.0 18.9 %collective-permute-done.39 = bf16[1,128,1280]{2,1,0:T(8,128)(2,1)S(1)} collective-permute-done((bf16[1,128,1280]{2,1,0:T(8,128)(2,1)S(1)}, bf16[1,128,1280]{2,1,0:T(8,128)(2,1)S(1)}, u32[]{:S(2)}, u32[]{:S(2)}) %collective-permute-start.39) | collective-permute-done | bytes 327712 | tf_op jit(solution)/shard_map/ppermute | solution.py:460
  598.9 8.0 %collective-permute-done.40 = bf16[1,128,1280]{2,1,0:T(8,128)(2,1)S(1)} collective-permute-done((bf16[1,128,1280]{2,1,0:T(8,128)(2,1)S(1)}, bf16[1,128,1280]{2,1,0:T(8,128)(2,1)S(1)}, u32[]{:S(2)}, u32[]{:S(2)}) %collective-permute-start.40) | collective-permute-done | bytes 327712 | tf_op jit(solution)/shard_map/ppermute | solution.py:460
  (456 shorter events, 233.0 us)
Async XLA Ops:
  7.3 131.0 %all-gather.6.cloned.1.call-start = ((), (), s32[]{:S(2)}) async-start(), calls=%async_computation.5 | async-start | bytes 10813440 | tf_op jit(solution)/shard_map/all_gather | solution.py:665
  11.8 243.6 %all-gather.4.cloned.1.call-start = ((), (), s32[]{:S(2)}) async-start(), calls=%async_computation.3 | async-start | bytes 17301504 | tf_op jit(solution)/shard_map/all_gather | solution.py:688
  11.9 36.0 %collective-permute-start.1 = (bf16[512,1024]{1,0:T(8,128)(2,1)}, bf16[512,1024]{1,0:T(8,128)(2,1)}, u32[]{:S(2)}, u32[]{:S(2)}) collective-permute-start(bf16[512,1024]{1,0:T(8,128)(2,1)} %bitcast.1), channel_id=1, source_target_pairs={{0,16},{8,24},{16,0},{24,8},{1,17},{9,25},{17,1},{25,9},{2,18},{10... | collective-permute-start | bytes 3145736 | tf_op jit(solution)/shard_map/ppermute | solution.py:448
  22.2 63.3 %collective-permute-start = (bf16[512,1024]{1,0:T(8,128)(2,1)}, bf16[512,1024]{1,0:T(8,128)(2,1)}, u32[]{:S(2)}, u32[]{:S(2)}) collective-permute-start(bf16[512,1024]{1,0:T(8,128)(2,1)} %bitcast.1), channel_id=1, source_target_pairs={{0,8},{8,0},{16,24},{24,16},{1,9},{9,1},{17,25},{25,17},{2,10},{10... | collective-permute-start | bytes 3145736 | tf_op jit(solution)/shard_map/ppermute | solution.py:444
  47.9 37.6 %collective-permute-start.5 = (bf16[512,1024]{1,0:T(8,128)(2,1)}, bf16[512,1024]{1,0:T(8,128)(2,1)}, u32[]{:S(2)}, u32[]{:S(2)}) collective-permute-start(bf16[512,1024]{1,0:T(8,128)(2,1)} %collective-permute-done.1), channel_id=1, source_target_pairs={{0,8},{8,0},{16,24},{24,16},{1,9},{9,1},{17,25},{25,17},{2,10},{10... | collective-permute-start | bytes 3145736 | tf_op jit(solution)/shard_map/ppermute | solution.py:444
  85.2 41.9 %collective-permute-start.10 = (bf16[512,1024]{1,0:T(8,128)(2,1)}, bf16[512,1024]{1,0:T(8,128)(2,1)S(1)}, u32[]{:S(2)}, u32[]{:S(2)}) collective-permute-start(bf16[512,1024]{1,0:T(8,128)(2,1)} %bitcast.313), channel_id=1, source_target_pairs={{0,16},{8,24},{16,0},{24,8},{1,17},{9,25},{17,1},{25,9},{2,18},{10... | collective-permute-start | bytes 3145736 | tf_op jit(solution)/shard_map/ppermute | solution.py:448
  138.4 389.0 %reduce-scatter.2.cloned.1.call-start = ((), (), s32[]{:S(2)}) async-start(), calls=%async_computation.4 | async-start | bytes 9437184 | tf_op jit(solution)/shard_map/reduce_scatter | solution.py:728
  301.7 36.8 %collective-permute-start.16 = (bf16[8,2,256,1024]{3,2,1,0:T(8,128)(2,1)}, bf16[8,2,256,1024]{3,2,1,0:T(8,128)(2,1)}, u32[]{:S(2)}, u32[]{:S(2)}) collective-permute-start(bf16[8,2,256,1024]{3,2,1,0:T(8,128)(2,1)} %get-tuple-element.116), channel_id=1, source_target_pairs={{0,8},{8,0},{16,24},{24,16},{1,9},{9,1},{17,25},{25,17},{2,10},{10... | collective-permute-start | bytes 25165832 | tf_op jit(solution)/shard_map/ppermute | solution.py:444
  359.0 38.8 %collective-permute-start.17 = (bf16[1024,1280]{1,0:T(8,128)(2,1)}, bf16[1024,1280]{1,0:T(8,128)(2,1)}, u32[]{:S(2)}, u32[]{:S(2)}) collective-permute-start(bf16[1024,1280]{1,0:T(8,128)(2,1)} %pad_maximum_fusion.3), channel_id=1, source_target_pairs={{0,8},{8,0},{16,24},{24,16},{1,9},{9,1},{17,25},{25,17},{2,10},{10... | collective-permute-start | bytes 7864328 | tf_op jit(solution)/shard_map/ppermute | solution.py:444
  418.3 43.3 %collective-permute-start.21 = (bf16[8,64,1280]{2,1,0:T(8,128)(2,1)}, bf16[8,64,1280]{2,1,0:T(8,128)(2,1)}, u32[]{:S(2)}, u32[]{:S(2)}) collective-permute-start(bf16[8,64,1280]{2,1,0:T(8,128)(2,1)} %dynamic-slice_bitcast_fusion.2), channel_id=1, source_target_pairs={{0,16},{8,24},{16,0},{24,8},{1,17},{9,25},{17,1},{25,9},{2,18},{10... | collective-permute-start | bytes 3932168 | tf_op jit(solution)/shard_map/ppermute | solution.py:448
  418.4 36.0 %collective-permute-start.19 = (bf16[512,256]{1,0:T(8,128)(2,1)}, bf16[512,256]{1,0:T(8,128)(2,1)}, u32[]{:S(2)}, u32[]{:S(2)}) collective-permute-start(bf16[512,256]{1,0:T(8,128)(2,1)} %get-tuple-element.210), channel_id=1, source_target_pairs={{0,16},{8,24},{16,0},{24,8},{1,17},{9,25},{17,1},{25,9},{2,18},{10... | collective-permute-start | bytes 786440 | tf_op jit(solution)/shard_map/ppermute | solution.py:448
  419.9 40.5 %collective-permute-start.20 = (bf16[512,256]{1,0:T(8,128)(2,1)}, bf16[512,256]{1,0:T(8,128)(2,1)}, u32[]{:S(2)}, u32[]{:S(2)}) collective-permute-start(bf16[512,256]{1,0:T(8,128)(2,1)} %get-tuple-element.209), channel_id=1, source_target_pairs={{0,24},{8,16},{16,8},{24,0},{1,25},{9,17},{17,9},{25,1},{2,26},{10... | collective-permute-start | bytes 786440 | tf_op jit(solution)/shard_map/ppermute | solution.py:452
  445.2 43.1 %collective-permute-start.24 = (bf16[1024,1280]{1,0:T(8,128)(2,1)S(1)}, bf16[1024,1280]{1,0:T(8,128)(2,1)S(1)}, u32[]{:S(2)}, u32[]{:S(2)}) collective-permute-start(bf16[1024,1280]{1,0:T(8,128)(2,1)S(1)} %pad_maximum_fusion.5), channel_id=1, source_target_pairs={{0,8},{8,0},{16,24},{24,16},{1,9},{9,1},{17,25},{25,17},{2,10},{10... | collective-permute-start | bytes 7864328 | tf_op jit(solution)/shard_map/ppermute | solution.py:444
  468.0 59.4 %collective-permute-start.29 = (bf16[512,1024]{1,0:T(8,128)(2,1)}, bf16[512,1024]{1,0:T(8,128)(2,1)}, u32[]{:S(2)}, u32[]{:S(2)}) collective-permute-start(bf16[512,1024]{1,0:T(8,128)(2,1)} %fusion.27), channel_id=1, source_target_pairs={{0,16},{8,24},{16,0},{24,8},{1,17},{9,25},{17,1},{25,9},{2,18},{10... | collective-permute-start | bytes 3145736 | tf_op jit(solution)/shard_map/ppermute | solution.py:448
  490.6 36.7 %collective-permute-start.28 = (bf16[4,128,1280]{2,1,0:T(8,128)(2,1)}, bf16[4,128,1280]{2,1,0:T(8,128)(2,1)}, u32[]{:S(2)}, u32[]{:S(2)}) collective-permute-start(bf16[4,128,1280]{2,1,0:T(8,128)(2,1)} %get-tuple-element.194), channel_id=1, source_target_pairs={{0,1},{1,0},{2,3},{3,2},{4,5},{5,4},{6,7},{7,6},{8,9},{9,8},{10,11... | collective-permute-start | bytes 3932168 | tf_op jit(solution)/shard_map/ppermute | solution.py:456
  491.7 33.8 %collective-permute-start.25 = (bf16[64,1280]{1,0:T(8,128)(2,1)}, bf16[64,1280]{1,0:T(8,128)(2,1)}, u32[]{:S(2)}, u32[]{:S(2)}) collective-permute-start(bf16[64,1280]{1,0:T(8,128)(2,1)} %get-tuple-element.229), channel_id=1, source_target_pairs={{0,2},{1,3},{2,0},{3,1},{4,6},{5,7},{6,4},{7,5},{8,10},{9,11},{10,... | collective-permute-start | bytes 491528 | tf_op jit(solution)/shard_map/ppermute | solution.py:460
  493.5 32.0 %collective-permute-start.26 = (bf16[64,1280]{1,0:T(8,128)(2,1)}, bf16[64,1280]{1,0:T(8,128)(2,1)}, u32[]{:S(2)}, u32[]{:S(2)}) collective-permute-start(bf16[64,1280]{1,0:T(8,128)(2,1)} %get-tuple-element.228), channel_id=1, source_target_pairs={{0,4},{1,5},{2,6},{3,7},{4,0},{5,1},{6,2},{7,3},{8,12},{9,13},{10,... | collective-permute-start | bytes 491528 | tf_op jit(solution)/shard_map/ppermute | solution.py:460
  497.1 30.3 %collective-permute-start.27 = (bf16[64,1280]{1,0:T(8,128)(2,1)}, bf16[64,1280]{1,0:T(8,128)(2,1)}, u32[]{:S(2)}, u32[]{:S(2)}) collective-permute-start(bf16[64,1280]{1,0:T(8,128)(2,1)} %get-tuple-element.227), channel_id=1, source_target_pairs={{0,6},{1,7},{2,4},{3,5},{4,2},{5,3},{6,0},{7,1},{8,14},{9,15},{10,... | collective-permute-start | bytes 491528 | tf_op jit(solution)/shard_map/ppermute | solution.py:460
  502.9 40.2 %all-to-all-start = ((bf16[8,128,384]{2,1,0:T(8,128)(2,1)}), bf16[8,128,384]{2,1,0:T(8,128)(2,1)}, u32[]{:S(2)}, u32[]{:S(2)}) async-start(bf16[8,128,384]{2,1,0:T(8,128)(2,1)} %bitcast.317), calls=%async_computation.1 | async-start | bytes 1572864 | tf_op jit(solution)/shard_map/all_to_all | solution.py:514
  549.0 60.7 %all-to-all-start.1 = ((bf16[8,144,384]{2,1,0:T(8,128)(2,1)}), bf16[8,144,384]{2,1,0:T(8,128)(2,1)}, u32[]{:S(2)}, u32[]{:S(2)}) async-start(bf16[8,144,384]{2,1,0:T(8,128)(2,1)} %maximum_maximum_fusion), calls=%async_computation.2 | async-start | bytes 1769472 | tf_op jit(solution)/shard_map/all_to_all | solution.py:514
  563.2 35.6 %collective-permute-start.39 = (bf16[1,128,1280]{2,1,0:T(8,128)(2,1)S(1)}, bf16[1,128,1280]{2,1,0:T(8,128)(2,1)S(1)}, u32[]{:S(2)}, u32[]{:S(2)}) collective-permute-start(bf16[1,128,1280]{2,1,0:T(8,128)(2,1)S(1)} %get-tuple-element.207), channel_id=1, source_target_pairs={{0,4},{1,5},{2,6},{3,7},{4,0},{5,1},{6,2},{7,3},{8,12},{9,13},{10,... | collective-permute-start | bytes 983048 | tf_op jit(solution)/shard_map/ppermute | solution.py:460
  565.3 41.6 %collective-permute-start.40 = (bf16[1,128,1280]{2,1,0:T(8,128)(2,1)S(1)}, bf16[1,128,1280]{2,1,0:T(8,128)(2,1)S(1)}, u32[]{:S(2)}, u32[]{:S(2)}) collective-permute-start(bf16[1,128,1280]{2,1,0:T(8,128)(2,1)S(1)} %get-tuple-element.206), channel_id=1, source_target_pairs={{0,6},{1,7},{2,4},{3,5},{4,2},{5,3},{6,0},{7,1},{8,14},{9,15},{10,... | collective-permute-start | bytes 983048 | tf_op jit(solution)/shard_map/ppermute | solution.py:460
  574.9 48.1 %collective-permute-start.43 = (bf16[2,256,1024]{2,1,0:T(8,128)(2,1)S(1)}, bf16[2,256,1024]{2,1,0:T(8,128)(2,1)S(1)}, u32[]{:S(2)}, u32[]{:S(2)}) collective-permute-start(bf16[2,256,1024]{2,1,0:T(8,128)(2,1)S(1)} %bitcast.281), channel_id=1, source_target_pairs={{0,8},{8,0},{16,24},{24,16},{1,9},{9,1},{17,25},{25,17},{2,10},{10... | collective-permute-start | bytes 3145736 | tf_op jit(solution)/shard_map/ppermute | solution.py:444
  575.6 42.8 %collective-permute-start.32 = (bf16[512,1024]{1,0:T(8,128)(2,1)}, bf16[512,1024]{1,0:T(8,128)(2,1)}, u32[]{:S(2)}, u32[]{:S(2)}) collective-permute-start(bf16[512,1024]{1,0:T(8,128)(2,1)} %fusion.23), channel_id=1, source_target_pairs={{0,16},{8,24},{16,0},{24,8},{1,17},{9,25},{17,1},{25,9},{2,18},{10... | collective-permute-start | bytes 3145736 | tf_op jit(solution)/shard_map/ppermute | solution.py:448
  (124 other events, 1075.4 us)
Sparse Core Ops, SparseCore 0:
  12.0 126.3 all-gather.5
  141.8 113.5 all-gather.3
  362.0 161.2 reduce-scatter.1

commit v5 on v4

--- a/solution.py
+++ b/solution.py
@@ -722,11 +722,10 @@
     def line_split(summed):
         return summed.reshape(8, 2, 64, summed.shape[1])
 
-    early_q, early_k, early_v = cross_half(0, cross_queries)
-    feed_keep, feed_got = after((feed_keep, feed_got), early_q)
     feed_half = added(feed_keep, feed_got).reshape(8 * 512, width)
     feed_share = lax.psum_scatter(feed_half, "fsdp", scatter_dimension=0, tiled=True)
-    first_q, first_k, first_v = after((early_q, early_k, early_v), feed_half)
+    early_q, early_k, early_v = cross_half(0, after(cross_queries, feed_half))
+    first_q, first_k, first_v = early_q, early_k, early_v
     keep, send = halves_dot(
         [(memory_all, first_k), (memory_all, first_v), (hidden_low, first_q), (cross_low, grad_cross_branch)], core
     )
@@ -785,18 +784,20 @@
     memory_got = to_y(memory_far)
     early_got = to_x(part_of(early, x ^ 1, 1))
     first_heads = jnp.concatenate(heads_back(0, heads_grad), axis=1)
-    first_heads, early_got, late_got = lax.optimization_barrier((first_heads, early_got, late_got))
+    first_heads, early_got, late_got, feed_share = lax.optimization_barrier((first_heads, early_got, late_got, feed_share))
+    feed_far = to_y(feed_share)
     first_blocks = own_blocks(first_heads)
     late = added(late_keep, late_got).reshape(4, 2, 128, 5 * share)
     late_got = to_x(part_of(late, x ^ 1, 1))
     early = added(part_of(early, x, 1), early_got)
     early_sends = [part_of(early, z ^ k, 0) for k in (1, 2, 3)]
-    first_total = from_fsdp(first_blocks)
+    first_total = lax.all_to_all(first_blocks, "fsdp", 0, 0)
     second_heads = jnp.concatenate(heads_back(1, after(heads_grad, (first_blocks, late, early_sends))), axis=1)
     early_pieces = [to_z(piece, k) for piece, k in zip(early_sends, (1, 2, 3))]
-    second_heads, early_pieces, late_got, memory_got, feed_share = lax.optimization_barrier(
-        (second_heads, early_pieces, late_got, memory_got, feed_share)
-    )
+    second_heads, early_pieces, late_got, memory_got, feed_far, first_total = lax.optimization_barrier(
+        (second_heads, early_pieces, late_got, memory_got, feed_far, first_total)
+    )
+    first_total = jnp.sum(first_total.astype(f32), axis=0)
     second_blocks = own_blocks(second_heads)
     ready_first, ready_second = after((first_heads, second_heads), second_blocks)
     token_terms = (
@@ -805,8 +806,7 @@
     ).astype(bf16)
     token_near, token_far = chip_sums(token_terms, rows)
     feed_near = feed_share
-    feed_far = to_y(feed_share)
-    token_got = to_y(after(token_far, feed_far))
+    token_got = to_y(token_far)
     token_grad = (residual_scale * grad_first + token_near + token_got.astype(f32))[None]
     memory_grad = (memory_near + memory_got.astype(f32))[None]
 

time: 648 us -> 655 us (1.011)
    ppermute x9, waiting for transfers between devices: 56.5 us -> 70.8 us  [to_z(): return lax.ppermute(v, 'fsdp', z_perm(k))]
    all_to_all x2 -> x1, starting transfers between devices: 16.1 us -> 4.44 us  [from_fsdp(): got = lax.all_to_all(blocks, 'fsdp', 0, 0)]
    ppermute x11, waiting for transfers between devices: 27.1 us -> 18 us  [to_y(): return lax.ppermute(v, 'ctx', y_perm())]
    unnamed x219 -> x211, local copies, waits for them, and re-layouts: 23.5 us -> 26.3 us
where the time goes in v5:
time: 655 us; the launch traced here: 647 us
  Pallas kernels  194 us (30%)
  waiting for transfers between devices  187 us (29%)
  matrix products  81.2 us (12%)
  other arithmetic  65.6 us (10%)
  local copies, waits for them, and re-layouts  52.4 us (8%)
  starting transfers between devices  51.7 us (8%)
  between operations  15.6 us (2%)
    pallas_call x4, Pallas kernels, attention_backward(): pl.pallas_call(body, grid_spec=pltpu.PrefetchScalarGridSpec(num_scalar_pr...  86.4 us
    ppermute x9, waiting for transfers between devices, to_z(): return lax.ppermute(v, 'fsdp', z_perm(k))  70.8 us
    dot_general x14, matrix products, dot(): return jnp.dot(left, right, preferred_element_type=f32)  59 us
    all_gather x1, waiting for transfers between devices, tiled_shards(): lax.all_gather(after(feed_own, (middle_all, heads_out)), ('fsdp', 'ctx'),...  55.9 us
    pallas_call x2, Pallas kernels, attention_forward(): pl.pallas_call(body, grid_spec=pltpu.PrefetchScalarGridSpec(num_scalar_pr...  52.6 us
    pallas_call x1, Pallas kernels, feed_forward(): pl.pallas_call(feed_body, grid_spec=pltpu.PrefetchScalarGridSpec(num_scal...  46.3 us
    convert_element_type x10, other arithmetic, added(): (keep.astype(jnp.float32) + got.astype(jnp.float32)).astype(jnp.bfloat16)  29.4 us
    unnamed x211, local copies, waits for them, and re-layouts  26.3 us
  transfers between devices with their start and end apart: 49, of which 20 were waited for; matrix products, arithmetic and copies ran while one was open for 24% of the time, Pallas kernels for 23%

profile of v5, /device:TPU:11, one launch (start us, length us, event | category | flops | bytes accessed | tf_op | source)
XLA Modules:
  0.0 646.9 jit_solution(17969937917417666271)
XLA Ops:
  27.9 9.7 %collective-permute-done.3.refs_3_ = bf16[144,768]{1,0:T(8,128)(2,1)S(1)} collective-permute-done((bf16[144,768]{1,0:T(8,128)(2,1)S(1)}, bf16[144,768]{1,0:T(8,128)(2,1)S(1)}, u32[]{:S(2)}, u32[]{:S(2)}) %collective-permute-start.3) | collective-permute-done | bytes 221216 | tf_op jit(solution)/shard_map/ppermute | solution.py:460
  37.6 10.3 %collective-permute-done.4.refs_4_ = bf16[144,768]{1,0:T(8,128)(2,1)S(1)} collective-permute-done((bf16[144,768]{1,0:T(8,128)(2,1)S(1)}, bf16[144,768]{1,0:T(8,128)(2,1)S(1)}, u32[]{:S(2)}, u32[]{:S(2)}) %collective-permute-start.4) | collective-permute-done | bytes 221216 | tf_op jit(solution)/shard_map/ppermute | solution.py:460
  62.7 8.1 %collective-permute-done.7.refs_6_ = bf16[144,768]{1,0:T(8,128)(2,1)S(1)} collective-permute-done((bf16[144,768]{1,0:T(8,128)(2,1)S(1)}, bf16[144,768]{1,0:T(8,128)(2,1)S(1)}, u32[]{:S(2)}, u32[]{:S(2)}) %collective-permute-start.7) | collective-permute-done | bytes 221216 | tf_op jit(solution)/shard_map/ppermute | solution.py:456
  85.6 5.6 add_convert_fusion.3.refs_3_.refs_4_.refs_5_.refs_7_.refs_8_
  91.2 23.1 %shard_map.434 = (bf16[2048,256]{1,0:T(8,128)(2,1)S(1)}, f32[2,8,4096]{2,1,0:T(8,128)S(1)}) custom-call(s32[4]{0:T(128)S(1)} %bitcast.285, s32[64]{0:T(128)S(1)} %reshape_squeeze.24.refs_1_, s32[1]{0:T(128)} %bitcast.3.refs_2_.me_ref, bf16[2048,768]{1,0:T(8,128)(2,1)S(1)} %add_convert_fusion.3.refs_3_.refs_4_.refs_5_.refs_7_.refs_8_, ...), custom_call_target="tpu_custom_call" | custom-call | flops 8589934592 | bytes 4194304 | tf_op jit(solution)/shard_map/pallas_call | solution.py:230
  114.3 12.8 %collective-permute-done.10 = bf16[512,1024]{1,0:T(8,128)(2,1)S(1)} collective-permute-done((bf16[512,1024]{1,0:T(8,128)(2,1)}, bf16[512,1024]{1,0:T(8,128)(2,1)S(1)}, u32[]{:S(2)}, u32[]{:S(2)}) %collective-permute-start.10) | collective-permute-done | bytes 1048608 | tf_op jit(solution)/shard_map/ppermute | solution.py:448
  128.1 10.2 %all-gather.6.cloned.1.call-done = bf16[160,32,1024]{2,1,0:T(8,128)(2,1)} async-done(((bf16[5,32,1024]{2,1,0:T(8,128)(2,1)}), bf16[160,32,1024]{2,1,0:T(8,128)(2,1)}) %all-gather.6.cloned.1.call-update) | async-done | bytes 10485776 | tf_op jit(solution)/shard_map/all_gather | solution.py:665
  147.7 6.1 add_convert_fusion.2.refs_2_.refs_5_
  153.8 6.1 convolution_convert_fusion.refs_1_.refs_4_
  165.3 29.5 %shard_map.435 = (bf16[512,1024]{1,0:T(8,128)(2,1)S(1)}, f32[8,8,1024]{2,1,0:T(8,128)S(1)}) custom-call(bf16[512,1024]{1,0:T(8,128)(2,1)S(1)} %add_convert_fusion.8.refs_0_, bf16[2048,1024]{1,0:T(8,128)(2,1)} %convolution_convert_fusion.refs_1_.refs_4_, bf16[2048,1024]{1,0:T(8,128)(2,1)} %add_convert_fusion.2.refs_2_.refs_5_), custom_call_target="tpu_custom_call" | custom-call | flops 8589934592 | bytes 10485760 | tf_op jit(solution)/shard_map/pallas_call | solution.py:230
  199.5 55.9 %all-gather.4.cloned.1.call-done = bf16[8192,1024]{1,0:T(8,128)(2,1)} async-done(((bf16[256,1024]{1,0:T(8,128)(2,1)}), bf16[8192,1024]{1,0:T(8,128)(2,1)}) %all-gather.4.cloned.1.call-update) | async-done | bytes 16777232 | tf_op jit(solution)/shard_map/all_gather | solution.py:688
  255.4 46.3 %shard_map.436 = (bf16[512,1024]{1,0:T(8,128)(2,1)}, f32[512,1024]{1,0:T(8,128)}, bf16[8,2,256,1024]{3,2,1,0:T(8,128)(2,1)}, bf16[8,2,256,1024]{3,2,1,0:T(8,128)...) custom-call(s32[1]{0:T(128)} %bitcast.core_ref, f32[512,1024]{1,0:T(8,128)} %multiply_add_fusion.1.hidden_ref, ...), custom_call_target="tpu_custom_call" | custom-call | flops 25769803776 | bytes 54525952 | tf_op jit(solution)/shard_map/pallas_call | solution.py:384
  315.3 9.0 %add_convert_fusion = bf16[8,2,256,1024]{3,2,1,0:T(8,128)(2,1)} fusion(bf16[8,2,256,1024]{3,2,1,0:T(8,128)(2,1)} %collective-permute-done.16, bf16[8,2,256,1024]{3,2,1,0:T(8,128)(2,1)S(1)} %bitcast.297), kind=kLoop, calls=%fused_computation | loop fusion | flops 16777216 | bytes 25165824 | tf_op jit(solution)/shard_map/convert_element_type | solution.py:523
  328.0 27.6 %shard_map.437 = (bf16[512,512]{1,0:T(8,128)(2,1)S(1)}, bf16[2048,512]{1,0:T(8,128)(2,1)S(1)}, bf16[2048,512]{1,0:T(8,128)(2,1)}) custom-call(bf16[512,1024]{1,0:T(8,128)(2,1)S(1)} %copy-done.13, bf16[512,1024]{1,0:T(8,128)(2,1)S(1)} %copy-done.14, bf16[512,1024]{1,0:T(8,128)(2,1)S(1)} %copy-done.8, f32[8,8,1024]{2,1,0:T(8,128)S(1)} %get-tuple-element.111.refs_3_, ...), custom_call_target="tpu_custom_call" | custom-call | flops 10737418240 | bytes 10485760 | tf_op jit(solution)/shard_map/pallas_call | solution.py:276
  368.0 27.5 %shard_map.438 = (bf16[512,512]{1,0:T(8,128)(2,1)S(1)}, bf16[2048,512]{1,0:T(8,128)(2,1)S(1)}, bf16[2048,512]{1,0:T(8,128)(2,1)}) custom-call(bf16[512,1024]{1,0:T(8,128)(2,1)S(1)} %copy-done.13, bf16[512,1024]{1,0:T(8,128)(2,1)S(1)} %copy-done.14, bf16[512,1024]{1,0:T(8,128)(2,1)S(1)} %copy-done.8, f32[8,8,1024]{2,1,0:T(8,128)S(1)} %get-tuple-element.111.refs_3_, ...), custom_call_target="tpu_custom_call" | custom-call | flops 10737418240 | bytes 10485760 | tf_op jit(solution)/shard_map/pallas_call | solution.py:276
  421.0 14.0 %fusion.15 = bf16[2048,1024]{1,0:T(8,128)(2,1)} fusion(bf16[1024,512]{1,0:T(8,128)(2,1)} %get-tuple-element.265, bf16[1024,512]{1,0:T(8,128)(2,1)} %get-tuple-element.190, bf16[1024,512]{1,0:T(8,128)(2,1)} %get-tuple-element.266, bf16[1024,512]{1,0:T(8,128)(2,1)S(1)} %copy-done.64, bf16[2048,512]{1,0:T(8,128)(2,1)} %get-tuple-element.126, ...), kind=kOutput, calls=%fused_computation.23 | convolution fusion | flops 8642363392 | bytes 16777216 | tf_op jit(solution)/shard_map/dot_general | solution.py:642
  452.2 6.2 collective-permute-done.20
  466.5 15.8 %shard_map.439 = (bf16[2048,128]{1,0:T(8,128)(2,1)S(1)}, bf16[2048,128]{1,0:T(8,128)(2,1)S(1)}, bf16[2048,128]{1,0:T(8,128)(2,1)S(1)}) custom-call(s32[4]{0:T(128)S(1)} %bitcast.286, s32[64]{0:T(128)S(1)} %reshape_squeeze.24.refs_1_, s32[1]{0:T(128)} %bitcast.3.refs_2_.me_ref, bf16[2048,768]{1,0:T(8,128)(2,1)} %copy-done.15, ...), custom_call_target="tpu_custom_call" | custom-call | flops 10737418240 | bytes 4194304 | tf_op jit(solution)/shard_map/pallas_call | solution.py:276
  488.1 5.6 collective-permute-start.28
  509.5 15.5 %shard_map.440 = (bf16[2048,128]{1,0:T(8,128)(2,1)S(1)}, bf16[2048,128]{1,0:T(8,128)(2,1)S(1)}, bf16[2048,128]{1,0:T(8,128)(2,1)S(1)}) custom-call(s32[4]{0:T(128)S(1)} %bitcast.287, s32[64]{0:T(128)S(1)} %reshape_squeeze.24.refs_1_, s32[1]{0:T(128)} %bitcast.3.refs_2_.me_ref, bf16[2048,768]{1,0:T(8,128)(2,1)} %copy-done.15, ...), custom_call_target="tpu_custom_call" | custom-call | flops 10737418240 | bytes 4194304 | tf_op jit(solution)/shard_map/pallas_call | solution.py:276
  537.7 5.5 convolution_convert_fusion.7
  574.4 14.5 %collective-permute-done.38 = bf16[1,128,1280]{2,1,0:T(8,128)(2,1)S(1)} collective-permute-done((bf16[1,128,1280]{2,1,0:T(8,128)(2,1)S(1)}, bf16[1,128,1280]{2,1,0:T(8,128)(2,1)S(1)}, u32[]{:S(2)}, u32[]{:S(2)}) %collective-permute-start.38) | collective-permute-done | bytes 327712 | tf_op jit(solution)/shard_map/ppermute | solution.py:460
  588.9 16.2 %collective-permute-done.39 = bf16[1,128,1280]{2,1,0:T(8,128)(2,1)S(1)} collective-permute-done((bf16[1,128,1280]{2,1,0:T(8,128)(2,1)S(1)}, bf16[1,128,1280]{2,1,0:T(8,128)(2,1)S(1)}, u32[]{:S(2)}, u32[]{:S(2)}) %collective-permute-start.39) | collective-permute-done | bytes 327712 | tf_op jit(solution)/shard_map/ppermute | solution.py:460
  605.1 8.0 %collective-permute-done.40 = bf16[1,128,1280]{2,1,0:T(8,128)(2,1)S(1)} collective-permute-done((bf16[1,128,1280]{2,1,0:T(8,128)(2,1)S(1)}, bf16[1,128,1280]{2,1,0:T(8,128)(2,1)S(1)}, u32[]{:S(2)}, u32[]{:S(2)}) %collective-permute-start.40) | collective-permute-done | bytes 327712 | tf_op jit(solution)/shard_map/ppermute | solution.py:460
  (449 shorter events, 242.2 us)
Async XLA Ops:
  7.3 131.0 %all-gather.6.cloned.1.call-start = ((), (), s32[]{:S(2)}) async-start(), calls=%async_computation.5 | async-start | bytes 10813440 | tf_op jit(solution)/shard_map/all_gather | solution.py:665
  11.8 243.5 %all-gather.4.cloned.1.call-start = ((), (), s32[]{:S(2)}) async-start(), calls=%async_computation.3 | async-start | bytes 17301504 | tf_op jit(solution)/shard_map/all_gather | solution.py:688
  11.9 36.0 %collective-permute-start.1 = (bf16[512,1024]{1,0:T(8,128)(2,1)}, bf16[512,1024]{1,0:T(8,128)(2,1)}, u32[]{:S(2)}, u32[]{:S(2)}) collective-permute-start(bf16[512,1024]{1,0:T(8,128)(2,1)} %bitcast.1), channel_id=1, source_target_pairs={{0,16},{8,24},{16,0},{24,8},{1,17},{9,25},{17,1},{25,9},{2,18},{10... | collective-permute-start | bytes 3145736 | tf_op jit(solution)/shard_map/ppermute | solution.py:448
  22.0 25.9 %collective-permute-start.4 = (bf16[144,768]{1,0:T(8,128)(2,1)S(1)}, bf16[144,768]{1,0:T(8,128)(2,1)S(1)}, u32[]{:S(2)}, u32[]{:S(2)}) collective-permute-start(bf16[144,768]{1,0:T(8,128)(2,1)S(1)} %concatenate.104.refs_1_), channel_id=1, source_target_pairs={{0,6},{1,7},{2,4},{3,5},{4,2},{5,3},{6,0},{7,1},{8,14},{9,15},{10,... | collective-permute-start | bytes 663560 | tf_op jit(solution)/shard_map/ppermute | solution.py:460
  22.2 63.3 %collective-permute-start = (bf16[512,1024]{1,0:T(8,128)(2,1)}, bf16[512,1024]{1,0:T(8,128)(2,1)}, u32[]{:S(2)}, u32[]{:S(2)}) collective-permute-start(bf16[512,1024]{1,0:T(8,128)(2,1)} %bitcast.1), channel_id=1, source_target_pairs={{0,8},{8,0},{16,24},{24,16},{1,9},{9,1},{17,25},{25,17},{2,10},{10... | collective-permute-start | bytes 3145736 | tf_op jit(solution)/shard_map/ppermute | solution.py:444
  47.9 37.6 %collective-permute-start.5 = (bf16[512,1024]{1,0:T(8,128)(2,1)}, bf16[512,1024]{1,0:T(8,128)(2,1)}, u32[]{:S(2)}, u32[]{:S(2)}) collective-permute-start(bf16[512,1024]{1,0:T(8,128)(2,1)} %collective-permute-done.1), channel_id=1, source_target_pairs={{0,8},{8,0},{16,24},{24,16},{1,9},{9,1},{17,25},{25,17},{2,10},{10... | collective-permute-start | bytes 3145736 | tf_op jit(solution)/shard_map/ppermute | solution.py:444
  85.2 41.9 %collective-permute-start.10 = (bf16[512,1024]{1,0:T(8,128)(2,1)}, bf16[512,1024]{1,0:T(8,128)(2,1)S(1)}, u32[]{:S(2)}, u32[]{:S(2)}) collective-permute-start(bf16[512,1024]{1,0:T(8,128)(2,1)} %bitcast.315), channel_id=1, source_target_pairs={{0,16},{8,24},{16,0},{24,8},{1,17},{9,25},{17,1},{25,9},{2,18},{10... | collective-permute-start | bytes 3145736 | tf_op jit(solution)/shard_map/ppermute | solution.py:448
  138.4 345.3 %reduce-scatter.2.cloned.1.call-start = ((), (), s32[]{:S(2)}) async-start(), calls=%async_computation.4 | async-start | bytes 9437184 | tf_op jit(solution)/shard_map/reduce_scatter | solution.py:726
  359.5 36.0 %collective-permute-start.17 = (bf16[1024,1280]{1,0:T(8,128)(2,1)S(1)}, bf16[1024,1280]{1,0:T(8,128)(2,1)}, u32[]{:S(2)}, u32[]{:S(2)}) collective-permute-start(bf16[1024,1280]{1,0:T(8,128)(2,1)S(1)} %pad_maximum_fusion.3), channel_id=1, source_target_pairs={{0,8},{8,0},{16,24},{24,16},{1,9},{9,1},{17,25},{25,17},{2,10},{10... | collective-permute-start | bytes 7864328 | tf_op jit(solution)/shard_map/ppermute | solution.py:444
  416.0 43.6 %collective-permute-start.21 = (bf16[8,64,1280]{2,1,0:T(8,128)(2,1)}, bf16[8,64,1280]{2,1,0:T(8,128)(2,1)}, u32[]{:S(2)}, u32[]{:S(2)}) collective-permute-start(bf16[8,64,1280]{2,1,0:T(8,128)(2,1)} %dynamic-slice_bitcast_fusion.2), channel_id=1, source_target_pairs={{0,16},{8,24},{16,0},{24,8},{1,17},{9,25},{17,1},{25,9},{2,18},{10... | collective-permute-start | bytes 3932168 | tf_op jit(solution)/shard_map/ppermute | solution.py:448
  416.7 35.5 %collective-permute-start.19 = (bf16[512,256]{1,0:T(8,128)(2,1)}, bf16[512,256]{1,0:T(8,128)(2,1)}, u32[]{:S(2)}, u32[]{:S(2)}) collective-permute-start(bf16[512,256]{1,0:T(8,128)(2,1)} %get-tuple-element.204), channel_id=1, source_target_pairs={{0,16},{8,24},{16,0},{24,8},{1,17},{9,25},{17,1},{25,9},{2,18},{10... | collective-permute-start | bytes 786440 | tf_op jit(solution)/shard_map/ppermute | solution.py:448
  417.7 40.8 %collective-permute-start.20 = (bf16[512,256]{1,0:T(8,128)(2,1)}, bf16[512,256]{1,0:T(8,128)(2,1)}, u32[]{:S(2)}, u32[]{:S(2)}) collective-permute-start(bf16[512,256]{1,0:T(8,128)(2,1)} %get-tuple-element.203), channel_id=1, source_target_pairs={{0,24},{8,16},{16,8},{24,0},{1,25},{9,17},{17,9},{25,1},{2,26},{10... | collective-permute-start | bytes 786440 | tf_op jit(solution)/shard_map/ppermute | solution.py:452
  437.1 24.9 %collective-permute-start.22 = (bf16[2,512,1024]{2,1,0:T(8,128)(2,1)S(1)}, bf16[2,512,1024]{2,1,0:T(8,128)(2,1)S(1)}, u32[]{:S(2)}, u32[]{:S(2)}) collective-permute-start(bf16[2,512,1024]{2,1,0:T(8,128)(2,1)S(1)} %slice_bitcast_fusion.1), channel_id=1, source_target_pairs={{0,8},{8,0},{16,24},{24,16},{1,9},{9,1},{17,25},{25,17},{2,10},{10... | collective-permute-start | bytes 6291464 | tf_op jit(solution)/shard_map/ppermute | solution.py:444
  443.6 40.0 %collective-permute-start.24 = (bf16[1024,1280]{1,0:T(8,128)(2,1)S(1)}, bf16[1024,1280]{1,0:T(8,128)(2,1)}, u32[]{:S(2)}, u32[]{:S(2)}) collective-permute-start(bf16[1024,1280]{1,0:T(8,128)(2,1)S(1)} %pad_maximum_fusion.5), channel_id=1, source_target_pairs={{0,8},{8,0},{16,24},{24,16},{1,9},{9,1},{17,25},{25,17},{2,10},{10... | collective-permute-start | bytes 7864328 | tf_op jit(solution)/shard_map/ppermute | solution.py:444
  465.3 59.8 %collective-permute-start.29 = (bf16[512,1024]{1,0:T(8,128)(2,1)}, bf16[512,1024]{1,0:T(8,128)(2,1)}, u32[]{:S(2)}, u32[]{:S(2)}) collective-permute-start(bf16[512,1024]{1,0:T(8,128)(2,1)} %fusion.27), channel_id=1, source_target_pairs={{0,16},{8,24},{16,0},{24,8},{1,17},{9,25},{17,1},{25,9},{2,18},{10... | collective-permute-start | bytes 3145736 | tf_op jit(solution)/shard_map/ppermute | solution.py:448
  488.1 49.5 %collective-permute-start.28 = (bf16[4,128,1280]{2,1,0:T(8,128)(2,1)}, bf16[4,128,1280]{2,1,0:T(8,128)(2,1)}, u32[]{:S(2)}, u32[]{:S(2)}) collective-permute-start(bf16[4,128,1280]{2,1,0:T(8,128)(2,1)} %get-tuple-element.188), channel_id=1, source_target_pairs={{0,1},{1,0},{2,3},{3,2},{4,5},{5,4},{6,7},{7,6},{8,9},{9,8},{10,11... | collective-permute-start | bytes 3932168 | tf_op jit(solution)/shard_map/ppermute | solution.py:456
  501.3 36.4 %all-to-all-start = ((bf16[8,128,384]{2,1,0:T(8,128)(2,1)}), bf16[8,128,384]{2,1,0:T(8,128)(2,1)}, u32[]{:S(2)}, u32[]{:S(2)}) async-start(bf16[8,128,384]{2,1,0:T(8,128)(2,1)} %bitcast.319), calls=%async_computation.1 | async-start | bytes 1572864 | tf_op jit(solution)/shard_map/all_to_all | solution.py:794
  506.8 26.3 %collective-permute-start.26 = (bf16[64,1280]{1,0:T(8,128)(2,1)S(1)}, bf16[64,1280]{1,0:T(8,128)(2,1)}, u32[]{:S(2)}, u32[]{:S(2)}) collective-permute-start(bf16[64,1280]{1,0:T(8,128)(2,1)S(1)} %get-tuple-element.222), channel_id=1, source_target_pairs={{0,4},{1,5},{2,6},{3,7},{4,0},{5,1},{6,2},{7,3},{8,12},{9,13},{10,... | collective-permute-start | bytes 491528 | tf_op jit(solution)/shard_map/ppermute | solution.py:460
  508.7 29.0 %collective-permute-start.30 = (bf16[512,1024]{1,0:T(8,128)(2,1)}, bf16[512,1024]{1,0:T(8,128)(2,1)}, u32[]{:S(2)}, u32[]{:S(2)}) collective-permute-start(bf16[512,1024]{1,0:T(8,128)(2,1)} %reduce-scatter.2.cloned.1.call-done), channel_id=1, source_target_pairs={{0,16},{8,24},{16,0},{24,8},{1,17},{9,25},{17,1},{25,9},{2,18},{10... | collective-permute-start | bytes 3145736 | tf_op jit(solution)/shard_map/ppermute | solution.py:448
  556.7 72.4 %collective-permute-start.43 = (bf16[2,256,1024]{2,1,0:T(8,128)(2,1)S(1)}, bf16[2,256,1024]{2,1,0:T(8,128)(2,1)S(1)}, u32[]{:S(2)}, u32[]{:S(2)}) collective-permute-start(bf16[2,256,1024]{2,1,0:T(8,128)(2,1)S(1)} %bitcast.281), channel_id=1, source_target_pairs={{0,8},{8,0},{16,24},{24,16},{1,9},{9,1},{17,25},{25,17},{2,10},{10... | collective-permute-start | bytes 3145736 | tf_op jit(solution)/shard_map/ppermute | solution.py:444
  560.5 55.2 %all-to-all-start.1 = ((bf16[8,144,384]{2,1,0:T(8,128)(2,1)}), bf16[8,144,384]{2,1,0:T(8,128)(2,1)}, u32[]{:S(2)}, u32[]{:S(2)}) async-start(bf16[8,144,384]{2,1,0:T(8,128)(2,1)} %maximum_maximum_fusion), calls=%async_computation.2 | async-start | bytes 1769472 | tf_op jit(solution)/shard_map/all_to_all | solution.py:514
  571.1 34.0 %collective-permute-start.39 = (bf16[1,128,1280]{2,1,0:T(8,128)(2,1)S(1)}, bf16[1,128,1280]{2,1,0:T(8,128)(2,1)S(1)}, u32[]{:S(2)}, u32[]{:S(2)}) collective-permute-start(bf16[1,128,1280]{2,1,0:T(8,128)(2,1)S(1)} %get-tuple-element.201), channel_id=1, source_target_pairs={{0,4},{1,5},{2,6},{3,7},{4,0},{5,1},{6,2},{7,3},{8,12},{9,13},{10,... | collective-permute-start | bytes 983048 | tf_op jit(solution)/shard_map/ppermute | solution.py:460
  573.0 40.1 %collective-permute-start.40 = (bf16[1,128,1280]{2,1,0:T(8,128)(2,1)S(1)}, bf16[1,128,1280]{2,1,0:T(8,128)(2,1)S(1)}, u32[]{:S(2)}, u32[]{:S(2)}) collective-permute-start(bf16[1,128,1280]{2,1,0:T(8,128)(2,1)S(1)} %get-tuple-element.200), channel_id=1, source_target_pairs={{0,6},{1,7},{2,4},{3,5},{4,2},{5,3},{6,0},{7,1},{8,14},{9,15},{10,... | collective-permute-start | bytes 983048 | tf_op jit(solution)/shard_map/ppermute | solution.py:460
  573.8 50.9 %collective-permute-start.32 = (bf16[512,1024]{1,0:T(8,128)(2,1)}, bf16[512,1024]{1,0:T(8,128)(2,1)}, u32[]{:S(2)}, u32[]{:S(2)}) collective-permute-start(bf16[512,1024]{1,0:T(8,128)(2,1)} %fusion.23), channel_id=1, source_target_pairs={{0,16},{8,24},{16,0},{24,8},{1,17},{9,25},{17,1},{25,9},{2,18},{10... | collective-permute-start | bytes 3145736 | tf_op jit(solution)/shard_map/ppermute | solution.py:448
  (120 other events, 1120.2 us)
Sparse Core Ops, SparseCore 0:
  12.0 126.3 all-gather.5
  141.8 113.5 all-gather.3
  324.4 146.5 reduce-scatter.1
